TPU v7x, 32 devices: a whole 2x2x4 slice. The times are simulated.
32 devices in a mesh: groups: 2 (over y), ctx: 16 (over z, x, core).
Axes of the slice: x: 2, y: 2, z: 4, core: 2. Of those that a mesh axis runs over, the one named last changes fastest.
Arguments:
- queries: bfloat16 [4096, 1024], P(('groups', 'ctx')), parts along dimension 0, may hold values from -256 to 256
- key_rows: bfloat16 [4096, 1024], P(('groups', 'ctx')), parts along dimension 0, may hold values from -256 to 256
- value_rows: bfloat16 [4096, 1024], P(('groups', 'ctx')), parts along dimension 0, may hold values from -6 to 6
- write_strength: float32 [8, 4096], P(None, ('groups', 'ctx')), parts along dimension 1, may hold values from 0 to 1, as said below
- log_decay: float32 [8, 4096], P(None, ('groups', 'ctx')), parts along dimension 1, may hold values from -2 to 0, as said below
- level_gates: float32 [5, 8, 4096], P(None, None, ('groups', 'ctx')), parts along dimension 2, may hold values from 0.2 to 2
Outputs:
- layer_out: float32 [4096, 1024], P(('groups', 'ctx')), parts along dimension 0
There are 2 independent parts, one for each index of `groups`. A program takes and returns all parts, laid end to end along the dimension named above; each array names one. Nothing has to cross between parts.
Inputs may be any that keep to these rules, and one draw needn't show every extreme that they name: `write_strength`: Positive. `log_decay`: never positive.
All inputs are finite; a program needn't handle non-finite values.
Results may differ from a plain program's by a relative error of at most 0.0003.
Values sent between devices are 32-bit elements; how exact they have to be, the bound alone decides.
No kernel may reach another device: no remote copies, remote signals or barrier semaphores. Data moves between devices by JAX's collectives and lax.ppermute only.
A program may use at most 64 MiB of HBM per device.

v0:
```python
import jax
import jax.numpy as jnp
from jax import lax
from jax.sharding import PartitionSpec as P

norm_eps = 1e-06


def from_partner(value, axis, distance):
    return lax.ppermute(value, axis, [(i, i ^ 1 << distance) for i in range(lax.axis_size(axis))])


def passed_along(value, axis, steps):
    count = lax.axis_size(axis)
    first, last = (max(0, -steps), min(count, count - steps))
    return lax.ppermute(value, axis, [(source, source + steps) for source in range(first, last)])


def unit_rows(matrix):
    return matrix * lax.rsqrt(jnp.sum(matrix * matrix, axis=-1, keepdims=True) + norm_eps)


def head_major(block, head_count):
    count = block.shape[0]
    return block.astype(jnp.float32).reshape(count, head_count, -1).transpose(1, 0, 2)


def head_product(left, right):
    return jnp.einsum("hij,hjk->hik", left, right, precision=lax.Precision.HIGHEST)


def block_solve(queries, key_rows, value_rows, write_strength, log_decay):
    head_count = write_strength.shape[0]
    count = write_strength.shape[1]
    query_unit = unit_rows(head_major(queries, head_count))
    key_unit = unit_rows(head_major(key_rows, head_count))
    value_head = head_major(value_rows, head_count)
    key_width = key_unit.shape[2]
    running = jnp.cumsum(log_decay, axis=1)
    row_index = lax.broadcasted_iota(jnp.int32, (count, count), 0)
    col_index = lax.broadcasted_iota(jnp.int32, (count, count), 1)
    lower_incl = (row_index >= col_index)[None]
    lower_strict = (row_index > col_index)[None]
    gap_log = jnp.where(lower_incl, running[:, :, None] - running[:, None, :], 0.0)
    decay_ratio = jnp.where(lower_incl, jnp.exp(gap_log), 0.0)
    key_gram = jnp.einsum("htk,hsk->hts", key_unit, key_unit, precision=lax.Precision.HIGHEST)
    identity = jnp.eye(count, dtype=jnp.float32)
    tri_matrix = identity[None] + jnp.where(
        lower_strict, write_strength[:, :, None] * key_gram * decay_ratio, 0.0
    )
    growth = jnp.exp(running)
    right_side = jnp.concatenate(
        [(write_strength * growth)[:, :, None] * key_unit, write_strength[:, :, None] * value_head],
        axis=2,
    )
    solved = jax.scipy.linalg.solve_triangular(
        tri_matrix, right_side, lower=True, unit_diagonal=True
    )
    erase_rows = solved[:, :, :key_width]
    written_value_rows = solved[:, :, key_width:]
    return (query_unit, key_unit, decay_ratio, growth, running, erase_rows, written_value_rows)


def query_terms(solved_parts):
    query_unit, key_unit, decay_ratio, growth, running, erase_rows, written_value_rows = (
        solved_parts
    )
    query_gram = (
        jnp.einsum("htk,hsk->hts", query_unit, key_unit, precision=lax.Precision.HIGHEST)
        * decay_ratio
    )
    local_read = jnp.einsum(
        "hts,hsv->htv", query_gram, written_value_rows, precision=lax.Precision.HIGHEST
    )
    effective_query = growth[:, :, None] * query_unit - jnp.einsum(
        "hts,hsk->htk", query_gram, erase_rows, precision=lax.Precision.HIGHEST
    )
    return (local_read, effective_query)


def block_totals(solved_parts):
    query_unit, key_unit, decay_ratio, growth, running, erase_rows, written_value_rows = (
        solved_parts
    )
    key_width = key_unit.shape[2]
    to_end = jnp.exp(running[:, -1:] - running)
    final_key_rows = key_unit * to_end[:, :, None]
    block_memory_state = jnp.einsum(
        "gjz,gjn->gzn", final_key_rows, written_value_rows, precision=lax.Precision.HIGHEST
    )
    key_eye = jnp.eye(key_width, dtype=jnp.float32)
    block_trans = growth[:, -1][:, None, None] * key_eye[None] - jnp.einsum(
        "hsk,hsj->hkj", final_key_rows, erase_rows, precision=lax.Precision.HIGHEST
    )
    return (block_memory_state, block_trans)


def gated_read(level_gates, effective_query, level_idx, level_memory):
    return level_gates[level_idx + 1][:, :, None] * jnp.einsum(
        "aui,aij->auj", effective_query, level_memory, precision=lax.Precision.HIGHEST
    )


def fenwick_levels(block_memory_state, block_trans, position, last_level):
    identity = jnp.broadcast_to(jnp.eye(block_trans.shape[1], dtype=jnp.float32), block_trans.shape)
    prefix_trans = identity
    group_trans = block_trans
    group_state = block_memory_state
    memories = []
    for level_idx in range(last_level + 1):
        upper_half = jnp.right_shift(position, level_idx) % 2 == 1
        if level_idx < last_level:
            other_trans, other_state = from_partner((group_trans, group_state), "ctx", level_idx)
        else:
            other_state = passed_along(group_state, "ctx", 2**level_idx)
        reached = head_product(prefix_trans, other_state)
        memories.append(jnp.where(upper_half, reached, 0.0))
        if level_idx < last_level:
            prefix_trans = jnp.where(
                upper_half, head_product(prefix_trans, other_trans), prefix_trans
            )
            later_trans = jnp.where(upper_half, group_trans, other_trans)
            later_state = jnp.where(upper_half, group_state, other_state)
            earlier_state = jnp.where(upper_half, other_state, group_state)
            if level_idx + 1 < last_level:
                earlier_trans = jnp.where(upper_half, other_trans, group_trans)
                group_trans = head_product(later_trans, earlier_trans)
            group_state = head_product(later_trans, earlier_state) + later_state
    return memories


def shards(queries, key_rows, value_rows, write_strength, log_decay, level_gates):
    level_count = lax.axis_size("ctx").bit_length() - 1
    position = lax.axis_index("ctx")
    solved_parts = block_solve(queries, key_rows, value_rows, write_strength, log_decay)
    block_memory_state, block_trans = block_totals(solved_parts)
    last_level = level_count - 1
    memories = fenwick_levels(block_memory_state, block_trans, position, last_level)
    local_read, effective_query = query_terms(solved_parts)
    level_sum = gated_read(level_gates, effective_query, 0, memories[0])
    for level_idx in range(1, level_count):
        level_sum = level_sum + gated_read(
            level_gates, effective_query, level_idx, memories[level_idx]
        )
    combined = level_gates[0][:, :, None] * local_read + level_sum
    return combined.transpose(1, 0, 2).reshape(combined.shape[1], -1)


def solution(mesh):
    placed = (
        P(("groups", "ctx"), None),
        P(("groups", "ctx"), None),
        P(("groups", "ctx"), None),
        P(None, ("groups", "ctx")),
        P(None, ("groups", "ctx")),
        P(None, None, ("groups", "ctx")),
    )
    return jax.shard_map(
        shards, mesh=mesh, in_specs=placed, out_specs=P(("groups", "ctx"), None), check_vma=False
    )
```

profile of v0, /device:TPU:25, one launch (start us, length us, event | category | flops | bytes accessed | tf_op | source)
XLA Modules:
  0.0 177.8 jit_solution(14027600477914459694)
XLA Ops:
  0.1 1.1 copy.18
  2.6 0.7 copy-done.1
  4.9 1.4 fusion.14
  6.4 78.8 %custom-call.4 = f32[8,1,128,128]{2,3,1,0:T(8,128)S(1)} custom-call(f32[8,1,128,128]{3,2,1,0:T(8,128)S(1)} %fusion.14), custom_call_target="InvertDiagBlocksLowerTriangular" | custom-call | tf_op jit(solution)/shard_map/jit(_solve_triangular)/vmap()/triangular_solve | solution.py:56
  85.1 1.0 fusion.15
  86.2 2.1 %fusion.32 = f32[8,128,128]{2,1,0:T(8,128)} fusion(f32[8,128,256]{2,1,0:T(8,128)S(1)} %fusion.15, f32[128,8,128]{2,0,1:T(8,128)S(1)} %copy.19, f32[8,128]{1,0:T(8,128)S(1)} %get-tuple-element.10, f32[8,128]{1,0:T(8,128)S(1)} %get-tuple-element.13), kind=kOutput, calls=%fused_computation.57 | convolution fusion | flops 201588736 | bytes 1581056 | tf_op jit(solution)/shard_map/gjz,gjn->gzn/dot_general | solution.py:88
  88.3 0.7 collective-permute-start
  89.1 1.3 convolution_subtract_fusion
  91.1 2.1 %convolution_multiply_fusion.1 = f32[8,128,128]{2,1,0:T(8,128)} fusion(f32[128,8,128]{2,0,1:T(8,128)S(1)} %copy.17, f32[128,8,128]{2,0,1:T(8,128)S(1)} %copy.19, f32[8,128]{1,0:T(8,128)S(1)} %reduce_window_sum.11, f32[8,128]{1,0:T(8,128)S(1)} %get-tuple-element.13, f32[8,128]{1,0:T(8,128)S(1)} %add_rsqrt_fusion.1, pred[128,128]{1,0:T(8,128)(4,1)S(1)} %get-tuple-element.16), kind=kOutput, calls=%fused_computation.15 | convolution fusion | flops 202113024 | bytes 1601536 | tf_op jit(solution)/shard_map/htk,hsk->hts/dot_general | solution.py:69
  93.3 2.1 %fusion.10 = f32[128,8,128]{0,2,1:T(8,128)S(1)} fusion(f32[8,128,128]{2,1,0:T(8,128)} %convolution_multiply_fusion.1, f32[8,128,256]{2,1,0:T(8,128)S(1)} %fusion.15, f32[128,8]{0,1:T(8,128)S(1)} %get-tuple-element.8), kind=kOutput, calls=%fused_computation.29 | convolution fusion | flops 201457664 | bytes 1576960 | tf_op jit(solution)/shard_map/hts,hsv->htv/dot_general | solution.py:72
  95.4 0.7 convolution_subtract_fusion.1
  96.2 2.0 %convolution_add_fusion.2 = f32[8,128,128]{2,1,0:T(8,128)S(1)} fusion(f32[8,128,128]{2,1,0:T(8,128)} %fusion.32, f32[8,128,128]{2,1,0:T(8,128)} %collective-permute-done, pred[]{:T(512)S(6)} %eq.35, f32[8,128,128]{2,1,0:T(8,128)S(1)} %convolution_subtract_fusion, f32[8,128,128]{2,1,0:T(8,128)S(1)} %collective-permute-done.1), kind=kOutput, calls=%fused_computation.9 | convolution fusion | flops 201850880 | bytes 2621441 | tf_op jit(solution)/shard_map/hij,hjk->hik/dot_general | solution.py:29
  98.2 1.3 collective-permute-start.2
  99.5 0.7 fusion.27
  100.5 1.6 convolution_select_fusion.6
  102.7 1.0 fusion.9
  103.7 7.6 %collective-permute-done.2 = f32[8,128,128]{2,1,0:T(8,128)S(1)} collective-permute-done((f32[8,128,128]{2,1,0:T(8,128)S(1)}, f32[8,128,128]{2,1,0:T(8,128)S(1)}, u32[]{:S(2)}, u32[]{:S(2)}) %collective-permute-start.2) | collective-permute-done | bytes 524320 | tf_op jit(solution)/shard_map/ppermute | solution.py:10
  111.3 11.2 %collective-permute-done.3 = f32[8,128,128]{2,1,0:T(8,128)S(1)} collective-permute-done((f32[8,128,128]{2,1,0:T(8,128)S(1)}, f32[8,128,128]{2,1,0:T(8,128)S(1)}, u32[]{:S(2)}, u32[]{:S(2)}) %collective-permute-start.3) | collective-permute-done | bytes 524320 | tf_op jit(solution)/shard_map/ppermute | solution.py:10
  122.5 0.7 convolution_add_fusion.1
  123.4 0.9 fusion.24
  124.3 1.4 collective-permute-start.5
  126.4 0.6 convolution_select_fusion.1
  127.0 1.0 fusion.8
  128.0 7.4 %collective-permute-done.4 = f32[8,128,128]{2,1,0:T(8,128)S(1)} collective-permute-done((f32[8,128,128]{2,1,0:T(8,128)S(1)}, f32[8,128,128]{2,1,0:T(8,128)S(1)}, u32[]{:S(2)}, u32[]{:S(2)}) %collective-permute-start.4) | collective-permute-done | bytes 524320 | tf_op jit(solution)/shard_map/ppermute | solution.py:10
  135.4 11.2 %collective-permute-done.5 = f32[8,128,128]{2,1,0:T(8,128)S(1)} collective-permute-done((f32[8,128,128]{2,1,0:T(8,128)S(1)}, f32[8,128,128]{2,1,0:T(8,128)S(1)}, u32[]{:S(2)}, u32[]{:S(2)}) %collective-permute-start.5) | collective-permute-done | bytes 524320 | tf_op jit(solution)/shard_map/ppermute | solution.py:10
  146.6 0.7 convolution_add_fusion
  147.3 1.3 collective-permute-start.6
  149.3 0.6 convolution_select_fusion
  149.9 1.0 fusion.6
  151.0 24.1 %collective-permute-done.6 = f32[8,128,128]{2,1,0:T(8,128)S(1)} collective-permute-done((f32[8,128,128]{2,1,0:T(8,128)S(1)}, f32[8,128,128]{2,1,0:T(8,128)S(1)}, u32[]{:S(2)}, u32[]{:S(2)}) %collective-permute-start.6) | collective-permute-done | bytes 524320 | tf_op jit(solution)/shard_map/ppermute | solution.py:16
  175.8 1.0 fusion.4
  176.8 1.0 copy.30
  (39 shorter events, 6.9 us)
Async XLA Ops:
  1.2 0.7 copy-start.5
  2.3 1.0 copy-start.1
  3.6 0.7 copy-start.4
  88.3 7.9 %collective-permute-start = (f32[8,128,128]{2,1,0:T(8,128)}, f32[8,128,128]{2,1,0:T(8,128)}, u32[]{:S(2)}, u32[]{:S(2)}) collective-permute-start(f32[8,128,128]{2,1,0:T(8,128)} %fusion.32), channel_id=1, source_target_pairs={{0,1},{1,0},{2,3},{3,2},{4,5},{5,4},{6,7},{7,6},{8,9},{9,8},{10,11... | collective-permute-start | bytes 1572872 | tf_op jit(solution)/shard_map/ppermute | solution.py:10
  89.1 1.4 copy-start.2
  90.4 5.7 %collective-permute-start.1 = (f32[8,128,128]{2,1,0:T(8,128)S(1)}, f32[8,128,128]{2,1,0:T(8,128)S(1)}, u32[]{:S(2)}, u32[]{:S(2)}) collective-permute-start(f32[8,128,128]{2,1,0:T(8,128)S(1)} %convolution_subtract_fusion), channel_id=1, source_target_pairs={{0,1},{1,0},{2,3},{3,2},{4,5},{5,4},{6,7},{7,6},{8,9},{9,8},{10,11... | collective-permute-start | bytes 1572872 | tf_op jit(solution)/shard_map/ppermute | solution.py:10
  91.1 2.2 %copy-start.3 = (f32[5,8,128]{2,1,0:T(8,128)S(1)}, f32[5,8,128]{2,1,0:T(8,128)}, u32[]{:S(2)}) copy-start(f32[5,8,128]{2,1,0:T(8,128)} %param.11) | copy-start | bytes 61444
  93.3 2.1 %copy-start = (f32[8,128,128]{2,1,0:T(8,128)S(1)}, f32[8,128,128]{2,1,0:T(8,128)}, u32[]{:S(2)}) copy-start(f32[8,128,128]{2,1,0:T(8,128)} %convolution_multiply_fusion.1) | copy-start | bytes 1572868
  98.2 13.1 %collective-permute-start.2 = (f32[8,128,128]{2,1,0:T(8,128)S(1)}, f32[8,128,128]{2,1,0:T(8,128)S(1)}, u32[]{:S(2)}, u32[]{:S(2)}) collective-permute-start(f32[8,128,128]{2,1,0:T(8,128)S(1)} %convolution_add_fusion.2), channel_id=1, source_target_pairs={{0,2},{1,3},{2,0},{3,1},{4,6},{5,7},{6,4},{7,5},{8,10},{9,11},{10,... | collective-permute-start | bytes 1572872 | tf_op jit(solution)/shard_map/ppermute | solution.py:10
  100.1 22.4 %collective-permute-start.3 = (f32[8,128,128]{2,1,0:T(8,128)S(1)}, f32[8,128,128]{2,1,0:T(8,128)S(1)}, u32[]{:S(2)}, u32[]{:S(2)}) collective-permute-start(f32[8,128,128]{2,1,0:T(8,128)S(1)} %fusion.27), channel_id=1, source_target_pairs={{0,2},{1,3},{2,0},{3,1},{4,6},{5,7},{6,4},{7,5},{8,10},{9,11},{10,... | collective-permute-start | bytes 1572872 | tf_op jit(solution)/shard_map/ppermute | solution.py:10
  123.2 12.2 %collective-permute-start.4 = (f32[8,128,128]{2,1,0:T(8,128)S(1)}, f32[8,128,128]{2,1,0:T(8,128)S(1)}, u32[]{:S(2)}, u32[]{:S(2)}) collective-permute-start(f32[8,128,128]{2,1,0:T(8,128)S(1)} %convolution_add_fusion.1), channel_id=1, source_target_pairs={{0,4},{1,5},{2,6},{3,7},{4,0},{5,1},{6,2},{7,3},{8,12},{9,13},{10,... | collective-permute-start | bytes 1572872 | tf_op jit(solution)/shard_map/ppermute | solution.py:10
  124.3 22.3 %collective-permute-start.5 = (f32[8,128,128]{2,1,0:T(8,128)S(1)}, f32[8,128,128]{2,1,0:T(8,128)S(1)}, u32[]{:S(2)}, u32[]{:S(2)}) collective-permute-start(f32[8,128,128]{2,1,0:T(8,128)S(1)} %fusion.24), channel_id=1, source_target_pairs={{0,4},{1,5},{2,6},{3,7},{4,0},{5,1},{6,2},{7,3},{8,12},{9,13},{10,... | collective-permute-start | bytes 1572872 | tf_op jit(solution)/shard_map/ppermute | solution.py:10
  147.3 27.8 %collective-permute-start.6 = (f32[8,128,128]{2,1,0:T(8,128)S(1)}, f32[8,128,128]{2,1,0:T(8,128)S(1)}, u32[]{:S(2)}, u32[]{:S(2)}) collective-permute-start(f32[8,128,128]{2,1,0:T(8,128)S(1)} %convolution_add_fusion), channel_id=1, source_target_pairs={{0,8},{1,9},{2,10},{3,11},{4,12},{5,13},{6,14},{7,15},{16,24},{17,... | collective-permute-start | bytes 1572872 | tf_op jit(solution)/shard_map/ppermute | solution.py:16
where the time goes:
time: 178 us
  other arithmetic  80.2 us (45%)
  waiting for transfers between devices  61.6 us (35%)
  matrix products  25.3 us (14%)
  starting transfers between devices  5.23 us (3%)
  local copies, waits for them, and re-layouts  5.13 us (3%)
    another operation x3, other arithmetic, block_solve(): jax.scipy.linalg.solve_triangular(tri_matrix, right_side, lower=True, uni...  78.8 us
    ppermute x6, waiting for transfers between devices, from_partner(): lax.ppermute(value, axis, [(i, i ^ 1 << distance) for i in range(lax.axis...  37.4 us
    ppermute x1, waiting for transfers between devices, passed_along(): lax.ppermute(value, axis, [(source, source + steps) for source in range(f...  24.1 us
    dot_general x12, matrix products, head_product(): jnp.einsum('hij,hjk->hik', left, right, precision=lax.Precision.HIGHEST)  10.4 us
    dot_general x4, matrix products, gated_read(): jnp.einsum('aui,aij->auj', effective_query, level_memory, precision=lax.P...  4.03 us
    ppermute x6, starting transfers between devices, from_partner(): lax.ppermute(value, axis, [(i, i ^ 1 << distance) for i in range(lax.axis...  3.94 us
  transfers between devices with their start and end apart: 7, of which 5 were waited for; matrix products, arithmetic and copies ran while one was open for 9% of the time, Pallas kernels for 0%

commit v1 on v0

v1 whole, which is shorter than its diff:
```python
import jax
import jax.numpy as jnp
from jax import lax
from jax.experimental import pallas as pl
from jax.experimental.pallas import tpu as pltpu
from jax.sharding import PartitionSpec as P

norm_eps = 1e-06
f32 = jnp.float32
bf16 = jnp.bfloat16


def parts(value):
    high = value.astype(bf16)
    return high, (value - high.astype(f32)).astype(bf16)


def mm(left, right, dims=((1,), (0,))):
    return lax.dot_general(left, right, (dims, ((), ())), preferred_element_type=f32)


def dot_ff(left, right):
    width = right.shape[1]
    left_parts = jnp.concatenate(parts(left), axis=1)
    right_row = jnp.concatenate(parts(right), axis=1)
    both = mm(left_parts, jnp.concatenate([right_row, right_row], axis=0))
    return both[:, :width] + both[:, width:]


def dot_fb(left, right):
    left_parts = jnp.concatenate(parts(left), axis=1)
    return mm(left_parts, jnp.concatenate([right, right], axis=0))


def dot_bf_t(left, right):
    width = right.shape[1]
    both = mm(left, jnp.concatenate(parts(right), axis=1), ((0,), (0,)))
    return both[:, :width] + both[:, width:]


def block_kernel(sel_ref, q_ref, k_ref, v_ref, beta_ref, decay_ref, gates_ref, tse_ref, local_ref):
    half = tse_ref.shape[0]
    count = q_ref.shape[0]
    width = q_ref.shape[1] // half
    heads = beta_ref.shape[0]
    upper = sel_ref[0] == 1

    def chosen_first(rows):
        return jnp.where(upper, pltpu.roll(rows, half, 0), rows)

    row = lax.broadcasted_iota(jnp.int32, (count, count), 0)
    col = lax.broadcasted_iota(jnp.int32, (count, count), 1)
    summing = jnp.where(row <= col, 1.0, 0.0).astype(bf16)
    decay = decay_ref[...]
    d1 = decay.astype(bf16)
    rest = decay - d1.astype(f32)
    d2 = rest.astype(bf16)
    d3 = (rest - d2.astype(f32)).astype(bf16)
    running = chosen_first(mm(d1, summing) + (mm(d2, summing) + mm(d3, summing)))
    beta = chosen_first(beta_ref[...])
    gate = chosen_first(gates_ref[0])
    growth = jnp.exp(running)
    to_end = jnp.exp(running[:, count - 1 :] - running)
    stack = jnp.concatenate(
        [running, beta, growth, to_end, gate, jnp.zeros((count - 5 * heads, count), f32)], axis=0
    )
    columns = stack.T

    def column(kind, head):
        return columns[:, kind * heads + head : kind * heads + head + 1]

    k_rows, q_rows, k_norm = [], [], jnp.zeros((count, count), f32)
    scales = []
    for j in range(half):
        lanes = slice(j * width, (j + 1) * width)
        kj = k_ref[:, lanes]
        qj = q_ref[:, lanes]
        kf = kj.astype(f32)
        qf = qj.astype(f32)
        k_scale = lax.rsqrt(jnp.sum(kf * kf, axis=1, keepdims=True) + norm_eps)
        q_scale = lax.rsqrt(jnp.sum(qf * qf, axis=1, keepdims=True) + norm_eps)
        k_norm = jnp.where(col == j, k_scale, k_norm)
        k_rows.append(kj)
        q_rows.append(qj)
        scales.append((k_scale, q_scale))
    k_norm_rows = k_norm.T

    lower_incl = row >= col
    nexts, inverses, query_grams = [], [], []
    for j in range(half):
        k_scale, q_scale = scales[j]
        kj = k_rows[j]
        run_row = running[j : j + 1]
        gap = jnp.where(lower_incl, column(0, j) - run_row, 0.0)
        ratio = jnp.where(lower_incl, jnp.exp(gap), 0.0) * k_norm_rows[j : j + 1]
        grams = mm(jnp.concatenate([kj, q_rows[j]], axis=0), kj, ((1,), (1,)))
        below = grams[:count] * ratio * (column(1, j) * k_scale)
        query_grams.append(grams[count:] * ratio * q_scale)
        nexts.append(below)
        first = jnp.where((row ^ col) == 1, below, 0.0)
        inverses.append(jnp.where(row == col, 1.0, jnp.where(row > col, -first, 0.0)))
    level = 1
    while (1 << level) < count:
        pair = ((row >> level) ^ (col >> level)) == 1
        pair = pair & (row > col)
        for j in range(half):
            link = jnp.where(pair, nexts[j], 0.0)
            inverse = inverses[j]
            inverses[j] = inverse - dot_ff(inverse, dot_ff(link, inverse))
        level += 1
    for j in range(half):
        lanes = slice(j * width, (j + 1) * width)
        k_scale, q_scale = scales[j]
        kj = k_rows[j]
        inverse = inverses[j]
        from_query = dot_ff(query_grams[j], inverse)
        from_key = dot_bf_t(kj, inverse * (column(3, j) * k_scale))
        both = jnp.concatenate([from_query, from_key], axis=0)
        beta_row = beta[j : j + 1]
        written = dot_fb(both * beta_row, v_ref[:, lanes])
        erased = dot_fb(both * (beta_row * growth[j : j + 1] * k_norm_rows[j : j + 1]), kj)
        local_ref[:, lanes] = column(4, j) * written[:count]
        last = growth[j : j + 1, count - 1 :]
        diagonal = jnp.where(row[:width, :width] == col[:width, :width], last, 0.0)
        tse_ref[j, :, :width] = diagonal - erased[count:]
        tse_ref[j, :, width : 2 * width] = written[count:]
        tse_ref[j, :, 2 * width :] = (column(2, j) * q_scale) * q_rows[j].astype(f32) - erased[:count]


def composed(later, earlier, width):
    both = dot_ff(later[:, :width], earlier)
    return jnp.concatenate([both[:, :width], both[:, width:] + later[:, width:]], axis=1)


def pair_kernel(sel_ref, own_ref, other_ref, send_ref, keep_ref):
    width = own_ref.shape[1]
    share = send_ref.shape[0]
    odd = sel_ref[0] == 1
    x = sel_ref[1]
    for target, base in ((send_ref, (1 - x) * share), (keep_ref, x * share)):
        for j in range(share):
            own = own_ref[base + j, :, : 2 * width]
            other = other_ref[base + j, :, : 2 * width]
            later = jnp.where(odd, own, other)
            earlier = jnp.where(odd, other, own)
            target[j] = composed(later, earlier, width)


def first_read_kernel(sel_ref, own_ref, other_ref, gates_ref, gates_other_ref, eff_ref, read_ref, cols_ref):
    half, width = own_ref.shape[:2]
    count = own_ref.shape[1]
    levels, heads = gates_ref.shape[0] - 1, gates_ref.shape[1]
    odd = sel_ref[0] == 1

    def chosen_first(rows):
        return jnp.where(odd, pltpu.roll(rows, half, 0), rows)

    even_gates, odd_gates = [], []
    for b in range(levels):
        mine = chosen_first(gates_ref[b + 1])
        others = chosen_first(gates_other_ref[b + 1])
        even_gates.append(jnp.where(odd, others, mine))
        odd_gates.append(jnp.where(odd, mine, others))
    filler = [jnp.zeros((count - heads * levels, count), f32)]
    even_cols = jnp.concatenate(even_gates + filler, axis=0).T
    odd_cols = jnp.concatenate(odd_gates + filler, axis=0).T
    cols_ref[0] = even_cols
    cols_ref[1] = odd_cols
    for j in range(half):
        own = own_ref[j]
        other = other_ref[j]
        eff_even = jnp.where(odd, other[:, 2 * width :], own[:, 2 * width :])
        eff_odd = jnp.where(odd, own[:, 2 * width :], other[:, 2 * width :])
        even_total = jnp.where(odd, other[:, : 2 * width], own[:, : 2 * width])
        both = dot_ff(eff_odd, even_total)
        eff_ref[j, :count] = eff_even
        eff_ref[j, count:] = both[:, :width]
        read_ref[j, :count] = jnp.zeros((count, width), f32)
        read_ref[j, count:] = odd_cols[:, j : j + 1] * both[:, width:]


def quad_kernel(sel_ref, own_ref, other_ref, out_ref):
    width = own_ref.shape[1]
    upper = sel_ref[1] == 1
    for j in range(own_ref.shape[0]):
        own = own_ref[j]
        other = other_ref[j]
        out_ref[j] = composed(jnp.where(upper, own, other), jnp.where(upper, other, own), width)


def second_read_kernel(sel_ref, eff_ref, read_ref, cols_ref, low_ref, high_ref, eff_out, read_out):
    half, _, width = eff_ref.shape
    count = cols_ref.shape[1]
    heads = 2 * half
    share = low_ref.shape[0]
    upper = sel_ref[1] == 1
    for j in range(half):
        total = low_ref[j] if j < share else high_ref[j - share]
        eff = eff_ref[j]
        both = dot_ff(eff, total)
        eff_out[j] = jnp.where(upper, both[:, :width], eff)
        gain = jnp.concatenate([cols_ref[0, :, heads + j : heads + j + 1], cols_ref[1, :, heads + j : heads + j + 1]], axis=0)
        read_out[j] = read_ref[j] + jnp.where(upper, gain * both[:, width:], 0.0)


def climb_kernel(first, sel_ref, total_ref, prefix_ref, other_ref, memory_ref, total_out, prefix_out):
    width = total_ref.shape[1]
    upper = sel_ref[2] == 1
    for j in range(total_ref.shape[0]):
        own = total_ref[j]
        other = other_ref[j]
        if first:
            reached = other
        else:
            prefix = prefix_ref[j]
            reached = dot_ff(prefix, other)
        memory_ref[j] = jnp.where(upper, reached[:, width:], 0.0)
        if first:
            diagonal = lax.broadcasted_iota(jnp.int32, (width, width), 0) == lax.broadcasted_iota(jnp.int32, (width, width), 1)
            prefix = jnp.where(diagonal, 1.0, 0.0)
        prefix_out[j] = jnp.where(upper, reached[:, :width], prefix)
        total_out[j] = composed(jnp.where(upper, own, other), jnp.where(upper, other, own), width)


def top_kernel(sel_ref, prefix_ref, other_ref, memory_ref):
    upper = sel_ref[2] == 1
    for j in range(prefix_ref.shape[0]):
        memory_ref[j] = jnp.where(upper, dot_ff(prefix_ref[j], other_ref[j]), 0.0)


def level_read(level, upper, eff_ref, read_ref, cols_ref, own_ref, other_ref):
    half = eff_ref.shape[0]
    heads = 2 * half
    share = own_ref.shape[0]
    for j in range(half):
        own = own_ref[j % share]
        other = other_ref[j % share]
        memory = jnp.where(upper, other, own) if j < share else jnp.where(upper, own, other)
        at = level * heads + j
        gain = jnp.concatenate([cols_ref[0, :, at : at + 1], cols_ref[1, :, at : at + 1]], axis=0)
        yield j, read_ref[j] + gain * dot_ff(eff_ref[j], memory)


def read_kernel(level, sel_ref, eff_ref, read_ref, cols_ref, own_ref, other_ref, read_out):
    for j, total in level_read(level, sel_ref[1] == 1, eff_ref, read_ref, cols_ref, own_ref, other_ref):
        read_out[j] = total


def last_read_kernel(level, sel_ref, eff_ref, read_ref, cols_ref, own_ref, other_ref, keep_ref, send_ref):
    count = cols_ref.shape[1]
    width = eff_ref.shape[2]
    odd = sel_ref[0] == 1
    for j, total in level_read(level, sel_ref[1] == 1, eff_ref, read_ref, cols_ref, own_ref, other_ref):
        lanes = slice(j * width, (j + 1) * width)
        keep_ref[:, lanes] = jnp.where(odd, total[count:], total[:count])
        send_ref[:, lanes] = jnp.where(odd, total[:count], total[count:])


def join_kernel(sel_ref, keep_ref, got_ref, local_own_ref, local_other_ref, out_ref):
    span = keep_ref.shape[1]
    odd = sel_ref[0] == 1
    own = keep_ref[...] + local_own_ref[...]
    other = got_ref[...] + local_other_ref[...]
    out_ref[:, :span] = jnp.where(odd, other, own)
    out_ref[:, span:] = jnp.where(odd, own, other)


def run(kernel, out_shapes, sel, *arrays, name):
    return pl.pallas_call(
        kernel,
        out_shape=out_shapes,
        in_specs=[pl.BlockSpec(memory_space=pltpu.SMEM)]
        + [pl.BlockSpec(memory_space=pltpu.VMEM)] * len(arrays),
        name=name,
    )(sel, *arrays)


def array(*shape):
    return jax.ShapeDtypeStruct(shape, f32)


def block_half(which, half, queries, key_rows, value_rows, write_strength, log_decay, level_gates):
    count = queries.shape[0]
    width = queries.shape[1] // (2 * half)
    value_width = value_rows.shape[1] // (2 * half)
    wide = pl.BlockSpec((count, half * width), lambda i, which_ref: (0, which_ref[0]))
    whole = lambda value: pl.BlockSpec(value.shape, lambda i, which_ref: (0,) * value.ndim)
    return pl.pallas_call(
        block_kernel,
        grid_spec=pltpu.PrefetchScalarGridSpec(
            num_scalar_prefetch=1,
            grid=(1,),
            in_specs=[wide, wide, wide, whole(write_strength), whole(log_decay), whole(level_gates)],
            out_specs=[
                pl.BlockSpec((half, count, 2 * width + value_width), lambda i, which_ref: (0, 0, 0)),
                pl.BlockSpec((count, half * value_width), lambda i, which_ref: (0, 0)),
            ],
        ),
        out_shape=[array(half, count, 2 * width + value_width), array(count, half * value_width)],
        name="block",
    )(which, queries, key_rows, value_rows, write_strength, log_decay, level_gates)


def shards(queries, key_rows, value_rows, write_strength, log_decay, level_gates):
    size = lax.axis_size("ctx")
    levels = size.bit_length() - 1
    position = lax.axis_index("ctx")
    heads = write_strength.shape[0]
    half, share = heads // 2, heads // 4
    count = queries.shape[0]
    width = queries.shape[1] // heads
    core = position & 1
    row = (position >> 1) & 1
    inputs = (queries, key_rows, value_rows, write_strength, log_decay, level_gates)

    def swapped(value, bit):
        return lax.ppermute(value, "ctx", [(i, i ^ (1 << bit)) for i in range(size)])

    def choice(bit):
        return jnp.stack([core, row, (position >> bit) & 1]).astype(jnp.int32)

    sel = choice(2)
    gates_other = swapped(level_gates, 0)
    send, local_other = block_half((1 - core).reshape(1), half, *inputs)
    got = swapped(send, 0)
    own, local_own = block_half(core.reshape(1), half, *inputs)
    pair_send, pair_keep = run(
        pair_kernel, [array(share, width, 2 * width)] * 2, sel, own, got, name="pair"
    )
    pair_got = swapped(pair_send, 1)
    eff, read, cols = run(
        first_read_kernel,
        [array(half, 2 * count, width), array(half, 2 * count, width), array(2, count, count)],
        sel, own, got, level_gates, gates_other, name="read0",
    )
    total = run(quad_kernel, array(share, width, 2 * width), sel, pair_keep, pair_got, name="quad")
    low = lax.ppermute(
        pair_keep, "ctx", [(i, i + 2) for i in range(size) if (i >> 1) & 1 == 0]
    )
    prefix = None
    for level in range(2, levels):
        sel_level = choice(level)
        if level < levels - 1:
            other = swapped(total, level)
            first = prefix is None
            if first:
                prefix = jnp.zeros((share, width, width), f32)
            memory, total, prefix = run(
                lambda *refs, first=first: climb_kernel(first, *refs),
                [array(share, width, width), array(share, width, 2 * width), array(share, width, width)],
                sel_level, total, prefix, other, name="climb",
            )
        else:
            distance = 1 << level
            other = lax.ppermute(
                total[:, :, width:], "ctx", [(i, i + distance) for i in range(size - distance)]
            )
            memory = run(top_kernel, array(share, width, width), sel_level, prefix, other, name="top")
        memory_other = swapped(memory, 1)
        if level == 2:
            eff, read = run(
                second_read_kernel,
                [array(half, 2 * count, width), array(half, 2 * count, width)],
                sel, eff, read, cols, low, pair_got, name="read1",
            )
        if level < levels - 1:
            read = run(
                lambda *refs, level=level: read_kernel(level, *refs),
                array(half, 2 * count, width),
                sel, eff, read, cols, memory, memory_other, name="readn",
            )
        else:
            keep, away = run(
                lambda *refs, level=level: last_read_kernel(level, *refs),
                [array(count, half * width)] * 2,
                sel, eff, read, cols, memory, memory_other, name="readlast",
            )
    back = swapped(away, 0)
    return run(
        join_kernel, array(count, heads * width), sel, keep, back, local_own, local_other, name="join"
    )


def solution(mesh):
    placed = (
        P(("groups", "ctx"), None),
        P(("groups", "ctx"), None),
        P(("groups", "ctx"), None),
        P(None, ("groups", "ctx")),
        P(None, ("groups", "ctx")),
        P(None, None, ("groups", "ctx")),
    )
    return jax.shard_map(
        shards, mesh=mesh, in_specs=placed, out_specs=P(("groups", "ctx"), None), check_vma=False
    )
```

time: 178 us -> 72.2 us (0.41)
  other arithmetic: 80.2 us -> 1.2 us
  waiting for transfers between devices: 61.6 us -> 20 us
  Pallas kernels: 0 us -> 32.4 us
  matrix products: 25.3 us -> 0 us
  starting transfers between devices: 5.23 us -> 10.8 us
  local copies, waits for them, and re-layouts: 5.13 us -> 7.31 us
    another operation x4 -> x2, other arithmetic: 79.1 us -> 1.2 us  [choice(): return jnp.stack([core, row, position >> bit & 1]).astype(jnp.int32)]
    ppermute x7 -> x9, waiting for transfers between devices: 61.6 us -> 20 us  [the longest x7 13 us: swapped(): return lax.ppermute(value, 'ctx', [(i, i ^ 1 << bit) for i in range(size)])]
    pallas_call x0 -> x11, Pallas kernels: none -> 32.4 us  [the longest x9 20.9 us: run(): pl.pallas_call(kernel, out_shape=out_shapes, in_specs=[pl.BlockSpec(memor...]
    dot_general x22 -> x0, matrix products: 24.2 us -> none  [the longest x12 10.4 us: head_product(): jnp.einsum('hij,hjk->hik', left, right, precision=lax.Precision.HIGHEST)]
    ppermute x7 -> x9, starting transfers between devices: 5.23 us -> 10.8 us  [the longest x7 6.4 us: swapped(): return lax.ppermute(value, 'ctx', [(i, i ^ 1 << bit) for i in range(size)])]
    unnamed x15 -> x24, local copies, waits for them, and re-layouts: 3.33 us -> 5.65 us
  transfers between devices with their start and end apart: 7 -> 9, of which waited for: 5 -> 5; matrix products, arithmetic and copies ran while one was open for 9% -> 4% of each run, Pallas kernels for 0% -> 25%
where the time goes in v1:
time: 72.2 us; the launch traced here: 71.7 us
  Pallas kernels  32.4 us (45%)
  waiting for transfers between devices  20 us (28%)
  starting transfers between devices  10.8 us (15%)
  local copies, waits for them, and re-layouts  7.31 us (10%)
  other arithmetic  1.2 us (2%)
    pallas_call x9, Pallas kernels, run(): pl.pallas_call(kernel, out_shape=out_shapes, in_specs=[pl.BlockSpec(memor...  20.9 us
    ppermute x7, waiting for transfers between devices, swapped(): return lax.ppermute(value, 'ctx', [(i, i ^ 1 << bit) for i in range(size)])  13 us
    pallas_call x2, Pallas kernels, block_half(): pl.pallas_call(block_kernel, grid_spec=pltpu.PrefetchScalarGridSpec(num_s...  11.5 us
    ppermute x1, waiting for transfers between devices, shards(): lax.ppermute(total[:, :, width:], 'ctx', [(i, i + distance) for i in rang...  7 us
    ppermute x7, starting transfers between devices, swapped(): return lax.ppermute(value, 'ctx', [(i, i ^ 1 << bit) for i in range(size)])  6.4 us
    unnamed x24, local copies, waits for them, and re-layouts  5.65 us
    ppermute x1, starting transfers between devices, shards(): lax.ppermute(pair_keep, 'ctx', [(i, i + 2) for i in range(size) if i >> 1...  3.09 us
  transfers between devices with their start and end apart: 9, of which 5 were waited for; matrix products, arithmetic and copies ran while one was open for 4% of the time, Pallas kernels for 25%

profile of v1, /device:TPU:25, one launch (start us, length us, event | category | flops | bytes accessed | tf_op | source)
XLA Modules:
  0.0 71.7 jit_solution(11877051370536294213)
XLA Ops:
  0.0 5.7 %block.3 = (f32[4,128,384]{2,1,0:T(8,128)}, f32[128,512]{1,0:T(8,128)}) custom-call(s32[1]{0:T(128)} %bitcast.3.sel_ref, bf16[128,1024]{1,0:T(8,128)(2,1)} %q_ref.3, bf16[128,1024]{1,0:T(8,128)(2,1)} %k_ref.3, bf16[128,1024]{1,0:T(8,128)(2,1)} %v_ref.3, f32[8,128]{1,0:T(8,128)} %beta_ref.3, f32[8,128]{1,0:T(8,128)} %decay_ref.3, f32[5,8,128]{2,1,0:T(8,128)} %gates_ref.5), custom_call_target="tpu_custom_call" | custom-call | tf_op jit(solution)/shard_map/block/pallas_call | solution.py:288
  5.7 0.7 collective-permute-start
  6.4 5.7 %block.2 = (f32[4,128,384]{2,1,0:T(8,128)}, f32[128,512]{1,0:T(8,128)}) custom-call(s32[1]{0:T(128)} %bitcast.sel_ref, bf16[128,1024]{1,0:T(8,128)(2,1)} %q_ref.3, bf16[128,1024]{1,0:T(8,128)(2,1)} %k_ref.3, bf16[128,1024]{1,0:T(8,128)(2,1)} %v_ref.3, f32[8,128]{1,0:T(8,128)} %beta_ref.3, f32[8,128]{1,0:T(8,128)} %decay_ref.3, f32[5,8,128]{2,1,0:T(8,128)} %gates_ref.5), custom_call_target="tpu_custom_call" | custom-call | tf_op jit(solution)/shard_map/block/pallas_call | solution.py:288
  12.7 0.9 %copy-done = f32[4,128,384]{2,1,0:T(8,128)} copy-done((f32[4,128,384]{2,1,0:T(8,128)}, f32[4,128,384]{2,1,0:T(8,128)S(1)}, u32[]{:S(2)}) %copy-start) | copy-done | bytes 786456
  13.6 2.4 %pair.1 = (f32[2,128,256]{2,1,0:T(8,128)}, f32[2,128,256]{2,1,0:T(8,128)}) custom-call(s32[3]{0:T(128)} %pad_add_fusion.sel_ref.refs_0_, f32[4,128,384]{2,1,0:T(8,128)} %get-tuple-element.21.own_ref, f32[4,128,384]{2,1,0:T(8,128)} %copy-done), custom_call_target="tpu_custom_call" | custom-call | tf_op jit(solution)/shard_map/pair/pallas_call | solution.py:269
  16.1 1.2 %collective-permute-start.3 = (f32[2,128,256]{2,1,0:T(8,128)}, f32[2,128,256]{2,1,0:T(8,128)S(1)}, u32[]{:S(2)}, u32[]{:S(2)}) collective-permute-start(f32[2,128,256]{2,1,0:T(8,128)} %get-tuple-element.27), channel_id=1, source_target_pairs={{0,2},{1,3},{2,0},{3,1},{4,6},{5,7},{6,4},{7,5},{8,10},{9,11},{10,... | collective-permute-start | bytes 786440 | tf_op jit(solution)/shard_map/ppermute | solution.py:317
  17.3 6.8 %collective-permute-done.3.high_ref.other_ref = f32[2,128,256]{2,1,0:T(8,128)S(1)} collective-permute-done((f32[2,128,256]{2,1,0:T(8,128)}, f32[2,128,256]{2,1,0:T(8,128)S(1)}, u32[]{:S(2)}, u32[]{:S(2)}) %collective-permute-start.3) | collective-permute-done | bytes 262176 | tf_op jit(solution)/shard_map/ppermute | solution.py:317
  24.2 0.7 copy-done.1
  24.9 2.0 %quad.1.refs_1_ = f32[2,128,256]{2,1,0:T(8,128)} custom-call(s32[3]{0:T(128)} %pad_add_fusion.sel_ref.refs_0_, f32[2,128,256]{2,1,0:T(8,128)} %get-tuple-element.26.own_ref, f32[2,128,256]{2,1,0:T(8,128)} %copy-done.1), custom_call_target="tpu_custom_call" | custom-call | tf_op jit(solution)/shard_map/quad/pallas_call | solution.py:269
  27.1 3.1 %collective-permute-start.2 = (f32[2,128,256]{2,1,0:T(8,128)S(1)}, f32[2,128,256]{2,1,0:T(8,128)S(1)}, u32[]{:S(2)}, u32[]{:S(2)}) collective-permute-start(f32[2,128,256]{2,1,0:T(8,128)S(1)} %copy-done.4), channel_id=1, source_target_pairs={{0,2},{1,3},{4,6},{5,7},{8,10},{9,11},{12,14},{13,15},{16,18},{17,... | collective-permute-start | bytes 786440 | tf_op jit(solution)/shard_map/ppermute | solution.py:337
  30.2 3.9 %collective-permute-done.4.refs_3_ = f32[2,128,256]{2,1,0:T(8,128)S(1)} collective-permute-done((f32[2,128,256]{2,1,0:T(8,128)}, f32[2,128,256]{2,1,0:T(8,128)S(1)}, u32[]{:S(2)}, u32[]{:S(2)}) %collective-permute-start.4) | collective-permute-done | bytes 262176 | tf_op jit(solution)/shard_map/ppermute | solution.py:317
  34.1 0.7 broadcast_in_dim.3.refs_2_
  34.9 2.1 %climb.1 = (f32[2,128,128]{2,1,0:T(8,128)}, f32[2,128,256]{2,1,0:T(8,128)}, f32[2,128,128]{2,1,0:T(8,128)}) custom-call(s32[3]{0:T(128)} %pad_add_fusion.sel_ref.refs_0_, f32[2,128,256]{2,1,0:T(8,128)} %quad.1.refs_1_, f32[2,128,128]{2,1,0:T(8,128)} %broadcast_in_dim.3.refs_2_, f32[2,128,256]{2,1,0:T(8,128)} %copy-done.3), custom_call_target="tpu_custom_call" | custom-call | tf_op jit(solution)/shard_map/climb/pallas_call | solution.py:269
  37.0 0.9 %slice.3 = f32[2,128,128]{2,1,0:T(8,128)S(1)} slice(f32[2,128,256]{2,1,0:T(8,128)} %get-tuple-element.32), slice={[0:2], [0:128], [128:256]} | slice | bytes 262144 | tf_op jit(solution)/shard_map/slice | solution.py:356
  37.9 1.3 %collective-permute-start.6 = (f32[2,128,128]{2,1,0:T(8,128)S(1)}, f32[2,128,128]{2,1,0:T(8,128)S(1)}, u32[]{:S(2)}, u32[]{:S(2)}) collective-permute-start(f32[2,128,128]{2,1,0:T(8,128)S(1)} %slice.3), channel_id=1, source_target_pairs={{0,8},{1,9},{2,10},{3,11},{4,12},{5,13},{6,14},{7,15},{16,24},{17,... | collective-permute-start | bytes 393224 | tf_op jit(solution)/shard_map/ppermute | solution.py:355
  39.9 1.3 %collective-permute-start.5 = (f32[2,128,128]{2,1,0:T(8,128)S(1)}, f32[2,128,128]{2,1,0:T(8,128)S(1)}, u32[]{:S(2)}, u32[]{:S(2)}) collective-permute-start(f32[2,128,128]{2,1,0:T(8,128)S(1)} %copy-done.7), channel_id=1, source_target_pairs={{0,2},{1,3},{2,0},{3,1},{4,6},{5,7},{6,4},{7,5},{8,10},{9,11},{10,... | collective-permute-start | bytes 393224 | tf_op jit(solution)/shard_map/ppermute | solution.py:317
  41.2 7.0 %collective-permute-done.6.other_ref = f32[2,128,128]{2,1,0:T(8,128)S(1)} collective-permute-done((f32[2,128,128]{2,1,0:T(8,128)S(1)}, f32[2,128,128]{2,1,0:T(8,128)S(1)}, u32[]{:S(2)}, u32[]{:S(2)}) %collective-permute-start.6) | collective-permute-done | bytes 131104 | tf_op jit(solution)/shard_map/ppermute | solution.py:355
  48.2 0.7 copy-done.9
  48.8 1.8 %top.1.refs_4_ = f32[2,128,128]{2,1,0:T(8,128)} custom-call(s32[3]{0:T(128)} %pad_add_fusion.2.sel_ref, f32[2,128,128]{2,1,0:T(8,128)} %get-tuple-element.31.prefix_ref, f32[2,128,128]{2,1,0:T(8,128)} %copy-done.9), custom_call_target="tpu_custom_call" | custom-call | tf_op jit(solution)/shard_map/top/pallas_call | solution.py:269
  50.7 1.1 %collective-permute-start.7 = (f32[2,128,128]{2,1,0:T(8,128)}, f32[2,128,128]{2,1,0:T(8,128)S(1)}, u32[]{:S(2)}, u32[]{:S(2)}) collective-permute-start(f32[2,128,128]{2,1,0:T(8,128)} %top.1.refs_4_), channel_id=1, source_target_pairs={{0,2},{1,3},{2,0},{3,1},{4,6},{5,7},{6,4},{7,5},{8,10},{9,11},{10,... | collective-permute-start | bytes 393224 | tf_op jit(solution)/shard_map/ppermute | solution.py:317
  51.8 1.5 %collective-permute-start.1 = (f32[5,8,128]{2,1,0:T(8,128)S(1)}, f32[5,8,128]{2,1,0:T(8,128)S(1)}, u32[]{:S(2)}, u32[]{:S(2)}) collective-permute-start(f32[5,8,128]{2,1,0:T(8,128)S(1)} %copy-done.6), channel_id=1, source_target_pairs={{0,1},{1,0},{2,3},{3,2},{4,5},{5,4},{6,7},{7,6},{8,9},{9,8},{10,11... | collective-permute-start | bytes 61448 | tf_op jit(solution)/shard_map/ppermute | solution.py:317
  53.4 0.8 %collective-permute-done.1.gates_other_ref = f32[5,8,128]{2,1,0:T(8,128)S(1)} collective-permute-done((f32[5,8,128]{2,1,0:T(8,128)S(1)}, f32[5,8,128]{2,1,0:T(8,128)S(1)}, u32[]{:S(2)}, u32[]{:S(2)}) %collective-permute-start.1) | collective-permute-done | bytes 20512 | tf_op jit(solution)/shard_map/ppermute | solution.py:317
  54.8 2.7 %read0.1 = (f32[4,256,128]{2,1,0:T(8,128)}, f32[4,256,128]{2,1,0:T(8,128)}, f32[2,128,128]{2,1,0:T(8,128)}) custom-call(s32[3]{0:T(128)} %pad_add_fusion.sel_ref.refs_0_, f32[4,128,384]{2,1,0:T(8,128)} %get-tuple-element.21.own_ref, f32[4,128,384]{2,1,0:T(8,128)} %copy-done, f32[5,8,128]{2,1,0:T(8,128)} %gates_ref.5, f32[5,8,128]{2,1,0:T(8,128)} %copy-done.11), custom_call_target="tpu_custom_call" | custom-call | tf_op jit(solution)/shard_map/read0/pallas_call | solution.py:269
  57.5 0.7 copy-done.2
  58.2 2.8 %read1.1 = (f32[4,256,128]{2,1,0:T(8,128)}, f32[4,256,128]{2,1,0:T(8,128)}) custom-call(s32[3]{0:T(128)} %pad_add_fusion.sel_ref.refs_0_, f32[4,256,128]{2,1,0:T(8,128)} %get-tuple-element.23.eff_ref, f32[4,256,128]{2,1,0:T(8,128)} %get-tuple-element.24.read_ref, f32[2,128,128]{2,1,0:T(8,128)} %get-tuple-element.25.cols_ref.refs_3_, ...), custom_call_target="tpu_custom_call" | custom-call | tf_op jit(solution)/shard_map/read1/pallas_call | solution.py:269
  61.1 0.7 copy-done.8
  61.7 2.4 %readn.1.refs_2_ = f32[4,256,128]{2,1,0:T(8,128)} custom-call(s32[3]{0:T(128)} %pad_add_fusion.sel_ref.refs_0_, f32[4,256,128]{2,1,0:T(8,128)} %get-tuple-element.28.refs_1_, f32[4,256,128]{2,1,0:T(8,128)} %get-tuple-element.29.refs_2_, f32[2,128,128]{2,1,0:T(8,128)} %get-tuple-element.25.cols_ref.refs_3_, f32[2,128,128]{2,1,0:T(8,128)} %get-tuple-element.30.refs_4_, ...), custom_call_target="tpu_custom_call" | custom-call | tf_op jit(solution)/shard_map/readn/pallas_call | solution.py:269
  64.2 0.7 copy-done.10
  64.8 2.4 %readlast.1 = (f32[128,512]{1,0:T(8,128)}, f32[128,512]{1,0:T(8,128)}) custom-call(s32[3]{0:T(128)} %pad_add_fusion.sel_ref.refs_0_, f32[4,256,128]{2,1,0:T(8,128)} %get-tuple-element.28.refs_1_, f32[4,256,128]{2,1,0:T(8,128)} %readn.1.refs_2_, f32[2,128,128]{2,1,0:T(8,128)} %get-tuple-element.25.cols_ref.refs_3_, f32[2,128,128]{2,1,0:T(8,128)} %top.1.refs_4_, ...), custom_call_target="tpu_custom_call" | custom-call | tf_op jit(solution)/shard_map/readlast/pallas_call | solution.py:269
  67.6 1.4 %collective-permute-done.8.got_ref = f32[128,512]{1,0:T(8,128)S(1)} collective-permute-done((f32[128,512]{1,0:T(8,128)}, f32[128,512]{1,0:T(8,128)S(1)}, u32[]{:S(2)}, u32[]{:S(2)}) %collective-permute-start.8) | collective-permute-done | bytes 262176 | tf_op jit(solution)/shard_map/ppermute | solution.py:317
  69.0 0.7 copy-done.5
  69.7 2.0 %join.1 = f32[128,1024]{1,0:T(8,128)} custom-call(s32[3]{0:T(128)} %pad_add_fusion.sel_ref.refs_0_, f32[128,512]{1,0:T(8,128)} %get-tuple-element.33.keep_ref, f32[128,512]{1,0:T(8,128)} %copy-done.5, f32[128,512]{1,0:T(8,128)} %get-tuple-element.35.local_own_ref, f32[128,512]{1,0:T(8,128)} %get-tuple-element.36.local_other_ref), custom_call_target="tpu_custom_call" | custom-call | tf_op jit(solution)/shard_map/join/pallas_call | solution.py:269
  (25 shorter events, 2.4 us)
Async XLA Ops:
  5.7 7.0 %collective-permute-start = (f32[4,128,384]{2,1,0:T(8,128)}, f32[4,128,384]{2,1,0:T(8,128)S(1)}, u32[]{:S(2)}, u32[]{:S(2)}) collective-permute-start(f32[4,128,384]{2,1,0:T(8,128)} %get-tuple-element.22), channel_id=1, source_target_pairs={{0,1},{1,0},{2,3},{3,2},{4,5},{5,4},{6,7},{7,6},{8,9},{9,8},{10,11... | collective-permute-start | bytes 2359304 | tf_op jit(solution)/shard_map/ppermute | solution.py:317
  12.7 0.9 %copy-start = (f32[4,128,384]{2,1,0:T(8,128)}, f32[4,128,384]{2,1,0:T(8,128)S(1)}, u32[]{:S(2)}) copy-start(f32[4,128,384]{2,1,0:T(8,128)S(1)} %collective-permute-done.other_ref) | copy-start | bytes 2359300
  16.1 8.1 %collective-permute-start.3 = (f32[2,128,256]{2,1,0:T(8,128)}, f32[2,128,256]{2,1,0:T(8,128)S(1)}, u32[]{:S(2)}, u32[]{:S(2)}) collective-permute-start(f32[2,128,256]{2,1,0:T(8,128)} %get-tuple-element.27), channel_id=1, source_target_pairs={{0,2},{1,3},{2,0},{3,1},{4,6},{5,7},{6,4},{7,5},{8,10},{9,11},{10,... | collective-permute-start | bytes 786440 | tf_op jit(solution)/shard_map/ppermute | solution.py:317
  24.1 0.7 %copy-start.1 = (f32[2,128,256]{2,1,0:T(8,128)}, f32[2,128,256]{2,1,0:T(8,128)S(1)}, u32[]{:S(2)}) copy-start(f32[2,128,256]{2,1,0:T(8,128)S(1)} %collective-permute-done.3.high_ref.other_ref) | copy-start | bytes 786436
  24.9 2.2 %copy-start.4 = (f32[2,128,256]{2,1,0:T(8,128)S(1)}, f32[2,128,256]{2,1,0:T(8,128)}, u32[]{:S(2)}) copy-start(f32[2,128,256]{2,1,0:T(8,128)} %get-tuple-element.26.own_ref) | copy-start | bytes 786436
  26.9 7.2 %collective-permute-start.4 = (f32[2,128,256]{2,1,0:T(8,128)}, f32[2,128,256]{2,1,0:T(8,128)S(1)}, u32[]{:S(2)}, u32[]{:S(2)}) collective-permute-start(f32[2,128,256]{2,1,0:T(8,128)} %quad.1.refs_1_), channel_id=1, source_target_pairs={{0,4},{1,5},{2,6},{3,7},{4,0},{5,1},{6,2},{7,3},{8,12},{9,13},{10,... | collective-permute-start | bytes 786440 | tf_op jit(solution)/shard_map/ppermute | solution.py:317
  27.1 30.4 %collective-permute-start.2 = (f32[2,128,256]{2,1,0:T(8,128)S(1)}, f32[2,128,256]{2,1,0:T(8,128)S(1)}, u32[]{:S(2)}, u32[]{:S(2)}) collective-permute-start(f32[2,128,256]{2,1,0:T(8,128)S(1)} %copy-done.4), channel_id=1, source_target_pairs={{0,2},{1,3},{4,6},{5,7},{8,10},{9,11},{12,14},{13,15},{16,18},{17,... | collective-permute-start | bytes 786440 | tf_op jit(solution)/shard_map/ppermute | solution.py:337
  34.1 0.8 %copy-start.3 = (f32[2,128,256]{2,1,0:T(8,128)}, f32[2,128,256]{2,1,0:T(8,128)S(1)}, u32[]{:S(2)}) copy-start(f32[2,128,256]{2,1,0:T(8,128)S(1)} %collective-permute-done.4.refs_3_) | copy-start | bytes 786436
  37.0 2.9 %copy-start.7 = (f32[2,128,128]{2,1,0:T(8,128)S(1)}, f32[2,128,128]{2,1,0:T(8,128)}, u32[]{:S(2)}) copy-start(f32[2,128,128]{2,1,0:T(8,128)} %get-tuple-element.30.refs_4_) | copy-start | bytes 393220
  37.9 10.2 %collective-permute-start.6 = (f32[2,128,128]{2,1,0:T(8,128)S(1)}, f32[2,128,128]{2,1,0:T(8,128)S(1)}, u32[]{:S(2)}, u32[]{:S(2)}) collective-permute-start(f32[2,128,128]{2,1,0:T(8,128)S(1)} %slice.3), channel_id=1, source_target_pairs={{0,8},{1,9},{2,10},{3,11},{4,12},{5,13},{6,14},{7,15},{16,24},{17,... | collective-permute-start | bytes 393224 | tf_op jit(solution)/shard_map/ppermute | solution.py:355
  39.9 21.2 %collective-permute-start.5 = (f32[2,128,128]{2,1,0:T(8,128)S(1)}, f32[2,128,128]{2,1,0:T(8,128)S(1)}, u32[]{:S(2)}, u32[]{:S(2)}) collective-permute-start(f32[2,128,128]{2,1,0:T(8,128)S(1)} %copy-done.7), channel_id=1, source_target_pairs={{0,2},{1,3},{2,0},{3,1},{4,6},{5,7},{6,4},{7,5},{8,10},{9,11},{10,... | collective-permute-start | bytes 393224 | tf_op jit(solution)/shard_map/ppermute | solution.py:317
  48.2 0.7 copy-start.9
  48.8 3.0 %copy-start.6 = (f32[5,8,128]{2,1,0:T(8,128)S(1)}, f32[5,8,128]{2,1,0:T(8,128)}, u32[]{:S(2)}) copy-start(f32[5,8,128]{2,1,0:T(8,128)} %gates_ref.5) | copy-start | bytes 61444
  50.7 13.5 %collective-permute-start.7 = (f32[2,128,128]{2,1,0:T(8,128)}, f32[2,128,128]{2,1,0:T(8,128)S(1)}, u32[]{:S(2)}, u32[]{:S(2)}) collective-permute-start(f32[2,128,128]{2,1,0:T(8,128)} %top.1.refs_4_), channel_id=1, source_target_pairs={{0,2},{1,3},{2,0},{3,1},{4,6},{5,7},{6,4},{7,5},{8,10},{9,11},{10,... | collective-permute-start | bytes 393224 | tf_op jit(solution)/shard_map/ppermute | solution.py:317
  51.8 2.4 %collective-permute-start.1 = (f32[5,8,128]{2,1,0:T(8,128)S(1)}, f32[5,8,128]{2,1,0:T(8,128)S(1)}, u32[]{:S(2)}, u32[]{:S(2)}) collective-permute-start(f32[5,8,128]{2,1,0:T(8,128)S(1)} %copy-done.6), channel_id=1, source_target_pairs={{0,1},{1,0},{2,3},{3,2},{4,5},{5,4},{6,7},{7,6},{8,9},{9,8},{10,11... | collective-permute-start | bytes 61448 | tf_op jit(solution)/shard_map/ppermute | solution.py:317
  54.2 0.6 copy-start.11
  57.5 0.7 copy-start.2
  61.1 0.7 copy-start.8
  64.2 0.7 copy-start.10
  67.2 1.7 %collective-permute-start.8 = (f32[128,512]{1,0:T(8,128)}, f32[128,512]{1,0:T(8,128)S(1)}, u32[]{:S(2)}, u32[]{:S(2)}) collective-permute-start(f32[128,512]{1,0:T(8,128)} %get-tuple-element.34), channel_id=1, source_target_pairs={{0,1},{1,0},{2,3},{3,2},{4,5},{5,4},{6,7},{7,6},{8,9},{9,8},{10,11... | collective-permute-start | bytes 786440 | tf_op jit(solution)/shard_map/ppermute | solution.py:317
  69.0 0.7 copy-start.5

commit v2 on v1

v2 whole, which is shorter than its diff:
```python
import jax
import jax.numpy as jnp
from jax import lax
from jax.experimental import pallas as pl
from jax.experimental.pallas import tpu as pltpu
from jax.sharding import PartitionSpec as P

norm_eps = 1e-06
f32 = jnp.float32
bf16 = jnp.bfloat16


def parts(value):
    high = value.astype(bf16)
    return high, (value - high.astype(f32)).astype(bf16)


def mm(left, right, dims=((1,), (0,))):
    return lax.dot_general(left, right, (dims, ((), ())), preferred_element_type=f32)


def dot_ff(left, right):
    width = right.shape[1]
    left_parts = jnp.concatenate(parts(left), axis=1)
    right_row = jnp.concatenate(parts(right), axis=1)
    both = mm(left_parts, jnp.concatenate([right_row, right_row], axis=0))
    return both[:, :width] + both[:, width:]


def dot_fb(left, right):
    left_parts = jnp.concatenate(parts(left), axis=1)
    return mm(left_parts, jnp.concatenate([right, right], axis=0))


def dot_bf_t(left, right):
    width = right.shape[1]
    both = mm(left, jnp.concatenate(parts(right), axis=1), ((0,), (0,)))
    return both[:, :width] + both[:, width:]


def bit_of(pos_ref, bit):
    return ((pos_ref[0] >> bit) & 1) == 1


def block_kernel(mine, pos_ref, q_ref, k_ref, v_ref, beta_ref, decay_ref, gates_ref, planes_ref, local_ref):
    heads = beta_ref.shape[0]
    half = heads // 2
    count = q_ref.shape[0]
    width = q_ref.shape[1] // half
    upper = bit_of(pos_ref, 0) if mine else jnp.logical_not(bit_of(pos_ref, 0))

    def chosen_first(rows):
        return jnp.where(upper, pltpu.roll(rows, half, 0), rows)

    row = lax.broadcasted_iota(jnp.int32, (count, count), 0)
    col = lax.broadcasted_iota(jnp.int32, (count, count), 1)
    summing = jnp.where(row <= col, 1.0, 0.0).astype(bf16)
    decay = decay_ref[...]
    d1 = decay.astype(bf16)
    rest = decay - d1.astype(f32)
    d2 = rest.astype(bf16)
    d3 = (rest - d2.astype(f32)).astype(bf16)
    running = chosen_first(mm(d1, summing) + (mm(d2, summing) + mm(d3, summing)))
    beta = chosen_first(beta_ref[...])
    growth = jnp.exp(running)
    to_end = jnp.exp(running[:, count - 1 :] - running)
    kinds = [running, beta, growth, to_end] + [chosen_first(gates_ref[b]) for b in range(gates_ref.shape[0])]
    filler = jnp.zeros((count - len(kinds) * heads, count), f32)
    columns = jnp.concatenate(kinds + [filler], axis=0).T
    planes_ref[3 * half] = columns

    def column(kind, head):
        return columns[:, kind * heads + head : kind * heads + head + 1]

    k_rows, q_rows, k_norm = [], [], jnp.zeros((count, count), f32)
    scales = []
    for j in range(half):
        lanes = slice(j * width, (j + 1) * width)
        kj = k_ref[:, lanes]
        qj = q_ref[:, lanes]
        kf = kj.astype(f32)
        qf = qj.astype(f32)
        k_scale = lax.rsqrt(jnp.sum(kf * kf, axis=1, keepdims=True) + norm_eps)
        q_scale = lax.rsqrt(jnp.sum(qf * qf, axis=1, keepdims=True) + norm_eps)
        k_norm = jnp.where(col == j, k_scale, k_norm)
        k_rows.append(kj)
        q_rows.append(qj)
        scales.append((k_scale, q_scale))
    k_norm_rows = k_norm.T

    lower_incl = row >= col
    belows, inverses, query_grams = [], [], []
    for j in range(half):
        k_scale, q_scale = scales[j]
        kj = k_rows[j]
        gap = jnp.where(lower_incl, column(0, j) - running[j : j + 1], 0.0)
        ratio = jnp.where(lower_incl, jnp.exp(gap), 0.0) * k_norm_rows[j : j + 1]
        grams = mm(jnp.concatenate([kj, q_rows[j]], axis=0), kj, ((1,), (1,)))
        below = grams[:count] * ratio * (column(1, j) * k_scale)
        query_grams.append(grams[count:] * ratio * q_scale)
        belows.append(below)
        first = jnp.where((row ^ col) == 1, below, 0.0)
        inverses.append(jnp.where(row == col, 1.0, jnp.where(row > col, -first, 0.0)))
    level = 1
    while (1 << level) < count:
        pair = ((row >> level) ^ (col >> level)) == 1
        pair = pair & (row > col)
        for j in range(half):
            link = jnp.where(pair, belows[j], 0.0)
            inverse = inverses[j]
            inverses[j] = inverse - dot_ff(inverse, dot_ff(link, inverse))
        level += 1
    for j in range(half):
        lanes = slice(j * width, (j + 1) * width)
        k_scale, q_scale = scales[j]
        kj = k_rows[j]
        inverse = inverses[j]
        from_query = dot_ff(query_grams[j], inverse)
        from_key = dot_bf_t(kj, inverse * (column(3, j) * k_scale))
        both = jnp.concatenate([from_query, from_key], axis=0)
        beta_row = beta[j : j + 1]
        written = dot_fb(both * beta_row, v_ref[:, lanes])
        erased = dot_fb(both * (beta_row * growth[j : j + 1] * k_norm_rows[j : j + 1]), kj)
        local_ref[:, lanes] = column(4, j) * written[:count]
        last = growth[j : j + 1, count - 1 :]
        planes_ref[3 * j] = jnp.where(row == col, last, 0.0) - erased[count:]
        planes_ref[3 * j + 1] = written[count:]
        planes_ref[3 * j + 2] = (column(2, j) * q_scale) * q_rows[j].astype(f32) - erased[:count]


def composed(later_trans, later_state, earlier):
    width = later_state.shape[1]
    both = dot_ff(later_trans, earlier)
    return jnp.concatenate([both[:, :width], both[:, width:] + later_state], axis=1)


def group_step(upper, own, other):
    width = own.shape[0]
    later = jnp.where(upper, own, other)
    return composed(later[:, :width], later[:, width:], jnp.where(upper, other, own))


def block_total(planes_ref, head):
    return jnp.concatenate([planes_ref[3 * head], planes_ref[3 * head + 1]], axis=1)


def pair_kernel(pos_ref, own_ref, other_ref, send_ref, keep_ref):
    share = send_ref.shape[0]
    odd = bit_of(pos_ref, 0)
    x = (pos_ref[0] >> 1) & 1
    for target, base in ((send_ref, (1 - x) * share), (keep_ref, x * share)):
        for j in range(share):
            own = block_total(own_ref, base + j)
            other = block_total(other_ref, base + j)
            target[j] = group_step(odd, own, other)


def gate_column(pos_ref, own_ref, other_ref, kind):
    at = own_ref.shape[0] - 1
    odd = bit_of(pos_ref, 0)
    own = own_ref[at, :, kind : kind + 1]
    other = other_ref[at, :, kind : kind + 1]
    return jnp.where(odd, other, own), jnp.where(odd, own, other)


def first_read_kernel(heads, pos_ref, own_ref, other_ref, eff_ref, read_ref):
    half = heads // 2
    count, width = own_ref.shape[1:]
    odd = bit_of(pos_ref, 0)
    for j in range(half):
        own_eff = own_ref[3 * j + 2]
        other_eff = other_ref[3 * j + 2]
        earlier = jnp.where(odd, block_total(other_ref, j), block_total(own_ref, j))
        both = dot_ff(jnp.where(odd, own_eff, other_eff), earlier)
        gain = gate_column(pos_ref, own_ref, other_ref, 5 * heads + j)[1]
        eff_ref[j, :count] = jnp.where(odd, other_eff, own_eff)
        eff_ref[j, count:] = both[:, :width]
        read_ref[j, :count] = jnp.zeros((count, width), f32)
        read_ref[j, count:] = gain * both[:, width:]


def quad_kernel(pos_ref, own_ref, other_ref, out_ref):
    upper = bit_of(pos_ref, 1)
    for j in range(own_ref.shape[0]):
        out_ref[j] = group_step(upper, own_ref[j], other_ref[j])


def second_read_kernel(heads, pos_ref, eff_ref, read_ref, low_ref, high_ref, own_ref, other_ref, eff_out, read_out):
    half = heads // 2
    width = eff_ref.shape[2]
    share = low_ref.shape[0]
    upper = bit_of(pos_ref, 1)
    for j in range(half):
        total = low_ref[j] if j < share else high_ref[j - share]
        eff = eff_ref[j]
        both = dot_ff(eff, total)
        eff_out[j] = jnp.where(upper, both[:, :width], eff)
        gain = jnp.concatenate(gate_column(pos_ref, own_ref, other_ref, 6 * heads + j), axis=0)
        read_out[j] = read_ref[j] + jnp.where(upper, gain * both[:, width:], 0.0)


def climb_kernel(level, first, top_next, pos_ref, total_ref, other_ref, *refs):
    prefix_ref = None if first else refs[0]
    memory_ref, prefix_out, total_out = refs[-3:]
    width = total_ref.shape[1]
    upper = bit_of(pos_ref, level)
    row = lax.broadcasted_iota(jnp.int32, (width, width), 0)
    col = lax.broadcasted_iota(jnp.int32, (width, width), 1)
    for j in range(total_ref.shape[0]):
        own = total_ref[j]
        other = other_ref[j]
        if first:
            prefix = jnp.where(row == col, 1.0, 0.0)
            reached = other
        else:
            prefix = prefix_ref[j]
            reached = dot_ff(prefix, other)
        memory_ref[j] = jnp.where(upper, reached[:, width:], 0.0)
        prefix_out[j] = jnp.where(upper, reached[:, :width], prefix)
        if top_next:
            later = jnp.where(upper, own, other)
            earlier = jnp.where(upper, other[:, width:], own[:, width:])
            total_out[j] = dot_ff(later[:, :width], earlier) + later[:, width:]
        else:
            total_out[j] = group_step(upper, own, other)


def top_kernel(level, pos_ref, prefix_ref, other_ref, memory_ref):
    upper = bit_of(pos_ref, level)
    for j in range(prefix_ref.shape[0]):
        memory_ref[j] = jnp.where(upper, dot_ff(prefix_ref[j], other_ref[j]), 0.0)


def level_memory(pos_ref, mine_ref, others_ref, head):
    share = mine_ref.shape[0]
    upper = bit_of(pos_ref, 1)
    mine = mine_ref[head % share]
    others = others_ref[head % share]
    return jnp.where(upper, others, mine) if head < share else jnp.where(upper, mine, others)


def read_kernel(heads, level, pos_ref, eff_ref, read_ref, mine_ref, others_ref, own_ref, other_ref, read_out):
    for j in range(heads // 2):
        gain = jnp.concatenate(
            gate_column(pos_ref, own_ref, other_ref, (5 + level) * heads + j), axis=0
        )
        memory = level_memory(pos_ref, mine_ref, others_ref, j)
        read_out[j] = read_ref[j] + gain * dot_ff(eff_ref[j], memory)


def last_read_kernel(heads, level, pos_ref, eff_ref, read_ref, mine_ref, others_ref, own_ref, other_ref, keep_ref, send_ref):
    count = own_ref.shape[1]
    width = eff_ref.shape[2]
    odd = bit_of(pos_ref, 0)
    for j in range(heads // 2):
        gain = jnp.concatenate(
            gate_column(pos_ref, own_ref, other_ref, (5 + level) * heads + j), axis=0
        )
        memory = level_memory(pos_ref, mine_ref, others_ref, j)
        total = read_ref[j] + gain * dot_ff(eff_ref[j], memory)
        lanes = slice(j * width, (j + 1) * width)
        keep_ref[:, lanes] = jnp.where(odd, total[count:], total[:count])
        send_ref[:, lanes] = jnp.where(odd, total[:count], total[count:])


def join_kernel(pos_ref, keep_ref, got_ref, local_own_ref, local_other_ref, out_ref):
    span = keep_ref.shape[1]
    odd = bit_of(pos_ref, 0)
    own = keep_ref[...] + local_own_ref[...]
    other = got_ref[...] + local_other_ref[...]
    out_ref[:, :span] = jnp.where(odd, other, own)
    out_ref[:, span:] = jnp.where(odd, own, other)


def near(*shape):
    return pltpu.VMEM(shape, f32)


def far(*shape):
    return jax.ShapeDtypeStruct(shape, f32)


def params():
    return pltpu.CompilerParams(vmem_limit_bytes=16 << 20)


def run(kernel, out_shapes, position, *arrays, name):
    held = [pltpu.with_memory_space_constraint(value, pltpu.VMEM) for value in arrays]
    return pl.pallas_call(
        kernel,
        out_shape=out_shapes,
        in_specs=[pl.BlockSpec(memory_space=pltpu.SMEM)]
        + [pl.BlockSpec(memory_space=pltpu.VMEM)] * len(arrays),
        compiler_params=params(),
        name=name,
    )(position, *held)


def block_half(mine, position, queries, key_rows, value_rows, write_strength, log_decay, level_gates):
    count = queries.shape[0]
    half = write_strength.shape[0] // 2
    span = value_rows.shape[1] // 2

    def side(i, pos_ref):
        core = pos_ref[0] & 1
        return (0, core if mine else 1 - core)

    wide = pl.BlockSpec((count, span), side)
    whole = lambda value: pl.BlockSpec(value.shape, lambda i, pos_ref: (0,) * value.ndim)
    return pl.pallas_call(
        lambda *refs: block_kernel(mine, *refs),
        grid_spec=pltpu.PrefetchScalarGridSpec(
            num_scalar_prefetch=1,
            grid=(1,),
            in_specs=[wide, wide, wide, whole(write_strength), whole(log_decay), whole(level_gates)],
            out_specs=[pl.BlockSpec(memory_space=pltpu.VMEM)] * 2,
        ),
        out_shape=[near(3 * half + 1, count, count), near(count, span)],
        compiler_params=params(),
        name="block_own" if mine else "block_sent",
    )(position, queries, key_rows, value_rows, write_strength, log_decay, level_gates)


def shards(queries, key_rows, value_rows, write_strength, log_decay, level_gates):
    size = lax.axis_size("ctx")
    levels = size.bit_length() - 1
    position = lax.axis_index("ctx").astype(jnp.int32).reshape(1)
    heads = write_strength.shape[0]
    half, share = heads // 2, heads // 4
    count = queries.shape[0]
    width = queries.shape[1] // heads
    inputs = (queries, key_rows, value_rows, write_strength, log_decay, level_gates)

    def swapped(value, bit):
        return lax.ppermute(value, "ctx", [(i, i ^ (1 << bit)) for i in range(size)])

    sent, local_other = block_half(False, position, *inputs)
    got = swapped(sent, 0)
    own, local_own = block_half(True, position, *inputs)
    pair_send, pair_keep = run(
        pair_kernel, [near(share, width, 2 * width)] * 2, position, own, got, name="pair"
    )
    pair_got = swapped(pair_send, 1)
    eff, read = run(
        lambda *refs: first_read_kernel(heads, *refs),
        [near(half, 2 * count, width)] * 2,
        position, own, got, name="read_first",
    )
    pair_got, eff, read = lax.optimization_barrier((pair_got, eff, read))
    total = run(quad_kernel, near(share, width, 2 * width), position, pair_keep, pair_got, name="quad")
    low = lax.ppermute(
        pair_keep, "ctx", [(i, i + 2) for i in range(size) if (i >> 1) & 1 == 0]
    )
    prefix, pending = (), []
    for level in range(2, levels - 1):
        other = swapped(total, level)
        memory, prefix, total = run(
            lambda *refs, level=level, first=not prefix: climb_kernel(
                level, first, level == levels - 2, *refs
            ),
            [near(share, width, width)] * 2
            + [near(share, width, width if level == levels - 2 else 2 * width)],
            position, total, other, *prefix, name="climb",
        )
        prefix = (prefix,)
        pending.append((level, memory, swapped(memory, 1)))
    top = levels - 1
    other = lax.ppermute(total, "ctx", [(i, i + (1 << top)) for i in range(size - (1 << top))])
    eff, read = run(
        lambda *refs: second_read_kernel(heads, *refs),
        [near(half, 2 * count, width)] * 2,
        position, eff, read, low, pair_got, own, got, name="read_second",
    )
    for level, memory, memory_other in pending:
        read = run(
            lambda *refs, level=level: read_kernel(heads, level, *refs),
            near(half, 2 * count, width),
            position, eff, read, memory, memory_other, own, got, name="read_level",
        )
    other, eff, read = lax.optimization_barrier((other, eff, read))
    memory = run(
        lambda *refs: top_kernel(top, *refs), near(share, width, width), position, *prefix, other, name="top"
    )
    memory_other = swapped(memory, 1)
    keep, away = run(
        lambda *refs: last_read_kernel(heads, top, *refs),
        [near(count, half * width)] * 2,
        position, eff, read, memory, memory_other, own, got, name="read_last",
    )
    back = swapped(away, 0)
    return run(
        join_kernel, far(count, heads * width), position, keep, back, local_own, local_other, name="join"
    )


def solution(mesh):
    placed = (
        P(("groups", "ctx"), None),
        P(("groups", "ctx"), None),
        P(("groups", "ctx"), None),
        P(None, ("groups", "ctx")),
        P(None, ("groups", "ctx")),
        P(None, None, ("groups", "ctx")),
    )
    return jax.shard_map(
        shards, mesh=mesh, in_specs=placed, out_specs=P(("groups", "ctx"), None), check_vma=False
    )
```

time: 72.2 us -> 49.7 us (0.69)
  Pallas kernels: 32.4 us -> 10.8 us
  waiting for transfers between devices: 20 us -> 22.4 us
  local copies, waits for them, and re-layouts: 7.31 us -> 4.95 us
  other arithmetic: 1.2 us -> 0 us
    pallas_call x9, Pallas kernels: 20.9 us -> 3.31 us  [run(): pl.pallas_call(kernel, out_shape=out_shapes, in_specs=[pl.BlockSpec(memor...]
    pallas_call x2, Pallas kernels: 11.5 us -> 7.54 us  [block_half(): pl.pallas_call(lambda *refs: block_kernel(mine, *refs), grid_spec=pltpu.P...]
    ppermute x7 -> x6, waiting for transfers between devices: 13 us -> 15.5 us  [swapped(): return lax.ppermute(value, 'ctx', [(i, i ^ 1 << bit) for i in range(size)])]
    another operation x2 -> x0, other arithmetic: 1.2 us -> none  [choice(): return jnp.stack([core, row, position >> bit & 1]).astype(jnp.int32)]
    slice x1 -> x0, local copies, waits for them, and re-layouts: 0.95 us -> none  [shards(): total[:, :, width:]]
    unnamed x24 -> x12, local copies, waits for them, and re-layouts: 5.65 us -> 4.95 us
    ppermute x7 -> x6, starting transfers between devices: 6.4 us -> 6.62 us  [swapped(): return lax.ppermute(value, 'ctx', [(i, i ^ 1 << bit) for i in range(size)])]
  transfers between devices with their start and end apart: 9 -> 8, of which waited for: 5 -> 6; matrix products, arithmetic and copies ran while one was open for 4% -> 0% of each run, Pallas kernels for 25% -> 10%
where the time goes in v2:
time: 49.7 us; the launch traced here: 49.4 us
  waiting for transfers between devices  22.4 us (45%)
  starting transfers between devices  11 us (22%)
  Pallas kernels  10.8 us (22%)
  local copies, waits for them, and re-layouts  4.95 us (10%)
    ppermute x6, waiting for transfers between devices, swapped(): return lax.ppermute(value, 'ctx', [(i, i ^ 1 << bit) for i in range(size)])  15.5 us
    pallas_call x2, Pallas kernels, block_half(): pl.pallas_call(lambda *refs: block_kernel(mine, *refs), grid_spec=pltpu.P...  7.54 us
    ppermute x1, waiting for transfers between devices, shards(): lax.ppermute(total, 'ctx', [(i, i + (1 << top)) for i in range(size - (1...  6.89 us
    ppermute x6, starting transfers between devices, swapped(): return lax.ppermute(value, 'ctx', [(i, i ^ 1 << bit) for i in range(size)])  6.62 us
    unnamed x12, local copies, waits for them, and re-layouts  4.95 us
    pallas_call x9, Pallas kernels, run(): pl.pallas_call(kernel, out_shape=out_shapes, in_specs=[pl.BlockSpec(memor...  3.31 us
    ppermute x1, starting transfers between devices, shards(): lax.ppermute(pair_keep, 'ctx', [(i, i + 2) for i in range(size) if i >> 1...  3.12 us
    ppermute x1, starting transfers between devices, shards(): lax.ppermute(total, 'ctx', [(i, i + (1 << top)) for i in range(size - (1...  1.28 us
  transfers between devices with their start and end apart: 8, of which 6 were waited for; matrix products, arithmetic and copies ran while one was open for 0% of the time, Pallas kernels for 10%

profile of v2, /device:TPU:25, one launch (start us, length us, event | category | flops | bytes accessed | tf_op | source)
XLA Modules:
  0.0 49.4 jit_solution(126236617490382228)
XLA Ops:
  0.0 0.7 %copy-done.4 = f32[8,128]{1,0:T(8,128)S(1)} copy-done((f32[8,128]{1,0:T(8,128)S(1)}, f32[8,128]{1,0:T(8,128)}, u32[]{:S(2)}) %copy-start.4) | copy-done | bytes 4120
  0.7 0.9 %copy-done = bf16[128,1024]{1,0:T(8,128)(2,1)S(1)} copy-done((bf16[128,1024]{1,0:T(8,128)(2,1)S(1)}, bf16[128,1024]{1,0:T(8,128)(2,1)}, u32[]{:S(2)}) %copy-start) | copy-done | bytes 262168
  1.6 0.9 %copy-done.1 = bf16[128,1024]{1,0:T(8,128)(2,1)S(1)} copy-done((bf16[128,1024]{1,0:T(8,128)(2,1)S(1)}, bf16[128,1024]{1,0:T(8,128)(2,1)}, u32[]{:S(2)}) %copy-start.1) | copy-done | bytes 262168
  2.6 0.9 %copy-done.2 = bf16[128,1024]{1,0:T(8,128)(2,1)S(1)} copy-done((bf16[128,1024]{1,0:T(8,128)(2,1)S(1)}, bf16[128,1024]{1,0:T(8,128)(2,1)}, u32[]{:S(2)}) %copy-start.2) | copy-done | bytes 262168
  3.5 0.7 %copy-done.3 = f32[5,8,128]{2,1,0:T(8,128)S(1)} copy-done((f32[5,8,128]{2,1,0:T(8,128)S(1)}, f32[5,8,128]{2,1,0:T(8,128)}, u32[]{:S(2)}) %copy-start.3) | copy-done | bytes 20504
  4.3 0.7 %copy-done.5 = f32[8,128]{1,0:T(8,128)S(1)} copy-done((f32[8,128]{1,0:T(8,128)S(1)}, f32[8,128]{1,0:T(8,128)}, u32[]{:S(2)}) %copy-start.5) | copy-done | bytes 4120
  5.0 3.8 %block_sent.1 = (f32[13,128,128]{2,1,0:T(8,128)S(1)}, f32[128,512]{1,0:T(8,128)S(1)}) custom-call(s32[1]{0:T(128)} %bitcast.refs_0_.pos_ref, bf16[128,1024]{1,0:T(8,128)(2,1)S(1)} %copy-done, bf16[128,1024]{1,0:T(8,128)(2,1)S(1)} %copy-done.1, bf16[128,1024]{1,0:T(8,128)(2,1)S(1)} %copy-done.2, f32[8,128]{1,0:T(8,128)S(1)} %copy-done.4, ...), custom_call_target="tpu_custom_call" | custom-call | tf_op jit(solution)/shard_map/block_sent/pallas_call | solution.py:310
  8.7 0.7 %collective-permute-start = (f32[13,128,128]{2,1,0:T(8,128)S(1)}, f32[13,128,128]{2,1,0:T(8,128)S(1)}, u32[]{:S(2)}, u32[]{:S(2)}) collective-permute-start(f32[13,128,128]{2,1,0:T(8,128)S(1)} %get-tuple-element.27), channel_id=1, source_target_pairs={{0,1},{1,0},{2,3},{3,2},{4,5},{5,4},{6,7},{7,6},{8,9},{9,8},{10,11... | collective-permute-start | bytes 2555912 | tf_op jit(solution)/shard_map/ppermute | solution.py:335
  9.5 3.8 %block_own.1 = (f32[13,128,128]{2,1,0:T(8,128)S(1)}, f32[128,512]{1,0:T(8,128)S(1)}) custom-call(s32[1]{0:T(128)} %bitcast.refs_0_.pos_ref, bf16[128,1024]{1,0:T(8,128)(2,1)S(1)} %copy-done, bf16[128,1024]{1,0:T(8,128)(2,1)S(1)} %copy-done.1, bf16[128,1024]{1,0:T(8,128)(2,1)S(1)} %copy-done.2, f32[8,128]{1,0:T(8,128)S(1)} %copy-done.4, ...), custom_call_target="tpu_custom_call" | custom-call | tf_op jit(solution)/shard_map/block_own/pallas_call | solution.py:310
  13.2 0.0 collective-permute-done.other_ref.refs_2_.refs_6_
  13.2 0.3 pair.1
  13.6 1.3 %collective-permute-start.1 = (f32[2,128,256]{2,1,0:T(8,128)S(1)}, f32[2,128,256]{2,1,0:T(8,128)S(1)}, u32[]{:S(2)}, u32[]{:S(2)}) collective-permute-start(f32[2,128,256]{2,1,0:T(8,128)S(1)} %get-tuple-element.29), channel_id=1, source_target_pairs={{0,2},{1,3},{2,0},{3,1},{4,6},{5,7},{6,4},{7,5},{8,10},{9,11},{10,... | collective-permute-start | bytes 786440 | tf_op jit(solution)/shard_map/ppermute | solution.py:335
  14.9 0.4 read_first.1
  15.2 6.3 %collective-permute-done.1.other_ref.refs_4_ = f32[2,128,256]{2,1,0:T(8,128)S(1)} collective-permute-done((f32[2,128,256]{2,1,0:T(8,128)S(1)}, f32[2,128,256]{2,1,0:T(8,128)S(1)}, u32[]{:S(2)}, u32[]{:S(2)}) %collective-permute-start.1) | collective-permute-done | bytes 262176 | tf_op jit(solution)/shard_map/ppermute | solution.py:335
  21.5 0.2 quad.1.refs_1_
  21.8 0.2 collective-permute-start.2
  22.0 3.1 %collective-permute-start.4 = (f32[2,128,256]{2,1,0:T(8,128)S(1)}, f32[2,128,256]{2,1,0:T(8,128)S(1)}, u32[]{:S(2)}, u32[]{:S(2)}) collective-permute-start(f32[2,128,256]{2,1,0:T(8,128)S(1)} %get-tuple-element.28.own_ref), channel_id=1, source_target_pairs={{0,2},{1,3},{4,6},{5,7},{8,10},{9,11},{12,14},{13,15},{16,18},{17,... | collective-permute-start | bytes 786440 | tf_op jit(solution)/shard_map/ppermute | solution.py:351
  25.1 3.7 %collective-permute-done.2.refs_2_ = f32[2,128,256]{2,1,0:T(8,128)S(1)} collective-permute-done((f32[2,128,256]{2,1,0:T(8,128)S(1)}, f32[2,128,256]{2,1,0:T(8,128)S(1)}, u32[]{:S(2)}, u32[]{:S(2)}) %collective-permute-start.2) | collective-permute-done | bytes 262176 | tf_op jit(solution)/shard_map/ppermute | solution.py:335
  28.8 0.2 climb.1
  29.0 1.3 %collective-permute-start.5 = (f32[2,128,128]{2,1,0:T(8,128)S(1)}, f32[2,128,128]{2,1,0:T(8,128)S(1)}, u32[]{:S(2)}, u32[]{:S(2)}) collective-permute-start(f32[2,128,128]{2,1,0:T(8,128)S(1)} %get-tuple-element.38.refs_3_), channel_id=1, source_target_pairs={{0,2},{1,3},{2,0},{3,1},{4,6},{5,7},{6,4},{7,5},{8,10},{9,11},{10,... | collective-permute-start | bytes 393224 | tf_op jit(solution)/shard_map/ppermute | solution.py:335
  30.3 1.3 %collective-permute-start.3 = (f32[2,128,128]{2,1,0:T(8,128)S(1)}, f32[2,128,128]{2,1,0:T(8,128)S(1)}, u32[]{:S(2)}, u32[]{:S(2)}) collective-permute-start(f32[2,128,128]{2,1,0:T(8,128)S(1)} %get-tuple-element.33), channel_id=1, source_target_pairs={{0,8},{1,9},{2,10},{3,11},{4,12},{5,13},{6,14},{7,15},{16,24},{17,... | collective-permute-start | bytes 393224 | tf_op jit(solution)/shard_map/ppermute | solution.py:368
  31.6 0.5 read_second.1
  32.1 0.8 %collective-permute-done.5.refs_4_ = f32[2,128,128]{2,1,0:T(8,128)S(1)} collective-permute-done((f32[2,128,128]{2,1,0:T(8,128)S(1)}, f32[2,128,128]{2,1,0:T(8,128)S(1)}, u32[]{:S(2)}, u32[]{:S(2)}) %collective-permute-start.5) | collective-permute-done | bytes 131104 | tf_op jit(solution)/shard_map/ppermute | solution.py:335
  32.9 0.3 read_level.1.refs_2_
  33.2 6.9 %collective-permute-done.3.refs_2_ = f32[2,128,128]{2,1,0:T(8,128)S(1)} collective-permute-done((f32[2,128,128]{2,1,0:T(8,128)S(1)}, f32[2,128,128]{2,1,0:T(8,128)S(1)}, u32[]{:S(2)}, u32[]{:S(2)}) %collective-permute-start.3) | collective-permute-done | bytes 131104 | tf_op jit(solution)/shard_map/ppermute | solution.py:368
  40.1 0.2 top.1.refs_3_
  40.3 0.3 collective-permute-start.6
  40.7 3.6 %collective-permute-done.6.refs_4_ = f32[2,128,128]{2,1,0:T(8,128)S(1)} collective-permute-done((f32[2,128,128]{2,1,0:T(8,128)S(1)}, f32[2,128,128]{2,1,0:T(8,128)S(1)}, u32[]{:S(2)}, u32[]{:S(2)}) %collective-permute-start.6) | collective-permute-done | bytes 131104 | tf_op jit(solution)/shard_map/ppermute | solution.py:335
  44.2 0.3 read_last.1
  44.6 2.8 %collective-permute-start.7 = (f32[128,512]{1,0:T(8,128)S(1)}, f32[128,512]{1,0:T(8,128)S(1)}, u32[]{:S(2)}, u32[]{:S(2)}) collective-permute-start(f32[128,512]{1,0:T(8,128)S(1)} %get-tuple-element.44), channel_id=1, source_target_pairs={{0,1},{1,0},{2,3},{3,2},{4,5},{5,4},{6,7},{7,6},{8,9},{9,8},{10,11... | collective-permute-start | bytes 786440 | tf_op jit(solution)/shard_map/ppermute | solution.py:335
  47.3 1.2 %collective-permute-done.7.got_ref = f32[128,512]{1,0:T(8,128)S(1)} collective-permute-done((f32[128,512]{1,0:T(8,128)S(1)}, f32[128,512]{1,0:T(8,128)S(1)}, u32[]{:S(2)}, u32[]{:S(2)}) %collective-permute-start.7) | collective-permute-done | bytes 262176 | tf_op jit(solution)/shard_map/ppermute | solution.py:335
  48.5 0.8 %join.1 = f32[128,1024]{1,0:T(8,128)} custom-call(s32[1]{0:T(128)} %bitcast.refs_0_.pos_ref, f32[128,512]{1,0:T(8,128)S(1)} %get-tuple-element.43.keep_ref, f32[128,512]{1,0:T(8,128)S(1)} %collective-permute-done.7.got_ref, f32[128,512]{1,0:T(8,128)S(1)} %get-tuple-element.45.local_own_ref, f32[128,512]{1,0:T(8,128)S(1)} %get-tuple-element.46.local_other_ref), custom_call_target="tpu_custom_call" | custom-call | tf_op jit(solution)/shard_map/join/pallas_call | solution.py:289
  (7 shorter events, 0.0 us)
Async XLA Ops:
  0.0 0.7 %copy-start.4 = (f32[8,128]{1,0:T(8,128)S(1)}, f32[8,128]{1,0:T(8,128)}, u32[]{:S(2)}) copy-start(f32[8,128]{1,0:T(8,128)} %refs_4_.3) | copy-start | bytes 12292
  0.7 0.9 %copy-start = (bf16[128,1024]{1,0:T(8,128)(2,1)S(1)}, bf16[128,1024]{1,0:T(8,128)(2,1)}, u32[]{:S(2)}) copy-start(bf16[128,1024]{1,0:T(8,128)(2,1)} %refs_1_.3) | copy-start | bytes 786436
  1.6 0.9 %copy-start.1 = (bf16[128,1024]{1,0:T(8,128)(2,1)S(1)}, bf16[128,1024]{1,0:T(8,128)(2,1)}, u32[]{:S(2)}) copy-start(bf16[128,1024]{1,0:T(8,128)(2,1)} %refs_2_.3) | copy-start | bytes 786436
  2.6 0.9 %copy-start.2 = (bf16[128,1024]{1,0:T(8,128)(2,1)S(1)}, bf16[128,1024]{1,0:T(8,128)(2,1)}, u32[]{:S(2)}) copy-start(bf16[128,1024]{1,0:T(8,128)(2,1)} %refs_3_.3) | copy-start | bytes 786436
  3.5 0.7 %copy-start.3 = (f32[5,8,128]{2,1,0:T(8,128)S(1)}, f32[5,8,128]{2,1,0:T(8,128)}, u32[]{:S(2)}) copy-start(f32[5,8,128]{2,1,0:T(8,128)} %refs_6_.3) | copy-start | bytes 61444
  4.3 0.7 %copy-start.5 = (f32[8,128]{1,0:T(8,128)S(1)}, f32[8,128]{1,0:T(8,128)}, u32[]{:S(2)}) copy-start(f32[8,128]{1,0:T(8,128)} %refs_5_.3) | copy-start | bytes 12292
  8.7 4.5 %collective-permute-start = (f32[13,128,128]{2,1,0:T(8,128)S(1)}, f32[13,128,128]{2,1,0:T(8,128)S(1)}, u32[]{:S(2)}, u32[]{:S(2)}) collective-permute-start(f32[13,128,128]{2,1,0:T(8,128)S(1)} %get-tuple-element.27), channel_id=1, source_target_pairs={{0,1},{1,0},{2,3},{3,2},{4,5},{5,4},{6,7},{7,6},{8,9},{9,8},{10,11... | collective-permute-start | bytes 2555912 | tf_op jit(solution)/shard_map/ppermute | solution.py:335
  13.6 7.9 %collective-permute-start.1 = (f32[2,128,256]{2,1,0:T(8,128)S(1)}, f32[2,128,256]{2,1,0:T(8,128)S(1)}, u32[]{:S(2)}, u32[]{:S(2)}) collective-permute-start(f32[2,128,256]{2,1,0:T(8,128)S(1)} %get-tuple-element.29), channel_id=1, source_target_pairs={{0,2},{1,3},{2,0},{3,1},{4,6},{5,7},{6,4},{7,5},{8,10},{9,11},{10,... | collective-permute-start | bytes 786440 | tf_op jit(solution)/shard_map/ppermute | solution.py:335
  21.8 7.1 %collective-permute-start.2 = (f32[2,128,256]{2,1,0:T(8,128)S(1)}, f32[2,128,256]{2,1,0:T(8,128)S(1)}, u32[]{:S(2)}, u32[]{:S(2)}) collective-permute-start(f32[2,128,256]{2,1,0:T(8,128)S(1)} %quad.1.refs_1_), channel_id=1, source_target_pairs={{0,4},{1,5},{2,6},{3,7},{4,0},{5,1},{6,2},{7,3},{8,12},{9,13},{10,... | collective-permute-start | bytes 786440 | tf_op jit(solution)/shard_map/ppermute | solution.py:335
  22.0 9.6 %collective-permute-start.4 = (f32[2,128,256]{2,1,0:T(8,128)S(1)}, f32[2,128,256]{2,1,0:T(8,128)S(1)}, u32[]{:S(2)}, u32[]{:S(2)}) collective-permute-start(f32[2,128,256]{2,1,0:T(8,128)S(1)} %get-tuple-element.28.own_ref), channel_id=1, source_target_pairs={{0,2},{1,3},{4,6},{5,7},{8,10},{9,11},{12,14},{13,15},{16,18},{17,... | collective-permute-start | bytes 786440 | tf_op jit(solution)/shard_map/ppermute | solution.py:351
  29.0 3.9 %collective-permute-start.5 = (f32[2,128,128]{2,1,0:T(8,128)S(1)}, f32[2,128,128]{2,1,0:T(8,128)S(1)}, u32[]{:S(2)}, u32[]{:S(2)}) collective-permute-start(f32[2,128,128]{2,1,0:T(8,128)S(1)} %get-tuple-element.38.refs_3_), channel_id=1, source_target_pairs={{0,2},{1,3},{2,0},{3,1},{4,6},{5,7},{6,4},{7,5},{8,10},{9,11},{10,... | collective-permute-start | bytes 393224 | tf_op jit(solution)/shard_map/ppermute | solution.py:335
  30.3 9.8 %collective-permute-start.3 = (f32[2,128,128]{2,1,0:T(8,128)S(1)}, f32[2,128,128]{2,1,0:T(8,128)S(1)}, u32[]{:S(2)}, u32[]{:S(2)}) collective-permute-start(f32[2,128,128]{2,1,0:T(8,128)S(1)} %get-tuple-element.33), channel_id=1, source_target_pairs={{0,8},{1,9},{2,10},{3,11},{4,12},{5,13},{6,14},{7,15},{16,24},{17,... | collective-permute-start | bytes 393224 | tf_op jit(solution)/shard_map/ppermute | solution.py:368
  40.3 3.9 %collective-permute-start.6 = (f32[2,128,128]{2,1,0:T(8,128)S(1)}, f32[2,128,128]{2,1,0:T(8,128)S(1)}, u32[]{:S(2)}, u32[]{:S(2)}) collective-permute-start(f32[2,128,128]{2,1,0:T(8,128)S(1)} %top.1.refs_3_), channel_id=1, source_target_pairs={{0,2},{1,3},{2,0},{3,1},{4,6},{5,7},{6,4},{7,5},{8,10},{9,11},{10,... | collective-permute-start | bytes 393224 | tf_op jit(solution)/shard_map/ppermute | solution.py:335
  44.6 3.9 %collective-permute-start.7 = (f32[128,512]{1,0:T(8,128)S(1)}, f32[128,512]{1,0:T(8,128)S(1)}, u32[]{:S(2)}, u32[]{:S(2)}) collective-permute-start(f32[128,512]{1,0:T(8,128)S(1)} %get-tuple-element.44), channel_id=1, source_target_pairs={{0,1},{1,0},{2,3},{3,2},{4,5},{5,4},{6,7},{7,6},{8,9},{9,8},{10,11... | collective-permute-start | bytes 786440 | tf_op jit(solution)/shard_map/ppermute | solution.py:335

commit v3 on v2

v3 whole, which is shorter than its diff:
```python
import functools

import jax
import jax.numpy as jnp
from jax import lax
from jax.experimental import pallas as pl
from jax.experimental.pallas import tpu as pltpu
from jax.sharding import PartitionSpec as P

norm_eps = 1e-06
f32 = jnp.float32
bf16 = jnp.bfloat16


def parts(value):
    high = value.astype(bf16)
    return high, (value - high.astype(f32)).astype(bf16)


def mm(left, right, dims=((1,), (0,))):
    return lax.dot_general(left, right, (dims, ((), ())), preferred_element_type=f32)


def dot_ff(left, right):
    width = right.shape[1]
    left_parts = jnp.concatenate(parts(left), axis=1)
    right_row = jnp.concatenate(parts(right), axis=1)
    both = mm(left_parts, jnp.concatenate([right_row, right_row], axis=0))
    return both[:, :width] + both[:, width:]


def dot_fb(left, right):
    left_parts = jnp.concatenate(parts(left), axis=1)
    return mm(left_parts, jnp.concatenate([right, right], axis=0))


def dot_bf_t(left, right):
    width = right.shape[1]
    both = mm(left, jnp.concatenate(parts(right), axis=1), ((0,), (0,)))
    return both[:, :width] + both[:, width:]


chunks = 2


def bit_of(pos_ref, bit):
    return ((pos_ref[0] >> bit) & 1) == 1


def prepare_kernel(pos_ref, *refs):
    arrays = refs[:6]
    q_ref, k_ref, v_ref, rows_ref, columns_ref, beta_ref, decay_ref, gates_ref, sems = refs[6:]
    targets = (q_ref, k_ref, v_ref, beta_ref, decay_ref, gates_ref)
    copies = [pltpu.make_async_copy(a, t, sems.at[i]) for i, (a, t) in enumerate(zip(arrays, targets))]
    for i in (4, 3, 5, 1, 0, 2):
        copies[i].start()
    heads, count = beta_ref.shape
    half = heads // 2
    odd = bit_of(pos_ref, 0)

    def chosen_first(rows):
        return jnp.where(odd, pltpu.roll(rows, half, 0), rows)

    row = lax.broadcasted_iota(jnp.int32, (count, count), 0)
    col = lax.broadcasted_iota(jnp.int32, (count, count), 1)
    summing = jnp.where(row <= col, 1.0, 0.0).astype(bf16)
    for i in (4, 3, 5):
        copies[i].wait()
    decay = decay_ref[...]
    d1 = decay.astype(bf16)
    rest = decay - d1.astype(f32)
    d2 = rest.astype(bf16)
    d3 = (rest - d2.astype(f32)).astype(bf16)
    running = chosen_first(mm(d1, summing) + (mm(d2, summing) + mm(d3, summing)))
    beta = chosen_first(beta_ref[...])
    growth = jnp.exp(running)
    to_end = jnp.exp(running[:, count - 1 :] - running)
    kinds = [running, beta, growth, to_end] + [chosen_first(gates_ref[b]) for b in range(gates_ref.shape[0])]
    filler = jnp.zeros((count - len(kinds) * heads, count), f32)
    columns_ref[...] = jnp.concatenate(kinds + [filler], axis=0).T
    rows_ref[...] = jnp.concatenate(kinds[:3], axis=0)
    for i in (1, 0, 2):
        copies[i].wait()


def block_kernel(heads, mine, pos_ref, q_ref, k_ref, v_ref, rows_ref, columns_ref, planes_ref, local_ref):
    half = heads // 2
    n = half
    count = q_ref.shape[0]
    width = q_ref.shape[1] // heads
    core = pos_ref[0] & 1
    side = core if mine else 1 - core
    row = lax.broadcasted_iota(jnp.int32, (count, count), 0)
    col = lax.broadcasted_iota(jnp.int32, (count, count), 1)
    base = 0 if mine else half
    columns = columns_ref[...]
    if planes_ref.shape[0] > 3 * n:
        planes_ref[3 * n] = columns

    def column(kind, j):
        at = kind * heads + base + j
        return columns[:, at : at + 1]

    def line(kind, j):
        at = kind * heads + base + j
        return rows_ref[at : at + 1]

    def lanes(ref, j):
        at = pl.multiple_of(side * (half * width) + j * width, 128)
        return ref[:, pl.ds(at, width)]

    k_rows, q_rows, k_norm = [], [], jnp.zeros((count, count), f32)
    scales = []
    for j in range(n):
        kj = lanes(k_ref, j)
        qj = lanes(q_ref, j)
        kf = kj.astype(f32)
        qf = qj.astype(f32)
        k_scale = lax.rsqrt(jnp.sum(kf * kf, axis=1, keepdims=True) + norm_eps)
        q_scale = lax.rsqrt(jnp.sum(qf * qf, axis=1, keepdims=True) + norm_eps)
        k_norm = jnp.where(col == j, k_scale, k_norm)
        k_rows.append(kj)
        q_rows.append(qj)
        scales.append((k_scale, q_scale))
    k_norm_rows = k_norm.T

    lower_incl = row >= col
    belows, query_grams, runs = [], [], []
    for j in range(n):
        k_scale, q_scale = scales[j]
        kj = k_rows[j]
        run_row = line(0, j)
        run_all = jnp.broadcast_to(column(0, j), (count, count))
        runs.append(run_all)
        gap = jnp.where(lower_incl, run_all - run_row, 0.0)
        ratio = jnp.where(lower_incl, jnp.exp(gap), 0.0) * k_norm_rows[j : j + 1]
        grams = mm(jnp.concatenate([kj, q_rows[j]], axis=0), kj, ((1,), (1,)))
        below = jnp.where(row > col, grams[:count] * ratio * (column(1, j) * k_scale), 0.0)
        query_grams.append(grams[count:] * ratio * q_scale)
        belows.append(below)
    step = 16
    folded = jnp.concatenate([folded_blocks(belows[j], step, row, col) for j in range(n)], axis=0)
    own_col = lax.broadcasted_iota(jnp.int32, (step, count), 1) % step
    own_row = lax.broadcasted_iota(jnp.int32, (step, count), 0)
    group = lax.broadcasted_iota(jnp.int32, folded.shape, 1) // step * step
    solved = [jnp.where(own_col == own_row, 1.0, 0.0)] * n
    for s in range(step - 1):
        factors = jnp.take_along_axis(folded, group + s, axis=1)
        for j in range(n):
            solved[j] = solved[j] - factors[j * step : (j + 1) * step] * solved[j][s : s + 1]
    inverses = []
    for j in range(n):
        spread = jnp.concatenate([solved[j]] * (count // step), axis=0)
        inverses.append(jnp.where(row // step == col // step, spread, 0.0))
    while step < count:
        pair = ((row // step) % 2 == 1) & (row // (2 * step) == col // (2 * step)) & ((col // step) % 2 == 0)
        starts = range(0, count, 2 * step)
        for j in range(n):
            inverse = inverses[j]
            odd_rows = jnp.concatenate([inverse[i + step : i + 2 * step] for i in starts], axis=0)
            link = jnp.where(pair, belows[j], 0.0)
            odd_rows = odd_rows - dot_ff(dot_ff(odd_rows, link), inverse)
            both = []
            for at, i in enumerate(starts):
                both += [inverse[i : i + step], odd_rows[at * step : (at + 1) * step]]
            inverses[j] = jnp.concatenate(both, axis=0)
        step *= 2
    for j in range(n):
        k_scale, q_scale = scales[j]
        kj = k_rows[j]
        inverse = inverses[j]
        run_end = line(0, j)[:, count - 1 :]
        from_query = dot_ff(query_grams[j], inverse)
        from_key = dot_bf_t(kj, inverse * (jnp.exp(run_end - runs[j]) * k_scale))
        both = jnp.concatenate([from_query, from_key], axis=0)
        beta_row = line(1, j)
        growth = line(2, j)
        written = dot_fb(both * beta_row, lanes(v_ref, j))
        erased = dot_fb(both * (beta_row * growth * k_norm_rows[j : j + 1]), kj)
        local_ref[:, j * width : (j + 1) * width] = written[:count]
        planes_ref[3 * j] = jnp.where(row == col, growth[:, count - 1 :], 0.0) - erased[count:]
        planes_ref[3 * j + 1] = written[count:]
        planes_ref[3 * j + 2] = (jnp.exp(runs[j]) * q_scale) * q_rows[j].astype(f32) - erased[:count]


def folded_blocks(matrix, step, row, col):
    count = matrix.shape[0]
    kept = jnp.where(row // step == col // step, matrix, 0.0)
    total = kept[:step]
    for i in range(step, count, step):
        total = total + kept[i : i + step]
    return total


def group_step(upper, own, other):
    width = own.shape[0]
    later = jnp.where(upper, own, other)
    both = dot_ff(later[:, :width], jnp.where(upper, other, own))
    return jnp.concatenate([both[:, :width], both[:, width:] + later[:, width:]], axis=1)


def block_total(planes_ref, head):
    return jnp.concatenate([planes_ref[3 * head], planes_ref[3 * head + 1]], axis=1)


def pair_kernel(pos_ref, own_ref, other_ref, *refs):
    share = refs[0].shape[0]
    width = own_ref.shape[1]
    odd = bit_of(pos_ref, 0)
    x = (pos_ref[0] >> 1) & 1
    low_ref = refs[-1]
    for c in range(chunks):
        for target, base in ((refs[2 * c], (1 - x) * share), (refs[2 * c + 1], x * share)):
            for j in range(share):
                at = base + c * 2 * share + j
                total = group_step(odd, block_total(own_ref, at), block_total(other_ref, at))
                target[j] = total
                if target is refs[2 * c + 1]:
                    low_ref[c + j * chunks] = total[:, width:]


def gate_columns(heads, level, j, pos_ref, own_ref, other_ref):
    half = heads // 2
    odd = bit_of(pos_ref, 0)
    at = (4 + level) * heads + j
    own = own_ref[:, at : at + 1]
    other = other_ref[other_ref.shape[0] - 1, :, at + half : at + half + 1]
    return jnp.where(odd, other, own), jnp.where(odd, own, other)


def first_read_kernel(heads, pos_ref, own_ref, other_ref, cols_ref, local_ref, local_sent_ref, eff_ref, read_ref, out_ref, sent_out):
    count, width = own_ref.shape[1:]
    half = heads // 2
    odd = bit_of(pos_ref, 0)
    for j in range(half):
        own_eff = own_ref[3 * j + 2]
        other_eff = other_ref[3 * j + 2]
        earlier = jnp.where(odd, block_total(other_ref, j), block_total(own_ref, j))
        both = dot_ff(jnp.where(odd, own_eff, other_eff), earlier)
        gain = gate_columns(heads, 1, j, pos_ref, cols_ref, other_ref)[1]
        eff_ref[j, :count] = jnp.where(odd, other_eff, own_eff)
        eff_ref[j, count:] = both[:, :width]
        read_ref[j, :count] = jnp.zeros((count, width), f32)
        read_ref[j, count:] = gain * both[:, width:]
        lanes = slice(j * width, (j + 1) * width)
        at = 4 * heads + j
        out_ref[:, lanes] = cols_ref[:, at : at + 1] * local_ref[:, lanes]
        sent_out[:, lanes] = cols_ref[:, at + half : at + half + 1] * local_sent_ref[:, lanes]


def quad_kernel(pos_ref, own_ref, other_ref, out_ref):
    upper = bit_of(pos_ref, 1)
    for j in range(own_ref.shape[0]):
        out_ref[j] = group_step(upper, own_ref[j], other_ref[j])


def climb_kernel(level, top_next, pieces, pos_ref, *refs):
    first = level == 2
    use_ref, send_ref, prefix_out, total_out = refs[-4:]
    width = use_ref.shape[1]
    upper = bit_of(pos_ref, level)
    x = bit_of(pos_ref, 1)
    row = lax.broadcasted_iota(jnp.int32, (width, width), 0)
    col = lax.broadcasted_iota(jnp.int32, (width, width), 1)
    for at in range(use_ref.shape[0]):
        c, j = at % pieces, at // pieces
        total_ref, other_ref = refs[c], refs[pieces + c]
        own = total_ref[j]
        other = other_ref[j]
        later = jnp.where(upper, own, other)
        if top_next:
            earlier = jnp.where(upper, other[:, width:], own[:, width:])
            total_out[at] = dot_ff(later[:, :width], earlier) + later[:, width:]
        else:
            total_out[at] = group_step(upper, own, other)
        if first:
            keep_ref, got_ref = refs[2 * pieces + c], refs[3 * pieces + c]
            passed = jnp.where(x, got_ref[j, :, :width], keep_ref[j, :, :width])
            prefix = jnp.concatenate([jnp.where(row == col, 1.0, 0.0), passed], axis=0)
            reached = jnp.concatenate([other, dot_ff(passed, other)], axis=0)
        else:
            prefix = refs[2 * pieces][at]
            reached = dot_ff(prefix, other)
        prefix_out[at] = jnp.where(upper, reached[:, :width], prefix)
        memory = jnp.where(upper, reached[:, width:], 0.0)
        use_ref[at] = jnp.where(x, memory[width:], memory[:width])
        send_ref[at] = jnp.where(x, memory[:width], memory[width:])


def top_kernel(level, pos_ref, prefix_ref, other_ref, use_ref, send_ref):
    width = other_ref.shape[1]
    upper = bit_of(pos_ref, level)
    x = bit_of(pos_ref, 1)
    for j in range(prefix_ref.shape[0]):
        memory = jnp.where(upper, dot_ff(prefix_ref[j], other_ref[j]), 0.0)
        use_ref[j] = jnp.where(x, memory[width:], memory[:width])
        send_ref[j] = jnp.where(x, memory[:width], memory[width:])


def gain_of(heads, level, j, pos_ref, cols_ref, got_ref):
    return jnp.concatenate(gate_columns(heads, level + 1, j, pos_ref, cols_ref, got_ref), axis=0)


def owned(x, j, share, mine, others):
    return jnp.where(x, others, mine) if j < share else jnp.where(x, mine, others)


def read_kernel(heads, level, top, pos_ref, eff_ref, read_ref, cols_ref, planes_ref, use_ref, got_ref, *refs):
    share, width = use_ref.shape[:2]
    low_refs, outs = (refs[: chunks + 1], refs[chunks + 1 :]) if level == 2 else ((), refs)
    x = bit_of(pos_ref, 1)
    for head in range(heads // 2):
        c, j = divmod(head, 2 * share // chunks)
        at = c + j % (share // chunks) * chunks
        memory = owned(x, j, share // chunks, use_ref[at], got_ref[at])
        gain = gain_of(heads, level, head, pos_ref, cols_ref, planes_ref)
        eff = eff_ref[head]
        if level > 2:
            outs[0][head] = read_ref[head] + gain * dot_ff(eff, memory)
        else:
            low_ref, pair_ref = low_refs[0], low_refs[1 + c]
            below = low_ref[at] if j < share // chunks else pair_ref[j - share // chunks, :, width:]
            both = dot_ff(eff, jnp.concatenate([jnp.where(x, below, 0.0), memory], axis=1))
            first = gain_of(heads, 1, head, pos_ref, cols_ref, planes_ref)
            outs[0][head] = read_ref[head] + first * both[:, :width] + gain * both[:, width:]
        if level == top - 1:
            outs[1][head] = gain_of(heads, top, head, pos_ref, cols_ref, planes_ref) * eff


def last_read_kernel(pos_ref, eff_ref, read_ref, use_ref, got_ref, keep_ref, away_ref):
    share, width = use_ref.shape[:2]
    count = keep_ref.shape[0]
    odd = bit_of(pos_ref, 0)
    x = bit_of(pos_ref, 1)
    for head in range(2 * share):
        c, j = divmod(head, 2 * share // chunks)
        at = c + j % (share // chunks) * chunks
        memory = owned(x, j, share // chunks, use_ref[at], got_ref[at])
        total = read_ref[head] + dot_ff(eff_ref[head], memory)
        lanes = slice(head * width, (head + 1) * width)
        keep_ref[:, lanes] = jnp.where(odd, total[count:], total[:count])
        away_ref[:, lanes] = jnp.where(odd, total[:count], total[count:])


def join_kernel(pos_ref, own_ref, sent_ref, keep_ref, got_ref, out_ref):
    half = out_ref.shape[1] // 2
    odd = bit_of(pos_ref, 0)
    own = keep_ref[...] + own_ref[...]
    other = got_ref[...] + sent_ref[...]
    out_ref[:, :half] = jnp.where(odd, other, own)
    out_ref[:, half:] = jnp.where(odd, own, other)


def near(*shape):
    return pltpu.VMEM(shape, f32)


def params():
    return pltpu.CompilerParams(vmem_limit_bytes=16 << 20)


def run(kernel, out_shapes, position, *arrays, name, static=()):
    held = [pltpu.with_memory_space_constraint(value, pltpu.VMEM) for value in arrays]
    return pl.pallas_call(
        lambda *refs: kernel(*static, *refs),
        out_shape=out_shapes,
        in_specs=[pl.BlockSpec(memory_space=pltpu.SMEM)]
        + [pl.BlockSpec(memory_space=pltpu.VMEM)] * len(arrays),
        compiler_params=params(),
        name=name,
    )(position, *held)


def prepare(position, queries, key_rows, value_rows, write_strength, log_decay, level_gates):
    heads = write_strength.shape[0]
    count = queries.shape[0]
    arrays = (queries, key_rows, value_rows, write_strength, log_decay, level_gates)
    return pl.pallas_call(
        prepare_kernel,
        out_shape=[pltpu.VMEM(value.shape, value.dtype) for value in arrays[:3]]
        + [near(3 * heads, count), near(count, count)],
        in_specs=[pl.BlockSpec(memory_space=pltpu.SMEM)] + [pl.BlockSpec(memory_space=pl.ANY)] * 6,
        scratch_shapes=[pltpu.VMEM(value.shape, value.dtype) for value in arrays[3:]]
        + [pltpu.SemaphoreType.DMA((6,))],
        compiler_params=params(),
        name="prepare",
    )(position, *[pltpu.with_memory_space_constraint(value, pltpu.HBM) for value in arrays])


def shards(queries, key_rows, value_rows, write_strength, log_decay, level_gates):
    size = lax.axis_size("ctx")
    levels = size.bit_length() - 1
    top = levels - 1
    position = lax.axis_index("ctx").astype(jnp.int32).reshape(1)
    heads = write_strength.shape[0]
    half = heads // 2
    share = half // chunks // 2
    count = queries.shape[0]
    width = queries.shape[1] // heads

    def swapped(value, bit):
        return lax.ppermute(value, "ctx", [(i, i ^ (1 << bit)) for i in range(size)])

    *tokens, columns = prepare(
        position, queries, key_rows, value_rows, write_strength, log_decay, level_gates
    )
    sent, local_sent = run(
        block_kernel, [near(3 * half + 1, count, count), near(count, half * width)],
        position, *tokens, columns, name="block_sent", static=(heads, False),
    )
    got = swapped(sent, 0)
    own, local_own = run(
        block_kernel, [near(3 * half, count, count), near(count, half * width)],
        position, *tokens, columns, name="block_own", static=(heads, True),
    )
    *pairs, low = run(
        pair_kernel,
        [near(share, width, 2 * width)] * (2 * chunks) + [near(chunks * share, width, width)],
        position, own, got, name="pair",
    )
    pairs_got = [swapped(pairs[2 * c], 1) for c in range(chunks)]
    eff, read, local_own, local_sent = run(
        first_read_kernel,
        [near(half, 2 * count, width)] * 2 + [near(count, half * width)] * 2,
        position, own, got, columns, local_own, local_sent, name="read_first", static=(heads,),
    )
    pairs_got[0], eff, read, local_own, local_sent = lax.optimization_barrier(
        (pairs_got[0], eff, read, local_own, local_sent)
    )
    totals = [
        run(quad_kernel, near(share, width, 2 * width), position, pairs[2 * c + 1], pairs_got[c], name="quad")
        for c in range(chunks)
    ]
    low, _ = lax.optimization_barrier((low, pairs_got[-1]))
    low = lax.ppermute(low, "ctx", [(i, i + 2) for i in range(size) if (i >> 1) & 1 == 0])
    owned_heads = chunks * share
    prefix = (*pairs[1::2], *pairs_got)
    pending = []
    for level in range(2, top):
        top_next = level == top - 1
        others = [swapped(total, level) for total in totals]
        use, send, *prefix, total = run(
            climb_kernel,
            [near(owned_heads, width, width)] * 2
            + [near(owned_heads, 2 * width, width), near(owned_heads, width, width if top_next else 2 * width)],
            position, *totals, *others, *prefix, name="climb", static=(level, top_next, len(totals)),
        )
        totals = [total]
        pending.append((level, use, send))
    distance = 1 << top
    other = lax.ppermute(totals[0], "ctx", [(i, i + distance) for i in range(size - distance)])
    for level, use, send in pending:
        extra = (low, *pairs_got) if level == 2 else ()
        read, *gated = run(
            functools.partial(read_kernel, heads, level, top),
            [near(half, 2 * count, width)] * (2 if level == top - 1 else 1), position, eff, read, columns,
            got, use, swapped(send, 1), *extra, name="read",
        )
    other, read = lax.optimization_barrier((other, read))
    use, send = run(
        top_kernel, [near(owned_heads, width, width)] * 2, position, *prefix, other, name="top", static=(top,)
    )
    keep, away = run(
        last_read_kernel, [near(count, half * width)] * 2,
        position, *gated, read, use, swapped(send, 1), name="read_last",
    )
    return run(
        join_kernel, jax.ShapeDtypeStruct((count, heads * width), f32), position, local_own, local_sent,
        keep, swapped(away, 0), name="join",
    )


def solution(mesh):
    placed = (
        P(("groups", "ctx"), None),
        P(("groups", "ctx"), None),
        P(("groups", "ctx"), None),
        P(None, ("groups", "ctx")),
        P(None, ("groups", "ctx")),
        P(None, None, ("groups", "ctx")),
    )
    return jax.shard_map(
        shards, mesh=mesh, in_specs=placed, out_specs=P(("groups", "ctx"), None), check_vma=False
    )
```

time: 49.7 us -> 41.5 us (0.84)
  local copies, waits for them, and re-layouts: 4.95 us -> 0 us
  waiting for transfers between devices: 22.4 us -> 19.2 us
    unnamed x12 -> x0, local copies, waits for them, and re-layouts: 4.95 us -> none
    ppermute x6 -> x8, waiting for transfers between devices: 15.5 us -> 13.2 us  [swapped(): return lax.ppermute(value, 'ctx', [(i, i ^ 1 << bit) for i in range(size)])]
    ppermute x2, waiting for transfers between devices: 6.89 us -> 6.06 us  [the longest x1 6.06 us: shards(): lax.ppermute(totals[0], 'ctx', [(i, i + distance) for i in range(size - d...]
    pallas_call x11 -> x12, Pallas kernels: 10.8 us -> 10.9 us  [the longest x11 9.69 us: run(): pl.pallas_call(lambda *refs: kernel(*static, *refs), out_shape=out_shapes...]
    ppermute x6 -> x8, starting transfers between devices: 6.62 us -> 6.62 us  [swapped(): return lax.ppermute(value, 'ctx', [(i, i ^ 1 << bit) for i in range(size)])]
  transfers between devices with their start and end apart: 8 -> 10, of which waited for: 6 -> 7; matrix products, arithmetic and copies ran while one was open for 0% -> 0% of each run, Pallas kernels for 10% -> 13%
where the time goes in v3:
time: 41.5 us; the launch traced here: 41.3 us
  waiting for transfers between devices  19.2 us (46%)
  starting transfers between devices  11 us (27%)
  Pallas kernels  10.9 us (26%)
    ppermute x8, waiting for transfers between devices, swapped(): return lax.ppermute(value, 'ctx', [(i, i ^ 1 << bit) for i in range(size)])  13.2 us
    pallas_call x11, Pallas kernels, run(): pl.pallas_call(lambda *refs: kernel(*static, *refs), out_shape=out_shapes...  9.69 us
    ppermute x8, starting transfers between devices, swapped(): return lax.ppermute(value, 'ctx', [(i, i ^ 1 << bit) for i in range(size)])  6.62 us
    ppermute x1, waiting for transfers between devices, shards(): lax.ppermute(totals[0], 'ctx', [(i, i + distance) for i in range(size - d...  6.06 us
    ppermute x1, starting transfers between devices, shards(): lax.ppermute(low, 'ctx', [(i, i + 2) for i in range(size) if i >> 1 & 1 =...  3.11 us
    ppermute x1, starting transfers between devices, shards(): lax.ppermute(totals[0], 'ctx', [(i, i + distance) for i in range(size - d...  1.28 us
    pallas_call x1, Pallas kernels, prepare(): pl.pallas_call(prepare_kernel, out_shape=[pltpu.VMEM(value.shape, value.d...  1.21 us
  transfers between devices with their start and end apart: 10, of which 7 were waited for; matrix products, arithmetic and copies ran while one was open for 0% of the time, Pallas kernels for 13%

profile of v3, /device:TPU:25, one launch (start us, length us, event | category | flops | bytes accessed | tf_op | source)
XLA Modules:
  0.0 41.3 jit_solution(6617716553621362839)
XLA Ops:
  0.0 1.2 %prepare.1 = (bf16[128,1024]{1,0:T(8,128)(2,1)S(1)}, bf16[128,1024]{1,0:T(8,128)(2,1)S(1)}, bf16[128,1024]{1,0:T(8,128)(2,1)S(1)}, f32[24,128]{1,0:T(8,128)S(1)}, f32[128,128]{1,0:T(8,128)S(1)}) custom-call(s32[1]{0:T(128)} %bitcast.pos_ref.refs_0_, bf16[128,1024]{1,0:T(8,128)(2,1)} %refs_0_.1, bf16[128,1024]{1,0:T(8,128)(2,1)} %refs_1_.1, ...), custom_call_target="tpu_custom_call" | custom-call | tf_op jit(solution)/shard_map/prepare/pallas_call | solution.py:378
  1.2 2.6 %block_sent.1 = (f32[13,128,128]{2,1,0:T(8,128)S(1)}, f32[128,512]{1,0:T(8,128)S(1)}) custom-call(s32[1]{0:T(128)} %bitcast.pos_ref.refs_0_, bf16[128,1024]{1,0:T(8,128)(2,1)S(1)} %get-tuple-element.41.refs_1_, bf16[128,1024]{1,0:T(8,128)(2,1)S(1)} %get-tuple-element.42.refs_2_, bf16[128,1024]{1,0:T(8,128)(2,1)S(1)} %get-tuple-element.43.refs_3_, ...), custom_call_target="tpu_custom_call" | custom-call | tf_op jit(solution)/shard_map/block_sent/pallas_call | solution.py:364
  3.8 0.7 %collective-permute-start = (f32[13,128,128]{2,1,0:T(8,128)S(1)}, f32[13,128,128]{2,1,0:T(8,128)S(1)}, u32[]{:S(2)}, u32[]{:S(2)}) collective-permute-start(f32[13,128,128]{2,1,0:T(8,128)S(1)} %get-tuple-element.47), channel_id=1, source_target_pairs={{0,1},{1,0},{2,3},{3,2},{4,5},{5,4},{6,7},{7,6},{8,9},{9,8},{10,11... | collective-permute-start | bytes 2555912 | tf_op jit(solution)/shard_map/ppermute | solution.py:402
  4.5 2.6 %block_own.1 = (f32[12,128,128]{2,1,0:T(8,128)S(1)}, f32[128,512]{1,0:T(8,128)S(1)}) custom-call(s32[1]{0:T(128)} %bitcast.pos_ref.refs_0_, bf16[128,1024]{1,0:T(8,128)(2,1)S(1)} %get-tuple-element.41.refs_1_, bf16[128,1024]{1,0:T(8,128)(2,1)S(1)} %get-tuple-element.42.refs_2_, bf16[128,1024]{1,0:T(8,128)(2,1)S(1)} %get-tuple-element.43.refs_3_, ...), custom_call_target="tpu_custom_call" | custom-call | tf_op jit(solution)/shard_map/block_own/pallas_call | solution.py:364
  7.1 0.0 collective-permute-done.refs_2_.refs_4_
  7.1 0.3 pair.1
  7.4 1.3 %collective-permute-start.1 = (f32[1,128,256]{2,1,0:T(8,128)S(1)}, f32[1,128,256]{2,1,0:T(8,128)S(1)}, u32[]{:S(2)}, u32[]{:S(2)}) collective-permute-start(f32[1,128,256]{2,1,0:T(8,128)S(1)} %get-tuple-element.48), channel_id=1, source_target_pairs={{0,2},{1,3},{2,0},{3,1},{4,6},{5,7},{6,4},{7,5},{8,10},{9,11},{10,... | collective-permute-start | bytes 393224 | tf_op jit(solution)/shard_map/ppermute | solution.py:402
  8.7 0.3 collective-permute-start.2
  9.0 0.6 %read_first.1 = (f32[4,256,128]{2,1,0:T(8,128)S(1)}, f32[4,256,128]{2,1,0:T(8,128)S(1)}, f32[128,512]{1,0:T(8,128)S(1)}, f32[128,512]{1,0:T(8,128)S(1)}) custom-call(s32[1]{0:T(128)} %bitcast.pos_ref.refs_0_, f32[12,128,128]{2,1,0:T(8,128)S(1)} %get-tuple-element.46.refs_1_, f32[13,128,128]{2,1,0:T(8,128)S(1)} %collective-permute-done.refs_2_.refs_4_, ...), custom_call_target="tpu_custom_call" | custom-call | tf_op jit(solution)/shard_map/read_first/pallas_call | solution.py:364
  9.5 3.0 %collective-permute-done.1.refs_2_.refs_7_.refs_8_ = f32[1,128,256]{2,1,0:T(8,128)S(1)} collective-permute-done((f32[1,128,256]{2,1,0:T(8,128)S(1)}, f32[1,128,256]{2,1,0:T(8,128)S(1)}, u32[]{:S(2)}, u32[]{:S(2)}) %collective-permute-start.1) | collective-permute-done | bytes 131104 | tf_op jit(solution)/shard_map/ppermute | solution.py:402
  12.6 0.2 quad.2.refs_1_
  12.8 0.2 collective-permute-start.3
  13.0 2.4 %collective-permute-done.2.refs_2_.refs_8_.refs_9_ = f32[1,128,256]{2,1,0:T(8,128)S(1)} collective-permute-done((f32[1,128,256]{2,1,0:T(8,128)S(1)}, f32[1,128,256]{2,1,0:T(8,128)S(1)}, u32[]{:S(2)}, u32[]{:S(2)}) %collective-permute-start.2) | collective-permute-done | bytes 131104 | tf_op jit(solution)/shard_map/ppermute | solution.py:402
  15.4 0.2 quad.3.refs_2_
  15.6 0.2 collective-permute-start.4
  15.8 3.1 %collective-permute-start.6 = (f32[2,128,128]{2,1,0:T(8,128)S(1)}, f32[2,128,128]{2,1,0:T(8,128)S(1)}, u32[]{:S(2)}, u32[]{:S(2)}) collective-permute-start(f32[2,128,128]{2,1,0:T(8,128)S(1)} %get-tuple-element.66), channel_id=1, source_target_pairs={{0,2},{1,3},{4,6},{5,7},{8,10},{9,11},{12,14},{13,15},{16,18},{17,... | collective-permute-start | bytes 393224 | tf_op jit(solution)/shard_map/ppermute | solution.py:435
  18.9 0.0 collective-permute-done.3.refs_3_
  18.9 1.7 %collective-permute-done.4.refs_4_ = f32[1,128,256]{2,1,0:T(8,128)S(1)} collective-permute-done((f32[1,128,256]{2,1,0:T(8,128)S(1)}, f32[1,128,256]{2,1,0:T(8,128)S(1)}, u32[]{:S(2)}, u32[]{:S(2)}) %collective-permute-start.4) | collective-permute-done | bytes 131104 | tf_op jit(solution)/shard_map/ppermute | solution.py:402
  20.6 0.3 climb.1
  20.9 1.3 %collective-permute-start.5 = (f32[2,128,128]{2,1,0:T(8,128)S(1)}, f32[2,128,128]{2,1,0:T(8,128)S(1)}, u32[]{:S(2)}, u32[]{:S(2)}) collective-permute-start(f32[2,128,128]{2,1,0:T(8,128)S(1)} %get-tuple-element.64), channel_id=1, source_target_pairs={{0,2},{1,3},{2,0},{3,1},{4,6},{5,7},{6,4},{7,5},{8,10},{9,11},{10,... | collective-permute-start | bytes 393224 | tf_op jit(solution)/shard_map/ppermute | solution.py:402
  22.2 1.3 %collective-permute-start.7 = (f32[2,128,128]{2,1,0:T(8,128)S(1)}, f32[2,128,128]{2,1,0:T(8,128)S(1)}, u32[]{:S(2)}, u32[]{:S(2)}) collective-permute-start(f32[2,128,128]{2,1,0:T(8,128)S(1)} %get-tuple-element.68), channel_id=1, source_target_pairs={{0,8},{1,9},{2,10},{3,11},{4,12},{5,13},{6,14},{7,15},{16,24},{17,... | collective-permute-start | bytes 393224 | tf_op jit(solution)/shard_map/ppermute | solution.py:451
  23.5 0.0 collective-permute-done.6.refs_7_
  23.5 1.3 %collective-permute-done.5.refs_6_ = f32[2,128,128]{2,1,0:T(8,128)S(1)} collective-permute-done((f32[2,128,128]{2,1,0:T(8,128)S(1)}, f32[2,128,128]{2,1,0:T(8,128)S(1)}, u32[]{:S(2)}, u32[]{:S(2)}) %collective-permute-start.5) | collective-permute-done | bytes 131104 | tf_op jit(solution)/shard_map/ppermute | solution.py:402
  24.8 1.6 %read.1 = (f32[4,256,128]{2,1,0:T(8,128)S(1)}, f32[4,256,128]{2,1,0:T(8,128)S(1)}) custom-call(s32[1]{0:T(128)} %bitcast.pos_ref.refs_0_, f32[4,256,128]{2,1,0:T(8,128)S(1)} %get-tuple-element.57.refs_1_, f32[4,256,128]{2,1,0:T(8,128)S(1)} %get-tuple-element.58.refs_2_, f32[128,128]{1,0:T(8,128)S(1)} %get-tuple-element.45.refs_5_.refs_3_, ...), custom_call_target="tpu_custom_call" | custom-call | tf_op jit(solution)/shard_map/read/pallas_call | solution.py:364
  26.4 6.1 %collective-permute-done.7.refs_2_ = f32[2,128,128]{2,1,0:T(8,128)S(1)} collective-permute-done((f32[2,128,128]{2,1,0:T(8,128)S(1)}, f32[2,128,128]{2,1,0:T(8,128)S(1)}, u32[]{:S(2)}, u32[]{:S(2)}) %collective-permute-start.7) | collective-permute-done | bytes 131104 | tf_op jit(solution)/shard_map/ppermute | solution.py:451
  32.5 0.2 top.1
  32.7 0.3 collective-permute-start.8
  33.0 3.6 %collective-permute-done.8.refs_4_ = f32[2,128,128]{2,1,0:T(8,128)S(1)} collective-permute-done((f32[2,128,128]{2,1,0:T(8,128)S(1)}, f32[2,128,128]{2,1,0:T(8,128)S(1)}, u32[]{:S(2)}, u32[]{:S(2)}) %collective-permute-start.8) | collective-permute-done | bytes 131104 | tf_op jit(solution)/shard_map/ppermute | solution.py:402
  36.6 0.3 read_last.1
  36.9 2.4 %collective-permute-start.9 = (f32[128,512]{1,0:T(8,128)S(1)}, f32[128,512]{1,0:T(8,128)S(1)}, u32[]{:S(2)}, u32[]{:S(2)}) collective-permute-start(f32[128,512]{1,0:T(8,128)S(1)} %get-tuple-element.76), channel_id=1, source_target_pairs={{0,1},{1,0},{2,3},{3,2},{4,5},{5,4},{6,7},{7,6},{8,9},{9,8},{10,11... | collective-permute-start | bytes 786440 | tf_op jit(solution)/shard_map/ppermute | solution.py:402
  39.3 1.2 %collective-permute-done.9.refs_4_ = f32[128,512]{1,0:T(8,128)S(1)} collective-permute-done((f32[128,512]{1,0:T(8,128)S(1)}, f32[128,512]{1,0:T(8,128)S(1)}, u32[]{:S(2)}, u32[]{:S(2)}) %collective-permute-start.9) | collective-permute-done | bytes 262176 | tf_op jit(solution)/shard_map/ppermute | solution.py:402
  40.4 0.8 %join.1 = f32[128,1024]{1,0:T(8,128)} custom-call(s32[1]{0:T(128)} %bitcast.pos_ref.refs_0_, f32[128,512]{1,0:T(8,128)S(1)} %get-tuple-element.55.refs_1_, f32[128,512]{1,0:T(8,128)S(1)} %get-tuple-element.56.refs_2_, f32[128,512]{1,0:T(8,128)S(1)} %get-tuple-element.75.refs_3_, f32[128,512]{1,0:T(8,128)S(1)} %collective-permute-done.9.refs_4_), custom_call_target="tpu_custom_call" | custom-call | tf_op jit(solution)/shard_map/join/pallas_call | solution.py:364
Async XLA Ops:
  3.8 3.3 %collective-permute-start = (f32[13,128,128]{2,1,0:T(8,128)S(1)}, f32[13,128,128]{2,1,0:T(8,128)S(1)}, u32[]{:S(2)}, u32[]{:S(2)}) collective-permute-start(f32[13,128,128]{2,1,0:T(8,128)S(1)} %get-tuple-element.47), channel_id=1, source_target_pairs={{0,1},{1,0},{2,3},{3,2},{4,5},{5,4},{6,7},{7,6},{8,9},{9,8},{10,11... | collective-permute-start | bytes 2555912 | tf_op jit(solution)/shard_map/ppermute | solution.py:402
  7.4 5.1 %collective-permute-start.1 = (f32[1,128,256]{2,1,0:T(8,128)S(1)}, f32[1,128,256]{2,1,0:T(8,128)S(1)}, u32[]{:S(2)}, u32[]{:S(2)}) collective-permute-start(f32[1,128,256]{2,1,0:T(8,128)S(1)} %get-tuple-element.48), channel_id=1, source_target_pairs={{0,2},{1,3},{2,0},{3,1},{4,6},{5,7},{6,4},{7,5},{8,10},{9,11},{10,... | collective-permute-start | bytes 393224 | tf_op jit(solution)/shard_map/ppermute | solution.py:402
  8.7 6.6 %collective-permute-start.2 = (f32[1,128,256]{2,1,0:T(8,128)S(1)}, f32[1,128,256]{2,1,0:T(8,128)S(1)}, u32[]{:S(2)}, u32[]{:S(2)}) collective-permute-start(f32[1,128,256]{2,1,0:T(8,128)S(1)} %get-tuple-element.62), channel_id=1, source_target_pairs={{0,2},{1,3},{2,0},{3,1},{4,6},{5,7},{6,4},{7,5},{8,10},{9,11},{10,... | collective-permute-start | bytes 393224 | tf_op jit(solution)/shard_map/ppermute | solution.py:402
  12.8 6.1 %collective-permute-start.3 = (f32[1,128,256]{2,1,0:T(8,128)S(1)}, f32[1,128,256]{2,1,0:T(8,128)S(1)}, u32[]{:S(2)}, u32[]{:S(2)}) collective-permute-start(f32[1,128,256]{2,1,0:T(8,128)S(1)} %quad.2.refs_1_), channel_id=1, source_target_pairs={{0,4},{1,5},{2,6},{3,7},{4,0},{5,1},{6,2},{7,3},{8,12},{9,13},{10,... | collective-permute-start | bytes 393224 | tf_op jit(solution)/shard_map/ppermute | solution.py:402
  15.6 5.1 %collective-permute-start.4 = (f32[1,128,256]{2,1,0:T(8,128)S(1)}, f32[1,128,256]{2,1,0:T(8,128)S(1)}, u32[]{:S(2)}, u32[]{:S(2)}) collective-permute-start(f32[1,128,256]{2,1,0:T(8,128)S(1)} %quad.3.refs_2_), channel_id=1, source_target_pairs={{0,4},{1,5},{2,6},{3,7},{4,0},{5,1},{6,2},{7,3},{8,12},{9,13},{10,... | collective-permute-start | bytes 393224 | tf_op jit(solution)/shard_map/ppermute | solution.py:402
  15.8 7.7 %collective-permute-start.6 = (f32[2,128,128]{2,1,0:T(8,128)S(1)}, f32[2,128,128]{2,1,0:T(8,128)S(1)}, u32[]{:S(2)}, u32[]{:S(2)}) collective-permute-start(f32[2,128,128]{2,1,0:T(8,128)S(1)} %get-tuple-element.66), channel_id=1, source_target_pairs={{0,2},{1,3},{4,6},{5,7},{8,10},{9,11},{12,14},{13,15},{16,18},{17,... | collective-permute-start | bytes 393224 | tf_op jit(solution)/shard_map/ppermute | solution.py:435
  20.9 3.9 %collective-permute-start.5 = (f32[2,128,128]{2,1,0:T(8,128)S(1)}, f32[2,128,128]{2,1,0:T(8,128)S(1)}, u32[]{:S(2)}, u32[]{:S(2)}) collective-permute-start(f32[2,128,128]{2,1,0:T(8,128)S(1)} %get-tuple-element.64), channel_id=1, source_target_pairs={{0,2},{1,3},{2,0},{3,1},{4,6},{5,7},{6,4},{7,5},{8,10},{9,11},{10,... | collective-permute-start | bytes 393224 | tf_op jit(solution)/shard_map/ppermute | solution.py:402
  22.2 10.3 %collective-permute-start.7 = (f32[2,128,128]{2,1,0:T(8,128)S(1)}, f32[2,128,128]{2,1,0:T(8,128)S(1)}, u32[]{:S(2)}, u32[]{:S(2)}) collective-permute-start(f32[2,128,128]{2,1,0:T(8,128)S(1)} %get-tuple-element.68), channel_id=1, source_target_pairs={{0,8},{1,9},{2,10},{3,11},{4,12},{5,13},{6,14},{7,15},{16,24},{17,... | collective-permute-start | bytes 393224 | tf_op jit(solution)/shard_map/ppermute | solution.py:451
  32.7 3.9 %collective-permute-start.8 = (f32[2,128,128]{2,1,0:T(8,128)S(1)}, f32[2,128,128]{2,1,0:T(8,128)S(1)}, u32[]{:S(2)}, u32[]{:S(2)}) collective-permute-start(f32[2,128,128]{2,1,0:T(8,128)S(1)} %get-tuple-element.74), channel_id=1, source_target_pairs={{0,2},{1,3},{2,0},{3,1},{4,6},{5,7},{6,4},{7,5},{8,10},{9,11},{10,... | collective-permute-start | bytes 393224 | tf_op jit(solution)/shard_map/ppermute | solution.py:402
  36.9 3.5 %collective-permute-start.9 = (f32[128,512]{1,0:T(8,128)S(1)}, f32[128,512]{1,0:T(8,128)S(1)}, u32[]{:S(2)}, u32[]{:S(2)}) collective-permute-start(f32[128,512]{1,0:T(8,128)S(1)} %get-tuple-element.76), channel_id=1, source_target_pairs={{0,1},{1,0},{2,3},{3,2},{4,5},{5,4},{6,7},{7,6},{8,9},{9,8},{10,11... | collective-permute-start | bytes 786440 | tf_op jit(solution)/shard_map/ppermute | solution.py:402

commit v4 on v3

--- a/solution.py
+++ b/solution.py
@@ -432,7 +432,7 @@
         for c in range(chunks)
     ]
     low, _ = lax.optimization_barrier((low, pairs_got[-1]))
-    low = lax.ppermute(low, "ctx", [(i, i + 2) for i in range(size) if (i >> 1) & 1 == 0])
+    low = swapped(low, 1)
     owned_heads = chunks * share
     prefix = (*pairs[1::2], *pairs_got)
     pending = []
@@ -447,22 +447,24 @@
         )
         totals = [total]
         pending.append((level, use, send))
-    distance = 1 << top
-    other = lax.ppermute(totals[0], "ctx", [(i, i + distance) for i in range(size - distance)])
-    for level, use, send in pending:
+    other = swapped(totals[0], top)
+    use, send = run(
+        top_kernel, [near(owned_heads, width, width)] * 2, position, *prefix, other, name="top", static=(top,)
+    )
+    last_other = swapped(send, 1)
+    for level, level_use, level_send in pending:
         extra = (low, *pairs_got) if level == 2 else ()
+        level_other = swapped(level_send, 1)
+        if level == top - 1:
+            level_other, _ = lax.optimization_barrier((level_other, send))
         read, *gated = run(
             functools.partial(read_kernel, heads, level, top),
             [near(half, 2 * count, width)] * (2 if level == top - 1 else 1), position, eff, read, columns,
-            got, use, swapped(send, 1), *extra, name="read",
+            got, level_use, level_other, *extra, name="read",
         )
-    other, read = lax.optimization_barrier((other, read))
-    use, send = run(
-        top_kernel, [near(owned_heads, width, width)] * 2, position, *prefix, other, name="top", static=(top,)
-    )
     keep, away = run(
         last_read_kernel, [near(count, half * width)] * 2,
-        position, *gated, read, use, swapped(send, 1), name="read_last",
+        position, *gated, read, use, last_other, name="read_last",
     )
     return run(
         join_kernel, jax.ShapeDtypeStruct((count, heads * width), f32), position, local_own, local_sent,

time: 41.5 us -> 39.6 us (0.954)
  the two profiles are of different devices: /device:TPU:25 before, /device:TPU:0 now
where the time goes in v4:
time: 39.6 us; the launch traced here: 39.4 us
  waiting for transfers between devices  14.4 us (36%)
  starting transfers between devices  14 us (35%)
  Pallas kernels  10.9 us (28%)
    ppermute x10, waiting for transfers between devices, swapped(): return lax.ppermute(value, 'ctx', [(i, i ^ 1 << bit) for i in range(size)])  14.4 us
    ppermute x10, starting transfers between devices, swapped(): return lax.ppermute(value, 'ctx', [(i, i ^ 1 << bit) for i in range(size)])  14 us
    pallas_call x11, Pallas kernels, run(): pl.pallas_call(lambda *refs: kernel(*static, *refs), out_shape=out_shapes...  9.7 us
    pallas_call x1, Pallas kernels, prepare(): pl.pallas_call(prepare_kernel, out_shape=[pltpu.VMEM(value.shape, value.d...  1.21 us
  transfers between devices with their start and end apart: 10, of which 7 were waited for; matrix products, arithmetic and copies ran while one was open for 0% of the time, Pallas kernels for 14%

profile of v4, /device:TPU:0, one launch (start us, length us, event | category | flops | bytes accessed | tf_op | source)
XLA Modules:
  0.0 39.4 jit_solution(4772946178092656038)
XLA Ops:
  0.0 1.2 %prepare.1 = (bf16[128,1024]{1,0:T(8,128)(2,1)S(1)}, bf16[128,1024]{1,0:T(8,128)(2,1)S(1)}, bf16[128,1024]{1,0:T(8,128)(2,1)S(1)}, f32[24,128]{1,0:T(8,128)S(1)}, f32[128,128]{1,0:T(8,128)S(1)}) custom-call(s32[1]{0:T(128)} %bitcast.pos_ref.refs_0_, bf16[128,1024]{1,0:T(8,128)(2,1)} %refs_0_.1, bf16[128,1024]{1,0:T(8,128)(2,1)} %refs_1_.1, ...), custom_call_target="tpu_custom_call" | custom-call | tf_op jit(solution)/shard_map/prepare/pallas_call | solution.py:378
  1.2 2.6 %block_sent.1 = (f32[13,128,128]{2,1,0:T(8,128)S(1)}, f32[128,512]{1,0:T(8,128)S(1)}) custom-call(s32[1]{0:T(128)} %bitcast.pos_ref.refs_0_, bf16[128,1024]{1,0:T(8,128)(2,1)S(1)} %get-tuple-element.40.refs_1_, bf16[128,1024]{1,0:T(8,128)(2,1)S(1)} %get-tuple-element.41.refs_2_, bf16[128,1024]{1,0:T(8,128)(2,1)S(1)} %get-tuple-element.42.refs_3_, ...), custom_call_target="tpu_custom_call" | custom-call | tf_op jit(solution)/shard_map/block_sent/pallas_call | solution.py:364
  3.8 0.6 %collective-permute-start = (f32[13,128,128]{2,1,0:T(8,128)S(1)}, f32[13,128,128]{2,1,0:T(8,128)S(1)}, u32[]{:S(2)}, u32[]{:S(2)}) collective-permute-start(f32[13,128,128]{2,1,0:T(8,128)S(1)} %get-tuple-element.46), channel_id=1, source_target_pairs={{0,1},{1,0},{2,3},{3,2},{4,5},{5,4},{6,7},{7,6},{8,9},{9,8},{10,11... | collective-permute-start | bytes 2555912 | tf_op jit(solution)/shard_map/ppermute | solution.py:402
  4.3 2.6 %block_own.1 = (f32[12,128,128]{2,1,0:T(8,128)S(1)}, f32[128,512]{1,0:T(8,128)S(1)}) custom-call(s32[1]{0:T(128)} %bitcast.pos_ref.refs_0_, bf16[128,1024]{1,0:T(8,128)(2,1)S(1)} %get-tuple-element.40.refs_1_, bf16[128,1024]{1,0:T(8,128)(2,1)S(1)} %get-tuple-element.41.refs_2_, bf16[128,1024]{1,0:T(8,128)(2,1)S(1)} %get-tuple-element.42.refs_3_, ...), custom_call_target="tpu_custom_call" | custom-call | tf_op jit(solution)/shard_map/block_own/pallas_call | solution.py:364
  6.9 0.0 collective-permute-done.refs_2_.refs_4_
  6.9 0.3 pair.1
  7.3 2.5 %collective-permute-start.1 = (f32[1,128,256]{2,1,0:T(8,128)S(1)}, f32[1,128,256]{2,1,0:T(8,128)S(1)}, u32[]{:S(2)}, u32[]{:S(2)}) collective-permute-start(f32[1,128,256]{2,1,0:T(8,128)S(1)} %get-tuple-element.47), channel_id=1, source_target_pairs={{0,2},{1,3},{2,0},{3,1},{4,6},{5,7},{6,4},{7,5},{8,10},{9,11},{10,... | collective-permute-start | bytes 393224 | tf_op jit(solution)/shard_map/ppermute | solution.py:402
  9.8 0.1 collective-permute-start.2
  9.9 0.6 %read_first.1 = (f32[4,256,128]{2,1,0:T(8,128)S(1)}, f32[4,256,128]{2,1,0:T(8,128)S(1)}, f32[128,512]{1,0:T(8,128)S(1)}, f32[128,512]{1,0:T(8,128)S(1)}) custom-call(s32[1]{0:T(128)} %bitcast.pos_ref.refs_0_, f32[12,128,128]{2,1,0:T(8,128)S(1)} %get-tuple-element.45.refs_1_, f32[13,128,128]{2,1,0:T(8,128)S(1)} %collective-permute-done.refs_2_.refs_4_, ...), custom_call_target="tpu_custom_call" | custom-call | tf_op jit(solution)/shard_map/read_first/pallas_call | solution.py:364
  10.5 3.7 %collective-permute-done.1.refs_2_.refs_7_.refs_8_ = f32[1,128,256]{2,1,0:T(8,128)S(1)} collective-permute-done((f32[1,128,256]{2,1,0:T(8,128)S(1)}, f32[1,128,256]{2,1,0:T(8,128)S(1)}, u32[]{:S(2)}, u32[]{:S(2)}) %collective-permute-start.1) | collective-permute-done | bytes 131104 | tf_op jit(solution)/shard_map/ppermute | solution.py:402
  14.2 0.2 quad.2.refs_1_
  14.4 2.2 %collective-permute-start.3 = (f32[1,128,256]{2,1,0:T(8,128)S(1)}, f32[1,128,256]{2,1,0:T(8,128)S(1)}, u32[]{:S(2)}, u32[]{:S(2)}) collective-permute-start(f32[1,128,256]{2,1,0:T(8,128)S(1)} %quad.2.refs_1_), channel_id=1, source_target_pairs={{0,4},{1,5},{2,6},{3,7},{4,0},{5,1},{6,2},{7,3},{8,12},{9,13},{10,... | collective-permute-start | bytes 393224 | tf_op jit(solution)/shard_map/ppermute | solution.py:402
  16.5 0.2 collective-permute-done.2.refs_2_.refs_8_.refs_9_
  16.8 0.2 quad.3.refs_2_
  17.0 1.9 %collective-permute-start.4 = (f32[1,128,256]{2,1,0:T(8,128)S(1)}, f32[1,128,256]{2,1,0:T(8,128)S(1)}, u32[]{:S(2)}, u32[]{:S(2)}) collective-permute-start(f32[1,128,256]{2,1,0:T(8,128)S(1)} %quad.3.refs_2_), channel_id=1, source_target_pairs={{0,4},{1,5},{2,6},{3,7},{4,0},{5,1},{6,2},{7,3},{8,12},{9,13},{10,... | collective-permute-start | bytes 393224 | tf_op jit(solution)/shard_map/ppermute | solution.py:402
  18.9 0.7 %collective-permute-done.3.refs_3_ = f32[1,128,256]{2,1,0:T(8,128)S(1)} collective-permute-done((f32[1,128,256]{2,1,0:T(8,128)S(1)}, f32[1,128,256]{2,1,0:T(8,128)S(1)}, u32[]{:S(2)}, u32[]{:S(2)}) %collective-permute-start.3) | collective-permute-done | bytes 131104 | tf_op jit(solution)/shard_map/ppermute | solution.py:402
  19.6 2.8 %collective-permute-done.4.refs_4_ = f32[1,128,256]{2,1,0:T(8,128)S(1)} collective-permute-done((f32[1,128,256]{2,1,0:T(8,128)S(1)}, f32[1,128,256]{2,1,0:T(8,128)S(1)}, u32[]{:S(2)}, u32[]{:S(2)}) %collective-permute-start.4) | collective-permute-done | bytes 131104 | tf_op jit(solution)/shard_map/ppermute | solution.py:402
  22.4 0.3 climb.1
  22.7 3.0 %collective-permute-start.6 = (f32[2,128,128]{2,1,0:T(8,128)S(1)}, f32[2,128,128]{2,1,0:T(8,128)S(1)}, u32[]{:S(2)}, u32[]{:S(2)}) collective-permute-start(f32[2,128,128]{2,1,0:T(8,128)S(1)} %get-tuple-element.65), channel_id=1, source_target_pairs={{0,8},{1,9},{2,10},{3,11},{4,12},{5,13},{6,14},{7,15},{8,0},{9,1},... | collective-permute-start | bytes 393224 | tf_op jit(solution)/shard_map/ppermute | solution.py:402
  25.7 1.5 %collective-permute-start.5 = (f32[2,128,128]{2,1,0:T(8,128)S(1)}, f32[2,128,128]{2,1,0:T(8,128)S(1)}, u32[]{:S(2)}, u32[]{:S(2)}) collective-permute-start(f32[2,128,128]{2,1,0:T(8,128)S(1)} %get-tuple-element.63), channel_id=1, source_target_pairs={{0,2},{1,3},{2,0},{3,1},{4,6},{5,7},{6,4},{7,5},{8,10},{9,11},{10,... | collective-permute-start | bytes 393224 | tf_op jit(solution)/shard_map/ppermute | solution.py:402
  27.2 0.5 %collective-permute-start.7 = (f32[2,128,128]{2,1,0:T(8,128)S(1)}, f32[2,128,128]{2,1,0:T(8,128)S(1)}, u32[]{:S(2)}, u32[]{:S(2)}) collective-permute-start(f32[2,128,128]{2,1,0:T(8,128)S(1)} %get-tuple-element.69), channel_id=1, source_target_pairs={{0,2},{1,3},{2,0},{3,1},{4,6},{5,7},{6,4},{7,5},{8,10},{9,11},{10,... | collective-permute-start | bytes 393224 | tf_op jit(solution)/shard_map/ppermute | solution.py:402
  27.7 3.6 %collective-permute-done.6.refs_2_ = f32[2,128,128]{2,1,0:T(8,128)S(1)} collective-permute-done((f32[2,128,128]{2,1,0:T(8,128)S(1)}, f32[2,128,128]{2,1,0:T(8,128)S(1)}, u32[]{:S(2)}, u32[]{:S(2)}) %collective-permute-start.6) | collective-permute-done | bytes 131104 | tf_op jit(solution)/shard_map/ppermute | solution.py:402
  31.4 0.2 top.1
  31.6 1.6 %collective-permute-start.8 = (f32[2,128,128]{2,1,0:T(8,128)S(1)}, f32[2,128,128]{2,1,0:T(8,128)S(1)}, u32[]{:S(2)}, u32[]{:S(2)}) collective-permute-start(f32[2,128,128]{2,1,0:T(8,128)S(1)} %get-tuple-element.66), channel_id=1, source_target_pairs={{0,2},{1,3},{2,0},{3,1},{4,6},{5,7},{6,4},{7,5},{8,10},{9,11},{10,... | collective-permute-start | bytes 393224 | tf_op jit(solution)/shard_map/ppermute | solution.py:402
  33.2 0.0 collective-permute-done.5.refs_6_
  33.2 0.0 collective-permute-done.7.refs_7_
  33.2 1.6 %read.1 = (f32[4,256,128]{2,1,0:T(8,128)S(1)}, f32[4,256,128]{2,1,0:T(8,128)S(1)}) custom-call(s32[1]{0:T(128)} %bitcast.pos_ref.refs_0_, f32[4,256,128]{2,1,0:T(8,128)S(1)} %get-tuple-element.56.refs_1_, f32[4,256,128]{2,1,0:T(8,128)S(1)} %get-tuple-element.57.refs_2_, f32[128,128]{1,0:T(8,128)S(1)} %get-tuple-element.44.refs_5_.refs_3_, ...), custom_call_target="tpu_custom_call" | custom-call | tf_op jit(solution)/shard_map/read/pallas_call | solution.py:364
  34.8 1.8 %collective-permute-done.8.refs_4_ = f32[2,128,128]{2,1,0:T(8,128)S(1)} collective-permute-done((f32[2,128,128]{2,1,0:T(8,128)S(1)}, f32[2,128,128]{2,1,0:T(8,128)S(1)}, u32[]{:S(2)}, u32[]{:S(2)}) %collective-permute-start.8) | collective-permute-done | bytes 131104 | tf_op jit(solution)/shard_map/ppermute | solution.py:402
  36.6 0.3 read_last.1
  37.0 0.1 collective-permute-start.9
  37.0 1.5 %collective-permute-done.9.refs_4_ = f32[128,512]{1,0:T(8,128)S(1)} collective-permute-done((f32[128,512]{1,0:T(8,128)S(1)}, f32[128,512]{1,0:T(8,128)S(1)}, u32[]{:S(2)}, u32[]{:S(2)}) %collective-permute-start.9) | collective-permute-done | bytes 262176 | tf_op jit(solution)/shard_map/ppermute | solution.py:402
  38.6 0.8 %join.1 = f32[128,1024]{1,0:T(8,128)} custom-call(s32[1]{0:T(128)} %bitcast.pos_ref.refs_0_, f32[128,512]{1,0:T(8,128)S(1)} %get-tuple-element.54.refs_1_, f32[128,512]{1,0:T(8,128)S(1)} %get-tuple-element.55.refs_2_, f32[128,512]{1,0:T(8,128)S(1)} %get-tuple-element.73.refs_3_, f32[128,512]{1,0:T(8,128)S(1)} %collective-permute-done.9.refs_4_), custom_call_target="tpu_custom_call" | custom-call | tf_op jit(solution)/shard_map/join/pallas_call | solution.py:364
Async XLA Ops:
  3.8 3.1 %collective-permute-start = (f32[13,128,128]{2,1,0:T(8,128)S(1)}, f32[13,128,128]{2,1,0:T(8,128)S(1)}, u32[]{:S(2)}, u32[]{:S(2)}) collective-permute-start(f32[13,128,128]{2,1,0:T(8,128)S(1)} %get-tuple-element.46), channel_id=1, source_target_pairs={{0,1},{1,0},{2,3},{3,2},{4,5},{5,4},{6,7},{7,6},{8,9},{9,8},{10,11... | collective-permute-start | bytes 2555912 | tf_op jit(solution)/shard_map/ppermute | solution.py:402
  7.3 6.9 %collective-permute-start.1 = (f32[1,128,256]{2,1,0:T(8,128)S(1)}, f32[1,128,256]{2,1,0:T(8,128)S(1)}, u32[]{:S(2)}, u32[]{:S(2)}) collective-permute-start(f32[1,128,256]{2,1,0:T(8,128)S(1)} %get-tuple-element.47), channel_id=1, source_target_pairs={{0,2},{1,3},{2,0},{3,1},{4,6},{5,7},{6,4},{7,5},{8,10},{9,11},{10,... | collective-permute-start | bytes 393224 | tf_op jit(solution)/shard_map/ppermute | solution.py:402
  9.8 7.0 %collective-permute-start.2 = (f32[1,128,256]{2,1,0:T(8,128)S(1)}, f32[1,128,256]{2,1,0:T(8,128)S(1)}, u32[]{:S(2)}, u32[]{:S(2)}) collective-permute-start(f32[1,128,256]{2,1,0:T(8,128)S(1)} %get-tuple-element.61), channel_id=1, source_target_pairs={{0,2},{1,3},{2,0},{3,1},{4,6},{5,7},{6,4},{7,5},{8,10},{9,11},{10,... | collective-permute-start | bytes 393224 | tf_op jit(solution)/shard_map/ppermute | solution.py:402
  14.4 5.2 %collective-permute-start.3 = (f32[1,128,256]{2,1,0:T(8,128)S(1)}, f32[1,128,256]{2,1,0:T(8,128)S(1)}, u32[]{:S(2)}, u32[]{:S(2)}) collective-permute-start(f32[1,128,256]{2,1,0:T(8,128)S(1)} %quad.2.refs_1_), channel_id=1, source_target_pairs={{0,4},{1,5},{2,6},{3,7},{4,0},{5,1},{6,2},{7,3},{8,12},{9,13},{10,... | collective-permute-start | bytes 393224 | tf_op jit(solution)/shard_map/ppermute | solution.py:402
  17.0 5.4 %collective-permute-start.4 = (f32[1,128,256]{2,1,0:T(8,128)S(1)}, f32[1,128,256]{2,1,0:T(8,128)S(1)}, u32[]{:S(2)}, u32[]{:S(2)}) collective-permute-start(f32[1,128,256]{2,1,0:T(8,128)S(1)} %quad.3.refs_2_), channel_id=1, source_target_pairs={{0,4},{1,5},{2,6},{3,7},{4,0},{5,1},{6,2},{7,3},{8,12},{9,13},{10,... | collective-permute-start | bytes 393224 | tf_op jit(solution)/shard_map/ppermute | solution.py:402
  22.7 8.7 %collective-permute-start.6 = (f32[2,128,128]{2,1,0:T(8,128)S(1)}, f32[2,128,128]{2,1,0:T(8,128)S(1)}, u32[]{:S(2)}, u32[]{:S(2)}) collective-permute-start(f32[2,128,128]{2,1,0:T(8,128)S(1)} %get-tuple-element.65), channel_id=1, source_target_pairs={{0,8},{1,9},{2,10},{3,11},{4,12},{5,13},{6,14},{7,15},{8,0},{9,1},... | collective-permute-start | bytes 393224 | tf_op jit(solution)/shard_map/ppermute | solution.py:402
  25.7 7.5 %collective-permute-start.5 = (f32[2,128,128]{2,1,0:T(8,128)S(1)}, f32[2,128,128]{2,1,0:T(8,128)S(1)}, u32[]{:S(2)}, u32[]{:S(2)}) collective-permute-start(f32[2,128,128]{2,1,0:T(8,128)S(1)} %get-tuple-element.63), channel_id=1, source_target_pairs={{0,2},{1,3},{2,0},{3,1},{4,6},{5,7},{6,4},{7,5},{8,10},{9,11},{10,... | collective-permute-start | bytes 393224 | tf_op jit(solution)/shard_map/ppermute | solution.py:402
  27.2 6.0 %collective-permute-start.7 = (f32[2,128,128]{2,1,0:T(8,128)S(1)}, f32[2,128,128]{2,1,0:T(8,128)S(1)}, u32[]{:S(2)}, u32[]{:S(2)}) collective-permute-start(f32[2,128,128]{2,1,0:T(8,128)S(1)} %get-tuple-element.69), channel_id=1, source_target_pairs={{0,2},{1,3},{2,0},{3,1},{4,6},{5,7},{6,4},{7,5},{8,10},{9,11},{10,... | collective-permute-start | bytes 393224 | tf_op jit(solution)/shard_map/ppermute | solution.py:402
  31.6 5.0 %collective-permute-start.8 = (f32[2,128,128]{2,1,0:T(8,128)S(1)}, f32[2,128,128]{2,1,0:T(8,128)S(1)}, u32[]{:S(2)}, u32[]{:S(2)}) collective-permute-start(f32[2,128,128]{2,1,0:T(8,128)S(1)} %get-tuple-element.66), channel_id=1, source_target_pairs={{0,2},{1,3},{2,0},{3,1},{4,6},{5,7},{6,4},{7,5},{8,10},{9,11},{10,... | collective-permute-start | bytes 393224 | tf_op jit(solution)/shard_map/ppermute | solution.py:402
  37.0 1.6 %collective-permute-start.9 = (f32[128,512]{1,0:T(8,128)S(1)}, f32[128,512]{1,0:T(8,128)S(1)}, u32[]{:S(2)}, u32[]{:S(2)}) collective-permute-start(f32[128,512]{1,0:T(8,128)S(1)} %get-tuple-element.74), channel_id=1, source_target_pairs={{0,1},{1,0},{2,3},{3,2},{4,5},{5,4},{6,7},{7,6},{8,9},{9,8},{10,11... | collective-permute-start | bytes 786440 | tf_op jit(solution)/shard_map/ppermute | solution.py:402

commit v5 on v4

--- a/solution.py
+++ b/solution.py
@@ -47,12 +47,13 @@
     return ((pos_ref[0] >> bit) & 1) == 1
 
 
-def prepare_kernel(pos_ref, *refs):
+def opening_kernel(pos_ref, *refs):
     arrays = refs[:6]
-    q_ref, k_ref, v_ref, rows_ref, columns_ref, beta_ref, decay_ref, gates_ref, sems = refs[6:]
+    q_ref, k_ref, v_ref, rows_ref, columns_ref, planes_ref, inverse_ref = refs[6:13]
+    beta_ref, decay_ref, gates_ref, sems = refs[13:]
     targets = (q_ref, k_ref, v_ref, beta_ref, decay_ref, gates_ref)
     copies = [pltpu.make_async_copy(a, t, sems.at[i]) for i, (a, t) in enumerate(zip(arrays, targets))]
-    for i in (4, 3, 5, 1, 0, 2):
+    for i in (4, 3, 5, 1, 2, 0):
         copies[i].start()
     heads, count = beta_ref.shape
     half = heads // 2
@@ -79,65 +80,68 @@
     filler = jnp.zeros((count - len(kinds) * heads, count), f32)
     columns_ref[...] = jnp.concatenate(kinds + [filler], axis=0).T
     rows_ref[...] = jnp.concatenate(kinds[:3], axis=0)
-    for i in (1, 0, 2):
-        copies[i].wait()
-
-
-def block_kernel(heads, mine, pos_ref, q_ref, k_ref, v_ref, rows_ref, columns_ref, planes_ref, local_ref):
-    half = heads // 2
-    n = half
-    count = q_ref.shape[0]
-    width = q_ref.shape[1] // heads
-    core = pos_ref[0] & 1
-    side = core if mine else 1 - core
-    row = lax.broadcasted_iota(jnp.int32, (count, count), 0)
-    col = lax.broadcasted_iota(jnp.int32, (count, count), 1)
-    base = 0 if mine else half
-    columns = columns_ref[...]
-    if planes_ref.shape[0] > 3 * n:
-        planes_ref[3 * n] = columns
-
-    def column(kind, j):
-        at = kind * heads + base + j
-        return columns[:, at : at + 1]
-
-    def line(kind, j):
-        at = kind * heads + base + j
-        return rows_ref[at : at + 1]
-
-    def lanes(ref, j):
-        at = pl.multiple_of(side * (half * width) + j * width, 128)
+    copies[1].wait()
+    copies[2].wait()
+    block_kernel(heads, False, pos_ref, k_ref, v_ref, rows_ref, columns_ref, planes_ref, inverse_ref)
+    copies[0].wait()
+
+
+class Tokens:
+    def __init__(self, heads, mine, pos_ref, rows_ref, columns_ref):
+        self.heads, self.half = heads, heads // 2
+        core = pos_ref[0] & 1
+        self.side = core if mine else 1 - core
+        self.base = 0 if mine else self.half
+        self.rows_ref, self.columns = rows_ref, columns_ref[...]
+        count = self.columns.shape[0]
+        self.row = lax.broadcasted_iota(jnp.int32, (count, count), 0)
+        self.col = lax.broadcasted_iota(jnp.int32, (count, count), 1)
+        self.lower_incl = self.row >= self.col
+
+    def column(self, kind, j):
+        at = kind * self.heads + self.base + j
+        return self.columns[:, at : at + 1]
+
+    def line(self, kind, j):
+        at = kind * self.heads + self.base + j
+        return self.rows_ref[at : at + 1]
+
+    def lanes(self, ref, j):
+        width = ref.shape[1] // self.heads
+        at = pl.multiple_of(self.side * (self.half * width) + j * width, 128)
         return ref[:, pl.ds(at, width)]
 
-    k_rows, q_rows, k_norm = [], [], jnp.zeros((count, count), f32)
-    scales = []
+    def scale(self, ref, j):
+        value = self.lanes(ref, j).astype(f32)
+        return lax.rsqrt(jnp.sum(value * value, axis=1, keepdims=True) + norm_eps)
+
+    def scale_rows(self, scales):
+        value = jnp.zeros(self.row.shape, f32)
+        for j, scale in enumerate(scales):
+            value = jnp.where(self.col == j, scale, value)
+        return value.T
+
+    def run_all(self, j):
+        return jnp.broadcast_to(self.column(0, j), self.row.shape)
+
+    def ratio(self, run_all, j):
+        gap = jnp.where(self.lower_incl, run_all - self.line(0, j), 0.0)
+        return jnp.where(self.lower_incl, jnp.exp(gap), 0.0)
+
+
+def block_kernel(heads, mine, pos_ref, k_ref, v_ref, rows_ref, columns_ref, planes_ref, inverse_ref):
+    t = Tokens(heads, mine, pos_ref, rows_ref, columns_ref)
+    n, row, col = t.half, t.row, t.col
+    count = row.shape[0]
+    scales = [t.scale(k_ref, j) for j in range(n)]
+    norm_rows = t.scale_rows(scales)
+    belows, runs = [], []
     for j in range(n):
-        kj = lanes(k_ref, j)
-        qj = lanes(q_ref, j)
-        kf = kj.astype(f32)
-        qf = qj.astype(f32)
-        k_scale = lax.rsqrt(jnp.sum(kf * kf, axis=1, keepdims=True) + norm_eps)
-        q_scale = lax.rsqrt(jnp.sum(qf * qf, axis=1, keepdims=True) + norm_eps)
-        k_norm = jnp.where(col == j, k_scale, k_norm)
-        k_rows.append(kj)
-        q_rows.append(qj)
-        scales.append((k_scale, q_scale))
-    k_norm_rows = k_norm.T
-
-    lower_incl = row >= col
-    belows, query_grams, runs = [], [], []
-    for j in range(n):
-        k_scale, q_scale = scales[j]
-        kj = k_rows[j]
-        run_row = line(0, j)
-        run_all = jnp.broadcast_to(column(0, j), (count, count))
-        runs.append(run_all)
-        gap = jnp.where(lower_incl, run_all - run_row, 0.0)
-        ratio = jnp.where(lower_incl, jnp.exp(gap), 0.0) * k_norm_rows[j : j + 1]
-        grams = mm(jnp.concatenate([kj, q_rows[j]], axis=0), kj, ((1,), (1,)))
-        below = jnp.where(row > col, grams[:count] * ratio * (column(1, j) * k_scale), 0.0)
-        query_grams.append(grams[count:] * ratio * q_scale)
-        belows.append(below)
+        kj = t.lanes(k_ref, j)
+        runs.append(t.run_all(j))
+        ratio = t.ratio(runs[j], j) * norm_rows[j : j + 1]
+        gram = mm(kj, kj, ((1,), (1,)))
+        belows.append(jnp.where(row > col, gram * ratio * (t.column(1, j) * scales[j]), 0.0))
     step = 16
     folded = jnp.concatenate([folded_blocks(belows[j], step, row, col) for j in range(n)], axis=0)
     own_col = lax.broadcasted_iota(jnp.int32, (step, count), 1) % step
@@ -166,21 +170,37 @@
             inverses[j] = jnp.concatenate(both, axis=0)
         step *= 2
     for j in range(n):
-        k_scale, q_scale = scales[j]
-        kj = k_rows[j]
+        kj = t.lanes(k_ref, j)
         inverse = inverses[j]
-        run_end = line(0, j)[:, count - 1 :]
-        from_query = dot_ff(query_grams[j], inverse)
-        from_key = dot_bf_t(kj, inverse * (jnp.exp(run_end - runs[j]) * k_scale))
-        both = jnp.concatenate([from_query, from_key], axis=0)
-        beta_row = line(1, j)
-        growth = line(2, j)
-        written = dot_fb(both * beta_row, lanes(v_ref, j))
-        erased = dot_fb(both * (beta_row * growth * k_norm_rows[j : j + 1]), kj)
-        local_ref[:, j * width : (j + 1) * width] = written[:count]
-        planes_ref[3 * j] = jnp.where(row == col, growth[:, count - 1 :], 0.0) - erased[count:]
-        planes_ref[3 * j + 1] = written[count:]
-        planes_ref[3 * j + 2] = (jnp.exp(runs[j]) * q_scale) * q_rows[j].astype(f32) - erased[:count]
+        inverse_ref[j] = inverse
+        run_end = t.line(0, j)[:, count - 1 :]
+        from_key = dot_bf_t(kj, inverse * (jnp.exp(run_end - runs[j]) * scales[j]))
+        beta_row, growth = t.line(1, j), t.line(2, j)
+        erased = dot_fb(from_key * (beta_row * growth * norm_rows[j : j + 1]), kj)
+        planes_ref[2 * j] = jnp.where(row == col, growth[:, count - 1 :], 0.0) - erased
+        planes_ref[2 * j + 1] = dot_fb(from_key * beta_row, t.lanes(v_ref, j))
+
+
+def query_kernel(heads, mine, pos_ref, q_ref, k_ref, v_ref, rows_ref, columns_ref, inverse_ref, eff_ref, local_ref):
+    t = Tokens(heads, mine, pos_ref, rows_ref, columns_ref)
+    n = t.half
+    width = q_ref.shape[1] // heads
+    norm_rows = t.scale_rows([t.scale(k_ref, j) for j in range(n)])
+    for j in range(n):
+        kj = t.lanes(k_ref, j)
+        qj = t.lanes(q_ref, j)
+        q_scale = t.scale(q_ref, j)
+        run_all = t.run_all(j)
+        ratio = t.ratio(run_all, j) * norm_rows[j : j + 1]
+        gram = mm(qj, kj, ((1,), (1,))) * ratio * q_scale
+        from_query = dot_ff(gram, inverse_ref[j])
+        beta_row, growth = t.line(1, j), t.line(2, j)
+        written = dot_fb(from_query * beta_row, t.lanes(v_ref, j))
+        erased = dot_fb(from_query * (beta_row * growth * norm_rows[j : j + 1]), kj)
+        local_ref[:, j * width : (j + 1) * width] = t.column(4, j) * written
+        eff_ref[j] = (jnp.exp(run_all) * q_scale) * qj.astype(f32) - erased
+    if not mine:
+        eff_ref[n] = t.columns
 
 
 def folded_blocks(matrix, step, row, col):
@@ -200,7 +220,7 @@
 
 
 def block_total(planes_ref, head):
-    return jnp.concatenate([planes_ref[3 * head], planes_ref[3 * head + 1]], axis=1)
+    return jnp.concatenate([planes_ref[2 * head], planes_ref[2 * head + 1]], axis=1)
 
 
 def pair_kernel(pos_ref, own_ref, other_ref, *refs):
@@ -228,24 +248,19 @@
     return jnp.where(odd, other, own), jnp.where(odd, own, other)
 
 
-def first_read_kernel(heads, pos_ref, own_ref, other_ref, cols_ref, local_ref, local_sent_ref, eff_ref, read_ref, out_ref, sent_out):
+def first_read_kernel(heads, pos_ref, own_ref, other_ref, own_eff_ref, other_eff_ref, cols_ref, eff_ref, read_ref):
     count, width = own_ref.shape[1:]
-    half = heads // 2
     odd = bit_of(pos_ref, 0)
-    for j in range(half):
-        own_eff = own_ref[3 * j + 2]
-        other_eff = other_ref[3 * j + 2]
+    for j in range(heads // 2):
+        own_eff = own_eff_ref[j]
+        other_eff = other_eff_ref[j]
         earlier = jnp.where(odd, block_total(other_ref, j), block_total(own_ref, j))
         both = dot_ff(jnp.where(odd, own_eff, other_eff), earlier)
-        gain = gate_columns(heads, 1, j, pos_ref, cols_ref, other_ref)[1]
+        gain = gate_columns(heads, 1, j, pos_ref, cols_ref, other_eff_ref)[1]
         eff_ref[j, :count] = jnp.where(odd, other_eff, own_eff)
         eff_ref[j, count:] = both[:, :width]
         read_ref[j, :count] = jnp.zeros((count, width), f32)
         read_ref[j, count:] = gain * both[:, width:]
-        lanes = slice(j * width, (j + 1) * width)
-        at = 4 * heads + j
-        out_ref[:, lanes] = cols_ref[:, at : at + 1] * local_ref[:, lanes]
-        sent_out[:, lanes] = cols_ref[:, at + half : at + half + 1] * local_sent_ref[:, lanes]
 
 
 def quad_kernel(pos_ref, own_ref, other_ref, out_ref):
@@ -371,19 +386,19 @@
     )(position, *held)
 
 
-def prepare(position, queries, key_rows, value_rows, write_strength, log_decay, level_gates):
+def opening(position, queries, key_rows, value_rows, write_strength, log_decay, level_gates):
     heads = write_strength.shape[0]
     count = queries.shape[0]
     arrays = (queries, key_rows, value_rows, write_strength, log_decay, level_gates)
     return pl.pallas_call(
-        prepare_kernel,
+        opening_kernel,
         out_shape=[pltpu.VMEM(value.shape, value.dtype) for value in arrays[:3]]
-        + [near(3 * heads, count), near(count, count)],
+        + [near(3 * heads, count), near(count, count), near(heads, count, count), near(heads // 2, count, count)],
         in_specs=[pl.BlockSpec(memory_space=pltpu.SMEM)] + [pl.BlockSpec(memory_space=pl.ANY)] * 6,
         scratch_shapes=[pltpu.VMEM(value.shape, value.dtype) for value in arrays[3:]]
         + [pltpu.SemaphoreType.DMA((6,))],
         compiler_params=params(),
-        name="prepare",
+        name="opening",
     )(position, *[pltpu.with_memory_space_constraint(value, pltpu.HBM) for value in arrays])
 
 
@@ -401,17 +416,13 @@
     def swapped(value, bit):
         return lax.ppermute(value, "ctx", [(i, i ^ (1 << bit)) for i in range(size)])
 
-    *tokens, columns = prepare(
+    *tokens, columns, sent, inverse_sent = opening(
         position, queries, key_rows, value_rows, write_strength, log_decay, level_gates
     )
-    sent, local_sent = run(
-        block_kernel, [near(3 * half + 1, count, count), near(count, half * width)],
-        position, *tokens, columns, name="block_sent", static=(heads, False),
-    )
     got = swapped(sent, 0)
-    own, local_own = run(
-        block_kernel, [near(3 * half, count, count), near(count, half * width)],
-        position, *tokens, columns, name="block_own", static=(heads, True),
+    own, inverse_own = run(
+        block_kernel, [near(2 * half, count, count), near(half, count, count)],
+        position, *tokens[1:], columns, name="block_own", static=(heads, True),
     )
     *pairs, low = run(
         pair_kernel,
@@ -419,13 +430,24 @@
         position, own, got, name="pair",
     )
     pairs_got = [swapped(pairs[2 * c], 1) for c in range(chunks)]
-    eff, read, local_own, local_sent = run(
-        first_read_kernel,
-        [near(half, 2 * count, width)] * 2 + [near(count, half * width)] * 2,
-        position, own, got, columns, local_own, local_sent, name="read_first", static=(heads,),
-    )
-    pairs_got[0], eff, read, local_own, local_sent = lax.optimization_barrier(
-        (pairs_got[0], eff, read, local_own, local_sent)
+    inverse_sent, inverse_own, _ = lax.optimization_barrier((inverse_sent, inverse_own, low))
+    inverses = (inverse_sent, inverse_own)
+    effs, locals_ = [], []
+    for mine in (False, True):
+        eff, local = run(
+            query_kernel, [near(half + (0 if mine else 1), count, width), near(count, half * width)],
+            position, *tokens, columns, inverses[mine], name="query", static=(heads, mine),
+        )
+        effs.append(eff)
+        locals_.append(local)
+    local_sent, local_own = locals_
+    eff_got = swapped(effs[0], 0)
+    pairs_got[0], eff_own, local_own, local_sent = lax.optimization_barrier(
+        (pairs_got[0], effs[1], local_own, local_sent)
+    )
+    eff, read = run(
+        first_read_kernel, [near(half, 2 * count, width)] * 2,
+        position, own, got, eff_own, eff_got, columns, name="read_first", static=(heads,),
     )
     totals = [
         run(quad_kernel, near(share, width, 2 * width), position, pairs[2 * c + 1], pairs_got[c], name="quad")
@@ -460,7 +482,7 @@
         read, *gated = run(
             functools.partial(read_kernel, heads, level, top),
             [near(half, 2 * count, width)] * (2 if level == top - 1 else 1), position, eff, read, columns,
-            got, level_use, level_other, *extra, name="read",
+            eff_got, level_use, level_other, *extra, name="read",
         )
     keep, away = run(
         last_read_kernel, [near(count, half * width)] * 2,

time: 39.6 us -> 38.9 us (0.982)
  waiting for transfers between devices: 14.4 us -> 11.9 us
  Pallas kernels: 10.9 us -> 12.8 us
    ppermute x10 -> x11, waiting for transfers between devices: 14.4 us -> 11.9 us  [swapped(): return lax.ppermute(value, 'ctx', [(i, i ^ 1 << bit) for i in range(size)])]
    pallas_call x1, Pallas kernels: 1.21 us -> 3.41 us  [opening(): pl.pallas_call(opening_kernel, out_shape=[pltpu.VMEM(value.shape, value.d...]
    pallas_call x11 -> x12, Pallas kernels: 9.7 us -> 9.36 us  [run(): pl.pallas_call(lambda *refs: kernel(*static, *refs), out_shape=out_shapes...]
    ppermute x10 -> x11, starting transfers between devices: 14 us -> 14 us  [swapped(): return lax.ppermute(value, 'ctx', [(i, i ^ 1 << bit) for i in range(size)])]
  transfers between devices with their start and end apart: 10 -> 11, of which waited for: 7 -> 7; matrix products, arithmetic and copies ran while one was open for 0% -> 0% of each run, Pallas kernels for 14% -> 20%
where the time goes in v5:
time: 38.9 us; the launch traced here: 38.7 us
  starting transfers between devices  14 us (36%)
  Pallas kernels  12.8 us (33%)
  waiting for transfers between devices  11.9 us (31%)
    ppermute x11, starting transfers between devices, swapped(): return lax.ppermute(value, 'ctx', [(i, i ^ 1 << bit) for i in range(size)])  14 us
    ppermute x11, waiting for transfers between devices, swapped(): return lax.ppermute(value, 'ctx', [(i, i ^ 1 << bit) for i in range(size)])  11.9 us
    pallas_call x12, Pallas kernels, run(): pl.pallas_call(lambda *refs: kernel(*static, *refs), out_shape=out_shapes...  9.36 us
    pallas_call x1, Pallas kernels, opening(): pl.pallas_call(opening_kernel, out_shape=[pltpu.VMEM(value.shape, value.d...  3.41 us
  transfers between devices with their start and end apart: 11, of which 7 were waited for; matrix products, arithmetic and copies ran while one was open for 0% of the time, Pallas kernels for 20%

profile of v5, /device:TPU:0, one launch (start us, length us, event | category | flops | bytes accessed | tf_op | source)
XLA Modules:
  0.0 38.7 jit_solution(2849906551042840224)
XLA Ops:
  0.0 3.4 %opening.1 = (bf16[128,1024]{1,0:T(8,128)(2,1)S(1)}, bf16[128,1024]{1,0:T(8,128)(2,1)S(1)}, bf16[128,1024]{1,0:T(8,128)(2,1)S(1)}, f32[24,128]{1,0:T(8,128)S(1)}...) custom-call(s32[1]{0:T(128)} %bitcast.pos_ref.refs_0_, ...), custom_call_target="tpu_custom_call" | custom-call | tf_op jit(solution)/shard_map/opening/pallas_call | solution.py:393
  3.4 0.6 %collective-permute-start = (f32[8,128,128]{2,1,0:T(8,128)S(1)}, f32[8,128,128]{2,1,0:T(8,128)S(1)}, u32[]{:S(2)}, u32[]{:S(2)}) collective-permute-start(f32[8,128,128]{2,1,0:T(8,128)S(1)} %get-tuple-element.48), channel_id=1, source_target_pairs={{0,1},{1,0},{2,3},{3,2},{4,5},{5,4},{6,7},{7,6},{8,9},{9,8},{10,11... | collective-permute-start | bytes 1572872 | tf_op jit(solution)/shard_map/ppermute | solution.py:417
  4.0 2.3 %block_own.1 = (f32[8,128,128]{2,1,0:T(8,128)S(1)}, f32[4,128,128]{2,1,0:T(8,128)S(1)}) custom-call(s32[1]{0:T(128)} %bitcast.pos_ref.refs_0_, bf16[128,1024]{1,0:T(8,128)(2,1)S(1)} %get-tuple-element.43.refs_1_.refs_2_, bf16[128,1024]{1,0:T(8,128)(2,1)S(1)} %get-tuple-element.44.refs_2_.refs_3_, f32[24,128]{1,0:T(8,128)S(1)} %get-tuple-element.45.refs_3_.refs_4_, ...), custom_call_target="tpu_custom_call" | custom-call | tf_op jit(solution)/shard_map/block_own/pallas_call | solution.py:379
  6.2 0.0 collective-permute-done.refs_2_
  6.3 0.3 pair.1
  6.6 2.6 %collective-permute-start.1 = (f32[1,128,256]{2,1,0:T(8,128)S(1)}, f32[1,128,256]{2,1,0:T(8,128)S(1)}, u32[]{:S(2)}, u32[]{:S(2)}) collective-permute-start(f32[1,128,256]{2,1,0:T(8,128)S(1)} %get-tuple-element.49), channel_id=1, source_target_pairs={{0,2},{1,3},{2,0},{3,1},{4,6},{5,7},{6,4},{7,5},{8,10},{9,11},{10,... | collective-permute-start | bytes 393224 | tf_op jit(solution)/shard_map/ppermute | solution.py:417
  9.2 0.1 collective-permute-start.3
  9.2 1.3 %query.2 = (f32[4,128,128]{2,1,0:T(8,128)S(1)}, f32[128,512]{1,0:T(8,128)S(1)}) custom-call(s32[1]{0:T(128)} %bitcast.pos_ref.refs_0_, bf16[128,1024]{1,0:T(8,128)(2,1)S(1)} %get-tuple-element.50.refs_1_, bf16[128,1024]{1,0:T(8,128)(2,1)S(1)} %get-tuple-element.43.refs_1_.refs_2_, bf16[128,1024]{1,0:T(8,128)(2,1)S(1)} %get-tuple-element.44.refs_2_.refs_3_, ...), custom_call_target="tpu_custom_call" | custom-call | tf_op jit(solution)/shard_map/query/pallas_call | solution.py:379
  10.6 1.3 %query.3 = (f32[5,128,128]{2,1,0:T(8,128)S(1)}, f32[128,512]{1,0:T(8,128)S(1)}) custom-call(s32[1]{0:T(128)} %bitcast.pos_ref.refs_0_, bf16[128,1024]{1,0:T(8,128)(2,1)S(1)} %get-tuple-element.50.refs_1_, bf16[128,1024]{1,0:T(8,128)(2,1)S(1)} %get-tuple-element.43.refs_1_.refs_2_, bf16[128,1024]{1,0:T(8,128)(2,1)S(1)} %get-tuple-element.44.refs_2_.refs_3_, ...), custom_call_target="tpu_custom_call" | custom-call | tf_op jit(solution)/shard_map/query/pallas_call | solution.py:379
  11.9 1.6 %collective-permute-done.1.refs_2_.refs_7_.refs_8_ = f32[1,128,256]{2,1,0:T(8,128)S(1)} collective-permute-done((f32[1,128,256]{2,1,0:T(8,128)S(1)}, f32[1,128,256]{2,1,0:T(8,128)S(1)}, u32[]{:S(2)}, u32[]{:S(2)}) %collective-permute-start.1) | collective-permute-done | bytes 131104 | tf_op jit(solution)/shard_map/ppermute | solution.py:417
  13.5 0.2 quad.2.refs_1_
  13.7 2.2 %collective-permute-start.4 = (f32[1,128,256]{2,1,0:T(8,128)S(1)}, f32[1,128,256]{2,1,0:T(8,128)S(1)}, u32[]{:S(2)}, u32[]{:S(2)}) collective-permute-start(f32[1,128,256]{2,1,0:T(8,128)S(1)} %quad.2.refs_1_), channel_id=1, source_target_pairs={{0,4},{1,5},{2,6},{3,7},{4,0},{5,1},{6,2},{7,3},{8,12},{9,13},{10,... | collective-permute-start | bytes 393224 | tf_op jit(solution)/shard_map/ppermute | solution.py:417
  15.9 0.2 collective-permute-done.3.refs_2_.refs_8_.refs_9_
  16.1 0.2 quad.3.refs_2_
  16.3 1.9 %collective-permute-start.5 = (f32[1,128,256]{2,1,0:T(8,128)S(1)}, f32[1,128,256]{2,1,0:T(8,128)S(1)}, u32[]{:S(2)}, u32[]{:S(2)}) collective-permute-start(f32[1,128,256]{2,1,0:T(8,128)S(1)} %quad.3.refs_2_), channel_id=1, source_target_pairs={{0,4},{1,5},{2,6},{3,7},{4,0},{5,1},{6,2},{7,3},{8,12},{9,13},{10,... | collective-permute-start | bytes 393224 | tf_op jit(solution)/shard_map/ppermute | solution.py:417
  18.2 0.0 collective-permute-start.2
  18.2 0.7 %collective-permute-done.4.refs_3_ = f32[1,128,256]{2,1,0:T(8,128)S(1)} collective-permute-done((f32[1,128,256]{2,1,0:T(8,128)S(1)}, f32[1,128,256]{2,1,0:T(8,128)S(1)}, u32[]{:S(2)}, u32[]{:S(2)}) %collective-permute-start.4) | collective-permute-done | bytes 131104 | tf_op jit(solution)/shard_map/ppermute | solution.py:417
  18.9 2.8 %collective-permute-done.5.refs_4_ = f32[1,128,256]{2,1,0:T(8,128)S(1)} collective-permute-done((f32[1,128,256]{2,1,0:T(8,128)S(1)}, f32[1,128,256]{2,1,0:T(8,128)S(1)}, u32[]{:S(2)}, u32[]{:S(2)}) %collective-permute-start.5) | collective-permute-done | bytes 131104 | tf_op jit(solution)/shard_map/ppermute | solution.py:417
  21.7 0.3 climb.1
  22.0 3.0 %collective-permute-start.7 = (f32[2,128,128]{2,1,0:T(8,128)S(1)}, f32[2,128,128]{2,1,0:T(8,128)S(1)}, u32[]{:S(2)}, u32[]{:S(2)}) collective-permute-start(f32[2,128,128]{2,1,0:T(8,128)S(1)} %get-tuple-element.72), channel_id=1, source_target_pairs={{0,8},{1,9},{2,10},{3,11},{4,12},{5,13},{6,14},{7,15},{8,0},{9,1},... | collective-permute-start | bytes 393224 | tf_op jit(solution)/shard_map/ppermute | solution.py:417
  25.0 1.5 %collective-permute-start.6 = (f32[2,128,128]{2,1,0:T(8,128)S(1)}, f32[2,128,128]{2,1,0:T(8,128)S(1)}, u32[]{:S(2)}, u32[]{:S(2)}) collective-permute-start(f32[2,128,128]{2,1,0:T(8,128)S(1)} %get-tuple-element.70), channel_id=1, source_target_pairs={{0,2},{1,3},{2,0},{3,1},{4,6},{5,7},{6,4},{7,5},{8,10},{9,11},{10,... | collective-permute-start | bytes 393224 | tf_op jit(solution)/shard_map/ppermute | solution.py:417
  26.5 0.5 %collective-permute-start.8 = (f32[2,128,128]{2,1,0:T(8,128)S(1)}, f32[2,128,128]{2,1,0:T(8,128)S(1)}, u32[]{:S(2)}, u32[]{:S(2)}) collective-permute-start(f32[2,128,128]{2,1,0:T(8,128)S(1)} %get-tuple-element.75), channel_id=1, source_target_pairs={{0,2},{1,3},{2,0},{3,1},{4,6},{5,7},{6,4},{7,5},{8,10},{9,11},{10,... | collective-permute-start | bytes 393224 | tf_op jit(solution)/shard_map/ppermute | solution.py:417
  27.1 3.6 %collective-permute-done.7.refs_2_ = f32[2,128,128]{2,1,0:T(8,128)S(1)} collective-permute-done((f32[2,128,128]{2,1,0:T(8,128)S(1)}, f32[2,128,128]{2,1,0:T(8,128)S(1)}, u32[]{:S(2)}, u32[]{:S(2)}) %collective-permute-start.7) | collective-permute-done | bytes 131104 | tf_op jit(solution)/shard_map/ppermute | solution.py:417
  30.7 0.2 top.1
  30.9 1.6 %collective-permute-start.9 = (f32[2,128,128]{2,1,0:T(8,128)S(1)}, f32[2,128,128]{2,1,0:T(8,128)S(1)}, u32[]{:S(2)}, u32[]{:S(2)}) collective-permute-start(f32[2,128,128]{2,1,0:T(8,128)S(1)} %get-tuple-element.73), channel_id=1, source_target_pairs={{0,2},{1,3},{2,0},{3,1},{4,6},{5,7},{6,4},{7,5},{8,10},{9,11},{10,... | collective-permute-start | bytes 393224 | tf_op jit(solution)/shard_map/ppermute | solution.py:417
  32.5 0.4 %read_first.1 = (f32[4,256,128]{2,1,0:T(8,128)S(1)}, f32[4,256,128]{2,1,0:T(8,128)S(1)}) custom-call(s32[1]{0:T(128)} %bitcast.pos_ref.refs_0_, f32[8,128,128]{2,1,0:T(8,128)S(1)} %get-tuple-element.47.refs_1_, f32[8,128,128]{2,1,0:T(8,128)S(1)} %collective-permute-done.refs_2_, f32[4,128,128]{2,1,0:T(8,128)S(1)} %get-tuple-element.61.refs_3_, ...), custom_call_target="tpu_custom_call" | custom-call | tf_op jit(solution)/shard_map/read_first/pallas_call | solution.py:379
  33.0 1.6 %read.1 = (f32[4,256,128]{2,1,0:T(8,128)S(1)}, f32[4,256,128]{2,1,0:T(8,128)S(1)}) custom-call(s32[1]{0:T(128)} %bitcast.pos_ref.refs_0_, f32[4,256,128]{2,1,0:T(8,128)S(1)} %get-tuple-element.63.refs_1_, f32[4,256,128]{2,1,0:T(8,128)S(1)} %get-tuple-element.64.refs_2_, f32[128,128]{1,0:T(8,128)S(1)} %get-tuple-element.46.refs_4_.refs_5_.refs_3_, ...), custom_call_target="tpu_custom_call" | custom-call | tf_op jit(solution)/shard_map/read/pallas_call | solution.py:379
  34.6 1.4 %collective-permute-done.9.refs_4_ = f32[2,128,128]{2,1,0:T(8,128)S(1)} collective-permute-done((f32[2,128,128]{2,1,0:T(8,128)S(1)}, f32[2,128,128]{2,1,0:T(8,128)S(1)}, u32[]{:S(2)}, u32[]{:S(2)}) %collective-permute-start.9) | collective-permute-done | bytes 131104 | tf_op jit(solution)/shard_map/ppermute | solution.py:417
  36.0 0.3 read_last.1
  36.3 0.1 collective-permute-start.10
  36.4 1.5 %collective-permute-done.10.refs_4_ = f32[128,512]{1,0:T(8,128)S(1)} collective-permute-done((f32[128,512]{1,0:T(8,128)S(1)}, f32[128,512]{1,0:T(8,128)S(1)}, u32[]{:S(2)}, u32[]{:S(2)}) %collective-permute-start.10) | collective-permute-done | bytes 262176 | tf_op jit(solution)/shard_map/ppermute | solution.py:417
  37.9 0.8 %join.1 = f32[128,1024]{1,0:T(8,128)} custom-call(s32[1]{0:T(128)} %bitcast.pos_ref.refs_0_, f32[128,512]{1,0:T(8,128)S(1)} %get-tuple-element.59.refs_1_, f32[128,512]{1,0:T(8,128)S(1)} %get-tuple-element.60.refs_2_, f32[128,512]{1,0:T(8,128)S(1)} %get-tuple-element.79.refs_3_, f32[128,512]{1,0:T(8,128)S(1)} %collective-permute-done.10.refs_4_), custom_call_target="tpu_custom_call" | custom-call | tf_op jit(solution)/shard_map/join/pallas_call | solution.py:379
  (3 shorter events, 0.0 us)
Async XLA Ops:
  3.4 2.8 %collective-permute-start = (f32[8,128,128]{2,1,0:T(8,128)S(1)}, f32[8,128,128]{2,1,0:T(8,128)S(1)}, u32[]{:S(2)}, u32[]{:S(2)}) collective-permute-start(f32[8,128,128]{2,1,0:T(8,128)S(1)} %get-tuple-element.48), channel_id=1, source_target_pairs={{0,1},{1,0},{2,3},{3,2},{4,5},{5,4},{6,7},{7,6},{8,9},{9,8},{10,11... | collective-permute-start | bytes 1572872 | tf_op jit(solution)/shard_map/ppermute | solution.py:417
  6.6 6.9 %collective-permute-start.1 = (f32[1,128,256]{2,1,0:T(8,128)S(1)}, f32[1,128,256]{2,1,0:T(8,128)S(1)}, u32[]{:S(2)}, u32[]{:S(2)}) collective-permute-start(f32[1,128,256]{2,1,0:T(8,128)S(1)} %get-tuple-element.49), channel_id=1, source_target_pairs={{0,2},{1,3},{2,0},{3,1},{4,6},{5,7},{6,4},{7,5},{8,10},{9,11},{10,... | collective-permute-start | bytes 393224 | tf_op jit(solution)/shard_map/ppermute | solution.py:417
  9.2 7.0 %collective-permute-start.3 = (f32[1,128,256]{2,1,0:T(8,128)S(1)}, f32[1,128,256]{2,1,0:T(8,128)S(1)}, u32[]{:S(2)}, u32[]{:S(2)}) collective-permute-start(f32[1,128,256]{2,1,0:T(8,128)S(1)} %get-tuple-element.68), channel_id=1, source_target_pairs={{0,2},{1,3},{2,0},{3,1},{4,6},{5,7},{6,4},{7,5},{8,10},{9,11},{10,... | collective-permute-start | bytes 393224 | tf_op jit(solution)/shard_map/ppermute | solution.py:417
  13.7 5.2 %collective-permute-start.4 = (f32[1,128,256]{2,1,0:T(8,128)S(1)}, f32[1,128,256]{2,1,0:T(8,128)S(1)}, u32[]{:S(2)}, u32[]{:S(2)}) collective-permute-start(f32[1,128,256]{2,1,0:T(8,128)S(1)} %quad.2.refs_1_), channel_id=1, source_target_pairs={{0,4},{1,5},{2,6},{3,7},{4,0},{5,1},{6,2},{7,3},{8,12},{9,13},{10,... | collective-permute-start | bytes 393224 | tf_op jit(solution)/shard_map/ppermute | solution.py:417
  16.3 5.4 %collective-permute-start.5 = (f32[1,128,256]{2,1,0:T(8,128)S(1)}, f32[1,128,256]{2,1,0:T(8,128)S(1)}, u32[]{:S(2)}, u32[]{:S(2)}) collective-permute-start(f32[1,128,256]{2,1,0:T(8,128)S(1)} %quad.3.refs_2_), channel_id=1, source_target_pairs={{0,4},{1,5},{2,6},{3,7},{4,0},{5,1},{6,2},{7,3},{8,12},{9,13},{10,... | collective-permute-start | bytes 393224 | tf_op jit(solution)/shard_map/ppermute | solution.py:417
  18.2 14.3 %collective-permute-start.2 = (f32[5,128,128]{2,1,0:T(8,128)S(1)}, f32[5,128,128]{2,1,0:T(8,128)S(1)}, u32[]{:S(2)}, u32[]{:S(2)}) collective-permute-start(f32[5,128,128]{2,1,0:T(8,128)S(1)} %get-tuple-element.62), channel_id=1, source_target_pairs={{0,1},{1,0},{2,3},{3,2},{4,5},{5,4},{6,7},{7,6},{8,9},{9,8},{10,11... | collective-permute-start | bytes 983048 | tf_op jit(solution)/shard_map/ppermute | solution.py:417
  22.0 8.7 %collective-permute-start.7 = (f32[2,128,128]{2,1,0:T(8,128)S(1)}, f32[2,128,128]{2,1,0:T(8,128)S(1)}, u32[]{:S(2)}, u32[]{:S(2)}) collective-permute-start(f32[2,128,128]{2,1,0:T(8,128)S(1)} %get-tuple-element.72), channel_id=1, source_target_pairs={{0,8},{1,9},{2,10},{3,11},{4,12},{5,13},{6,14},{7,15},{8,0},{9,1},... | collective-permute-start | bytes 393224 | tf_op jit(solution)/shard_map/ppermute | solution.py:417
  25.0 7.9 %collective-permute-start.6 = (f32[2,128,128]{2,1,0:T(8,128)S(1)}, f32[2,128,128]{2,1,0:T(8,128)S(1)}, u32[]{:S(2)}, u32[]{:S(2)}) collective-permute-start(f32[2,128,128]{2,1,0:T(8,128)S(1)} %get-tuple-element.70), channel_id=1, source_target_pairs={{0,2},{1,3},{2,0},{3,1},{4,6},{5,7},{6,4},{7,5},{8,10},{9,11},{10,... | collective-permute-start | bytes 393224 | tf_op jit(solution)/shard_map/ppermute | solution.py:417
  26.5 6.5 %collective-permute-start.8 = (f32[2,128,128]{2,1,0:T(8,128)S(1)}, f32[2,128,128]{2,1,0:T(8,128)S(1)}, u32[]{:S(2)}, u32[]{:S(2)}) collective-permute-start(f32[2,128,128]{2,1,0:T(8,128)S(1)} %get-tuple-element.75), channel_id=1, source_target_pairs={{0,2},{1,3},{2,0},{3,1},{4,6},{5,7},{6,4},{7,5},{8,10},{9,11},{10,... | collective-permute-start | bytes 393224 | tf_op jit(solution)/shard_map/ppermute | solution.py:417
  30.9 5.0 %collective-permute-start.9 = (f32[2,128,128]{2,1,0:T(8,128)S(1)}, f32[2,128,128]{2,1,0:T(8,128)S(1)}, u32[]{:S(2)}, u32[]{:S(2)}) collective-permute-start(f32[2,128,128]{2,1,0:T(8,128)S(1)} %get-tuple-element.73), channel_id=1, source_target_pairs={{0,2},{1,3},{2,0},{3,1},{4,6},{5,7},{6,4},{7,5},{8,10},{9,11},{10,... | collective-permute-start | bytes 393224 | tf_op jit(solution)/shard_map/ppermute | solution.py:417
  36.3 1.6 %collective-permute-start.10 = (f32[128,512]{1,0:T(8,128)S(1)}, f32[128,512]{1,0:T(8,128)S(1)}, u32[]{:S(2)}, u32[]{:S(2)}) collective-permute-start(f32[128,512]{1,0:T(8,128)S(1)} %get-tuple-element.80), channel_id=1, source_target_pairs={{0,1},{1,0},{2,3},{3,2},{4,5},{5,4},{6,7},{7,6},{8,9},{9,8},{10,11... | collective-permute-start | bytes 786440 | tf_op jit(solution)/shard_map/ppermute | solution.py:417
